TPU v7x, 32 devices: a whole 2x2x4 slice. The times are simulated.
32 devices in a mesh: grp: 4 (over z), row: 2 (over x), col: 4 (over y, core).
Axes of the slice: x: 2, y: 2, z: 4, core: 2. Of those that a mesh axis runs over, the one named last changes fastest.
Arguments:
- dec_input: bfloat16 [3, 4, 16, 64, 128], P(None, None, 'row', 'col'), may hold values from -6 to 6
- target: bfloat16 [3, 3, 4, 16, 64], P(None, None, 'col', 'row'), may hold values from -5 to 5
- conv_first: bfloat16 [3456, 128], replicated, may hold values from -0.109375 to 0.109375
- conv_second: bfloat16 [3456, 128], replicated, may hold values from -0.109375 to 0.109375
- rgb_weight: bfloat16 [3, 128], replicated, may hold values from -0.5 to 0.5
- vgg_first: bfloat16 [27, 64], replicated, may hold values from -1.25 to 1.25
- vgg_second: bfloat16 [576, 64], replicated, may hold values from -0.25 to 0.25
- vgg_third: bfloat16 [576, 128], replicated, may hold values from -0.25 to 0.25
Outputs:
- grad_first: float32 [442368], P(('grp', 'row', 'col'))
- grad_second: float32 [442368], P(('grp', 'row', 'col'))
All inputs are finite; a program needn't handle non-finite values.
Results may differ from a plain program's by a relative error of at most 0.015.
Values may be sent and summed in bfloat16 or wider, within the bound.
No kernel may reach another device: no remote copies, remote signals or barrier semaphores. Data moves between devices by JAX's collectives and lax.ppermute only.
A program may use at most 128 MiB of HBM per device.

v0:
```python
import functools

import jax
import jax.numpy as jnp
from jax import lax
from jax.experimental import pallas as pl
from jax.experimental.pallas import tpu as pltpu
from jax.sharding import PartitionSpec as P

gelu_scale = 0.7978845608028654
gelu_cubic = 0.044715
plane = ("row", "col")
vmem_bytes = 62 * 2**20


def repeat(count, body, unroll=1):
    lax.fori_loop(0, count, lambda i, carry: (body(i), carry)[1], 0, unroll=unroll)


def matmul(left, right):
    return jnp.dot(left, right, preferred_element_type=jnp.float32)


def gelu_tanh(z):
    return jnp.tanh(gelu_scale * (z + gelu_cubic * z * z * z))


def gelu_slope(z, t):
    return 0.5 * (1.0 + t) + 0.5 * z * (1.0 - t * t) * gelu_scale * (
        1.0 + 3.0 * gelu_cubic * z * z
    )


def corner(rows, cols, height, width, view_rows, view_cols):
    top, left = lax.axis_index("row") * rows, lax.axis_index("col") * cols
    return (
        top,
        left,
        jnp.clip(top - 10, 0, height - view_rows),
        jnp.clip(left - 10, 0, width - view_cols),
    )


def col_mask(first_col, cols, width, slots, frames):
    at = lax.broadcasted_iota(jnp.int32, (cols * slots, 1), 0)
    col = at // slots + first_col
    return (at % slots < frames) & (col >= 0) & (col < width)


def conv_frames(source, row, cols, weight):
    slots, channels = source.shape[-2:]
    slabs = [
        source[row + dr, pl.ds(dc, cols)].reshape(cols * slots, channels)
        for dr in range(3)
        for dc in range(3)
    ]
    sums = matmul(jnp.concatenate(slabs, axis=1), weight)
    count = cols * slots
    return (
        pltpu.roll(sums[:, :channels], 1, 0)
        + sums[:, channels : 2 * channels]
        + pltpu.roll(sums[:, 2 * channels :], count - 1, 0)
    )


def frame_weight(ref):
    third = ref.shape[0] // 3
    return jnp.concatenate([ref[pl.ds(third * k, third)] for k in range(3)], axis=1)


def forward_kernel(
    frames, own, up, down, left, right, first, second, project,
    cells_out, hidden_out, slope_first, slope_second, colour, cells, hidden, spread_weight,
):
    rows, cols, slots, channels = own.shape
    half = slots // 2
    height, width = rows * lax.axis_size("row"), cols * lax.axis_size("col")
    top, left_col = lax.axis_index("row") * rows, lax.axis_index("col") * cols
    cells[3 : 3 + rows, 3 : 3 + cols] = own[...]
    cells[0:3, 3 : 3 + cols] = up[...]
    cells[3 + rows :, 3 : 3 + cols] = down[...]
    cells[:, 0:3] = left[...]
    cells[:, 3 + cols :] = right[...]
    cells_out[...] = cells[2 : 4 + rows, 2 : 4 + cols]
    spread_weight[...] = frame_weight(first)

    def first_layer(r):
        pre = conv_frames(cells, r, cols + 4, spread_weight[...])
        row = top - 2 + r
        keep = col_mask(left_col - 2, cols + 4, width, slots, frames) & (
            (row >= 0) & (row < height)
        )
        gate = 0.5 + 0.5 * jnp.tanh(0.5 * pre)
        out = jnp.where(keep, pre * gate, 0.0).astype(jnp.bfloat16)
        hidden[r] = out.reshape(cols + 4, slots, channels)
        slope = jnp.where(keep, gate * (1.0 + pre * (1.0 - gate)), 0.0)

        @pl.when((r >= 2) & (r < 2 + rows))
        def _():
            slope_first[r - 2] = slope[2 * slots : (2 + cols) * slots]

    repeat(rows + 4, first_layer, 2)
    hidden_out[...] = hidden[1 : 3 + rows, 1 : 3 + cols]
    spread_weight[...] = frame_weight(second)

    def second_layer(r):
        pre = conv_frames(hidden, r, cols + 2, spread_weight[...])
        row = top - 1 + r
        keep = col_mask(left_col - 1, cols + 2, width, slots, frames) & (
            (row >= 0) & (row < height)
        )
        gate = 0.5 + 0.5 * jnp.tanh(0.5 * pre)
        slope_second[r] = jnp.where(keep, gate * (1.0 + pre * (1.0 - gate)), 0.0)
        out = jnp.where(keep, pre * gate, 0.0)[slots : (1 + cols) * slots]
        out = out.reshape(cols, 2, half, channels)
        both = jnp.concatenate(
            [out[:, k].reshape(cols * half, channels) for k in range(2)], axis=1
        ).astype(jnp.bfloat16)

        @pl.when((r >= 1) & (r < 1 + rows))
        def _():
            colour[r - 1] = lax.dot_general(
                project[...], both, (((1,), (1,)), ((), ())),
                preferred_element_type=jnp.float32,
            ).astype(jnp.bfloat16)

    repeat(rows + 2, second_layer, 2)


def image_line(images, row, rows, cols, width, half, left):
    parts = lax.axis_size("col")
    line = jnp.concatenate(
        [images[(row // rows) * parts + k, row % rows].astype(jnp.float32) for k in range(parts)],
        axis=1,
    )
    span = width * half
    return pltpu.roll(line, lax.rem(span - left * half, span), 1)


def plane_slabs(wide, narrow, row, count, half):
    pieces = []
    for dr in range(3):
        pieces.append(wide[row + dr, pl.ds(0, count)])
        if half % 16:
            pieces.append(narrow[row + dr])
        else:
            pieces.append(wide[row + dr, pl.ds(half, count)])
        pieces.append(wide[row + dr, pl.ds(2 * half, count)])
    return jnp.concatenate(pieces, axis=1)


def store_slab(wide, narrow, row, value, half):
    wide[row] = value.astype(jnp.bfloat16)
    if half % 16:
        narrow[row] = value[half : value.shape[0] - half].astype(jnp.bfloat16)


def store_wide(wide, narrow, row, value, half):
    edge = jnp.zeros((half, value.shape[1]), jnp.float32)
    store_slab(wide, narrow, row, jnp.concatenate([edge, value, edge], axis=0), half)


def kept_row(row, first, number):
    return jnp.clip(row - first, -1, number) + 1


def clear_edges(wide, narrow):
    for ref in (wide, narrow):
        for at in (0, ref.shape[0] - 1):
            ref[at] = jnp.zeros(ref.shape[1:], ref.dtype)


def features(
    images, guides, geometry, weight_1, weight_2, weight_3,
    lines, wide_1, narrow_1, wide_3, narrow_3, on_first, on_second, on_third,
):
    rows, cols, height, width, view_rows, view_cols, half, view_top, view_left = geometry
    count = view_cols * half
    lanes = lines.shape[2]
    span = width * half
    lane = lax.broadcasted_iota(jnp.int32, (8, lanes), 1)

    def line_step(w):
        line = image_line(images, view_top + w, rows, cols, width, half, view_left)
        before = pltpu.roll(line, half, 1)[:, :lanes]
        after = pltpu.roll(line, span - half, 1)[:, :lanes]
        lines[w + 1] = jnp.concatenate(
            [
                jnp.where(lane < half, 0.0, before),
                line[:, :lanes],
                jnp.where(lane >= count - half, 0.0, after),
            ],
            axis=0,
        )

    lines[0] = jnp.zeros(lines.shape[1:], jnp.float32)
    lines[view_rows + 1] = jnp.zeros(lines.shape[1:], jnp.float32)
    repeat(view_rows, line_step, 2)
    clear_edges(wide_1, narrow_1)
    clear_edges(wide_3, narrow_3)

    def first_step(w):
        pieces = [lines[w], lines[w + 1], lines[w + 2]]
        if guides is not None:
            pieces.append(
                image_line(guides, view_top + w, rows, cols, width, half, view_left)[:, :lanes]
            )
        filled = sum(piece.shape[0] for piece in pieces)
        pieces.append(jnp.zeros((128 - filled, lanes), jnp.float32))
        patches = jnp.concatenate(pieces, axis=0).T[:count].astype(jnp.bfloat16)
        plane_1 = matmul(patches, weight_1[...])
        on_first(w, plane_1)
        z = plane_1[:, :128]
        store_wide(wide_1, narrow_1, w + 1, 0.5 * z * (1.0 + gelu_tanh(z)), half)

    repeat(view_rows, first_step, 2)

    def second_step(q):
        total = 0.0
        for part in range(2):
            w = 2 * q + part
            z = matmul(plane_slabs(wide_1, narrow_1, w, count, half), weight_2[...])
            value = 0.5 * z * (1.0 + gelu_tanh(z))
            on_second(w, z, value)
            total = total + value
        pooled = total.reshape(view_cols // 2, 2, half, 128)
        pooled = 0.25 * (pooled[:, 0] + pooled[:, 1])
        store_wide(wide_3, narrow_3, q + 1, pooled.reshape(count // 2, 128), half)

    repeat(view_rows // 2, second_step)

    def third_step(q):
        on_third(q, matmul(plane_slabs(wide_3, narrow_3, q, count // 2, half), weight_3[...]))

    repeat(view_rows // 2, third_step, 2)


def guide_kernel(
    tile, guides, weight_1, weight_2, weight_3, guide_2, guide_3,
    lines, wide_1, narrow_1, wide_3, narrow_3,
):
    rows, cols, half = tile
    height, width = rows * lax.axis_size("row"), cols * lax.axis_size("col")
    view_rows, view_cols = min(height, rows + 20), min(width, cols + 20)
    top, _, view_top, view_left = corner(rows, cols, height, width, view_rows, view_cols)

    def on_second(w, z, value):
        guide_2[kept_row(view_top + w, top - 3, rows + 6), pl.ds(3 * half, view_cols * half)] = value

    def on_third(q, z):
        guide_3[q] = 0.5 * z * (1.0 + gelu_tanh(z))

    features(
        guides, None,
        (rows, cols, height, width, view_rows, view_cols, half, view_top, view_left),
        weight_1, weight_2, weight_3, lines, wide_1, narrow_1, wide_3, narrow_3,
        lambda w, z: None, on_second, on_third,
    )


def gradient_taps(source, delta, shifted, sums, first_tap):
    rows = delta.shape[0]
    slots, channels = source.shape[-2:]
    cols = source.shape[1] - 2
    count = cols * slots

    def turn(r):
        block = delta[r].astype(jnp.float32)
        for dt in range(3):
            moved = block if dt == 1 else pltpu.roll(block, (dt - 1) % count, 0)
            shifted[dt, r] = moved.T.astype(jnp.bfloat16)

    repeat(rows, turn, 2)

    def tap_step(step):
        tap = jnp.minimum(first_tap + step, 26)
        dt, dr, dc = tap // 9, tap // 3 % 3, tap % 3
        total = 0.0
        for r in range(rows):
            slab = source[r + dr, pl.ds(dc, cols)].reshape(count, channels)
            total = total + matmul(shifted[dt, r], slab)
        sums[pl.ds(pl.multiple_of(step * channels, channels), channels)] = total.T

    repeat(sums.shape[0] // channels, tap_step)


def backward_kernel(
    frames, out_rows, images, guides, guide_2, guide_3, slope_first, slope_second, cells, hidden,
    weight_1, weight_2, weight_3, back_3, back_2, back_1, paint, back_second,
    terms,
    lines, wide_1, narrow_1, wide_3, narrow_3, plane_1, plane_2, differ, wide_g, narrow_g, spread,
    wide_b, narrow_b, wide_a, narrow_a, delta_second, delta_own, shifted, sums,
):
    slots, channels = cells.shape[-2:]
    rows, cols, half = cells.shape[0] - 2, cells.shape[1] - 2, slots // 2
    height, width = rows * lax.axis_size("row"), cols * lax.axis_size("col")
    view_rows, view_cols = min(height, rows + 20), min(width, cols + 20)
    top, left, view_top, view_left = corner(rows, cols, height, width, view_rows, view_cols)
    count = view_cols * half
    body = pl.ds(3 * half, count)

    def on_first(w, z):
        row = view_top + w
        plane_1[kept_row(row, top - 2, rows + 4), body] = z[:, :128]
        differ[kept_row(row, top - 1, rows + 2), body] = z[:, 128:]

    def on_second(w, z, value):
        plane_2[kept_row(view_top + w, top - 3, rows + 6), body] = z

    clear_edges(wide_g, narrow_g)

    def on_third(q, z):
        t = gelu_tanh(z)
        delta = (64.0 / (z.shape[1] // 2)) * (0.5 * z * (1.0 + t) - guide_3[q]) * gelu_slope(z, t)
        store_wide(wide_g, narrow_g, q + 1, delta, half)

    features(
        images, guides,
        (rows, cols, height, width, view_rows, view_cols, half, view_top, view_left),
        weight_1, weight_2, weight_3, lines, wide_1, narrow_1, wide_3, narrow_3,
        on_first, on_second, on_third,
    )

    def pool_step(q):
        grad = 0.25 * matmul(plane_slabs(wide_g, narrow_g, q, count // 2, half), back_3[...])
        grad = grad.reshape(view_cols // 2, 1, half, 128)
        grad = jnp.concatenate([grad, grad], axis=1)
        pool_row = view_top // 2 + q
        spread[kept_row(pool_row, top // 2 - 2, rows // 2 + 4), body] = grad.reshape(count, 128)

    repeat(view_rows // 2, pool_step, 2)

    def at(reach, a, number):
        row = top - reach + a
        keep = col_mask(left - reach, cols + 2 * reach, width, half, half) & (
            (row >= 0) & (row < height)
        )
        start = pl.multiple_of((left - view_left + 3 - reach) * half, half)
        return keep, pl.ds(start, number)

    def second_delta(a):
        number = (cols + 6) * half
        keep, span = at(3, a, number)
        z = plane_2[a + 1, span]
        t = gelu_tanh(z)
        value = 0.5 * z * (1.0 + t)
        delta = spread[(a + 1) // 2 + 1, span] + (16.0 / (z.shape[1] // 2)) * (value - guide_2[a + 1, span])
        delta = jnp.where(keep, delta * gelu_slope(z, t), 0.0)
        store_slab(wide_b, narrow_b, a, delta, half)

    repeat(rows + 6, second_delta)

    def first_delta(a):
        number = (cols + 4) * half
        keep, span = at(2, a, number)
        grad = matmul(plane_slabs(wide_b, narrow_b, a, number, half), back_2[...])
        z = plane_1[a + 1, span]
        delta = jnp.where(keep, grad * gelu_slope(z, gelu_tanh(z)), 0.0)
        store_slab(wide_a, narrow_a, a, delta, half)

    repeat(rows + 4, first_delta, 2)

    def pixel_step(a):
        number = (cols + 2) * half
        keep, span = at(1, a, number)
        grad = matmul(plane_slabs(wide_a, narrow_a, a, number, half), back_1[...])
        grad = jnp.where(keep, grad + (1.0 / 6.0) * differ[a + 1, span], 0.0)
        painted = matmul(grad.astype(jnp.bfloat16), paint[...])
        painted = jnp.concatenate(
            [
                painted[:, k * channels : (k + 1) * channels].reshape(cols + 2, 1, half, channels)
                for k in range(2)
            ],
            axis=1,
        ).reshape((cols + 2) * slots, channels)
        delta = (painted * slope_second[a]).astype(jnp.bfloat16)
        delta_second[a] = delta.reshape(cols + 2, slots, channels)

    repeat(rows + 2, pixel_step, 2)

    first_row = lax.axis_index("grp") * out_rows
    first_tap = first_row // channels
    skip = pl.multiple_of(first_row - first_tap * channels, 32)
    device = lax.axis_index("row") * lax.axis_size("col") + lax.axis_index("col")

    def put(which):
        value = sums[pl.ds(skip, out_rows)].astype(jnp.float32)
        if len(terms.shape) == 3:
            terms[which] = value.astype(jnp.bfloat16)
        else:
            chunks, _, size, _ = terms.shape
            for k in range(chunks):
                piece = value[k * size : (k + 1) * size].astype(jnp.bfloat16)
                terms[lax.rem(k - device + chunks, chunks), which] = piece

    def own_step(r):
        delta_own[r] = delta_second[r + 1, 1 : 1 + cols].reshape(cols * slots, channels)

    repeat(rows, own_step)
    gradient_taps(hidden, delta_own, shifted, sums, first_tap)
    put(1)

    def back_step(r):
        back = conv_frames(delta_second, r, cols, back_second[...])
        delta_own[r] = (back * slope_first[r]).astype(jnp.bfloat16)

    repeat(rows, back_step, 2)
    gradient_taps(cells, delta_own, shifted, sums, first_tap)
    put(0)


def twice(blocks):
    zero = jnp.zeros_like(blocks)
    return jnp.concatenate(
        [jnp.concatenate([blocks, zero], axis=2), jnp.concatenate([zero, blocks], axis=2)], axis=1
    )


def turned(weight):
    taps = weight.reshape(9, -1, weight.shape[1])[::-1]
    return jnp.transpose(taps, (0, 2, 1))


def plane_weights(vgg_first, vgg_second, vgg_third, rgb_weight):
    first = jnp.pad(twice(vgg_first.reshape(9, 3, -1)), ((0, 0), (0, 2), (0, 0)))
    first = jnp.pad(first.reshape(72, -1), ((0, 56), (0, 0)))
    pick = jnp.pad(jnp.eye(6, 128, dtype=jnp.bfloat16), ((0, 2), (0, 0)))
    pick = jnp.concatenate(
        [jnp.zeros((32, 128), jnp.bfloat16), pick, jnp.zeros((32, 128), jnp.bfloat16), -pick],
        axis=0,
    )
    pick = jnp.pad(pick, ((0, 48), (0, 0)))
    second = twice(vgg_second.reshape(9, 64, 64)).reshape(9 * 128, 128)
    third = twice(vgg_third.reshape(9, 64, 128)).reshape(9 * 128, 256)
    back_third = twice(turned(vgg_third)).reshape(9 * 256, 128)
    back_second = twice(turned(vgg_second)).reshape(9 * 128, 128)
    back_first = twice(turned(vgg_first))
    back_first = jnp.pad(back_first, ((0, 0), (0, 0), (0, 122))).reshape(9 * 128, 128)
    paint = twice(rgb_weight[None])[0]
    return (
        first,
        jnp.concatenate([first, pick], axis=1),
        second,
        third,
        back_third,
        back_second,
        back_first,
        jnp.pad(paint, ((0, 2), (0, 0))),
        jnp.pad(paint, ((0, 122), (0, 0))),
    )


def call(kernel, outs, scratch):
    return pl.pallas_call(
        kernel,
        out_shape=outs,
        scratch_shapes=[pltpu.VMEM(*shape) for shape in scratch],
        compiler_params=pltpu.CompilerParams(vmem_limit_bytes=vmem_bytes),
    )


def exchange(shard, axis, dim, width):
    count, length = lax.axis_size(axis), shard.shape[dim]
    last = lax.slice_in_dim(shard, length - width, length, axis=dim)
    first = lax.slice_in_dim(shard, 0, width, axis=dim)
    before = lax.ppermute(last, axis, [(i, i + 1) for i in range(count - 1)])
    after = lax.ppermute(first, axis, [(i + 1, i) for i in range(count - 1)])
    return before, after


def gather_plane(shard):
    count = lax.axis_size("row") * lax.axis_size("col")
    return lax.all_to_all(
        jnp.broadcast_to(shard[None], (count,) + shard.shape),
        plane,
        split_axis=0,
        concat_axis=0,
        tiled=True,
    )


def guide_lines(target, slots):
    row_count, col_count = lax.axis_size("row"), lax.axis_size("col")
    _, blocks, own, rows, width = target.shape
    cols, half = width // col_count, slots // 2
    frames = blocks * own * col_count
    whole = gather_plane(target)
    whole = whole.reshape(row_count, col_count, 3, blocks, own, rows, width)
    whole = jnp.transpose(whole, (2, 3, 1, 4, 0, 5, 6))
    whole = whole.reshape(3, frames, row_count, rows, col_count, cols)
    whole = jnp.pad(whole, ((0, 0), (0, slots - frames)) + ((0, 0),) * 4)
    whole = whole.reshape(3, 2, half, row_count, rows, col_count, cols)
    whole = jnp.transpose(whole, (3, 5, 4, 1, 0, 6, 2))
    whole = whole.reshape(row_count * col_count, rows, 6, cols * half)
    return jnp.pad(whole, ((0, 0), (0, 0), (0, 2), (0, 0)))


def local(dec_input, target, conv_first, conv_second, rgb_weight, vgg_first, vgg_second, vgg_third):
    f32, bf16 = jnp.float32, jnp.bfloat16
    row_count, col_count = lax.axis_size("row"), lax.axis_size("col")
    blocks, block_frames, rows, cols, channels = dec_input.shape
    frames = blocks * block_frames
    slots = -(-(frames + 1) // 16) * 16
    half = slots // 2
    height, width = rows * row_count, cols * col_count
    view_rows, view_cols = min(height, rows + 20), min(width, cols + 20)
    count = view_cols * half
    lanes = -(-count // 128) * 128

    own = jnp.transpose(dec_input.reshape(frames, rows, cols, channels), (1, 2, 0, 3))
    own = jnp.pad(own, ((0, 0), (0, 0), (0, slots - frames), (0, 0)))
    up, down = exchange(own, "row", 0, 3)
    tall = jnp.concatenate([up, own, down], axis=0)
    before, after = exchange(tall, "col", 1, 3)

    (
        first_plain, first_pick, second, third, back_third, back_second, back_first,
        project, paint,
    ) = plane_weights(vgg_first, vgg_second, vgg_third, rgb_weight)
    back_volume = conv_second.reshape(3, 9, channels, channels)[::-1, ::-1]
    back_volume = jnp.transpose(back_volume, (1, 3, 0, 2)).reshape(9 * channels, 3 * channels)

    guides = guide_lines(target, slots)
    thin = half % 16 != 0
    feature_scratch = [
        ((view_rows + 2, 24, lanes), f32),
        ((view_rows + 2, count + 2 * half, 128), bf16),
        ((view_rows + 2, count if thin else 16, 128), bf16),
        ((view_rows // 2 + 2, count // 2 + 2 * half, 128), bf16),
        ((view_rows // 2 + 2, count // 2 if thin else 16, 128), bf16),
    ]
    guide_2, guide_3 = call(
        functools.partial(guide_kernel, (rows, cols, half)),
        (
            jax.ShapeDtypeStruct((rows + 8, count + 6 * half, 128), f32),
            jax.ShapeDtypeStruct((view_rows // 2, count // 2, 256), f32),
        ),
        feature_scratch,
    )(guides, first_plain, second, third)

    cells, hidden, slope_first, slope_second, colour = call(
        functools.partial(forward_kernel, frames),
        (
            jax.ShapeDtypeStruct((rows + 2, cols + 2, slots, channels), bf16),
            jax.ShapeDtypeStruct((rows + 2, cols + 2, slots, channels), bf16),
            jax.ShapeDtypeStruct((rows, cols * slots, channels), f32),
            jax.ShapeDtypeStruct((rows + 2, (cols + 2) * slots, channels), f32),
            jax.ShapeDtypeStruct((rows, 8, cols * half), bf16),
        ),
        [
            ((rows + 6, cols + 6, slots, channels), bf16),
            ((rows + 4, cols + 4, slots, channels), bf16),
            ((9 * channels, 3 * channels), bf16),
        ],
    )(own, up, down, before, after, conv_first, conv_second, project)

    images = gather_plane(colour)
    groups, devices = lax.axis_size("grp"), row_count * col_count
    out_rows = conv_first.shape[0] // groups
    taps = max(
        -(-(g + 1) * out_rows // channels) - g * out_rows // channels for g in range(groups)
    )
    even = out_rows % devices == 0
    out_shape = (
        (devices, 2, out_rows // devices, channels) if even else (2, out_rows, channels)
    )
    wide_count = count + 6 * half
    terms = call(
        functools.partial(backward_kernel, frames, out_rows),
        jax.ShapeDtypeStruct(out_shape, bf16),
        feature_scratch
        + [
            ((rows + 6, wide_count, 128), f32),
            ((rows + 8, wide_count, 128), f32),
            ((rows + 4, wide_count, 128), f32),
            ((view_rows // 2 + 2, count // 2 + 2 * half, 256), bf16),
            ((view_rows // 2 + 2, count // 2 if thin else 16, 256), bf16),
            ((rows // 2 + 6, wide_count, 128), f32),
            ((rows + 6, (cols + 6) * half, 128), bf16),
            ((rows + 6, (cols + 4) * half if thin else 16, 128), bf16),
            ((rows + 4, (cols + 4) * half, 128), bf16),
            ((rows + 4, (cols + 2) * half if thin else 16, 128), bf16),
            ((rows + 2, cols + 2, slots, channels), bf16),
            ((rows, cols * slots, channels), bf16),
            ((3, rows, channels, cols * slots), bf16),
            ((taps * channels, channels), f32),
        ],
    )(
        images, guides, guide_2, guide_3, slope_first, slope_second, cells, hidden,
        first_pick, second, third, back_third, back_second, back_first, paint, back_volume,
    )

    if even:
        pieces = [terms[0]]
        for step in range(1, devices):
            ring = [(i, (i + step) % devices) for i in range(devices)]
            pieces.append(lax.ppermute(terms[step], plane, ring))
        total = sum(piece.astype(f32) for piece in pieces)
    else:
        pieces = jnp.swapaxes(terms.reshape(2, devices, -1), 0, 1)
        pieces = lax.all_to_all(pieces, plane, split_axis=0, concat_axis=0, tiled=True)
        total = jnp.sum(pieces.astype(f32), axis=0)
    return total[0].reshape(-1), total[1].reshape(-1)


def solution(mesh):
    in_specs = (
        P(None, None, "row", "col", None),
        P(None, None, "col", "row", None),
        P(),
        P(),
        P(),
        P(),
        P(),
        P(),
    )
    out_specs = (P(("grp", "row", "col")), P(("grp", "row", "col")))
    return jax.shard_map(local, mesh=mesh, in_specs=in_specs, out_specs=out_specs, check_vma=False)
```

profile of v0, /device:TPU:0, one launch (start us, length us, event | category | flops | bytes accessed | tf_op | source)
XLA Modules:
  0.0 128.8 jit_solution(14020678865112740382)
XLA Ops:
  2.2 5.2 %all-to-all-start.1 = ((bf16[8,2,2304]{2,1,0:T(2,128)(2,1)}), bf16[8,2,2304]{2,1,0:T(2,128)(2,1)S(1)}, u32[]{:S(2)}, u32[]{:S(2)}) async-start(bf16[8,2,2304]{2,1,0:T(2,128)(2,1)} %reshape.79), calls=%async_computation.1 | async-start | bytes 147456 | tf_op jit(solution)/shard_map/all_to_all | solution.py:473
  7.4 1.3 copy.54
  8.8 1.4 %collective-permute-start.1 = (bf16[3,16,16,128]{3,2,1,0:T(8,128)(2,1)S(1)}, bf16[3,16,16,128]{3,2,1,0:T(8,128)(2,1)S(1)}, u32[]{:S(2)}, u32[]{:S(2)}) collective-permute-start(bf16[3,16,16,128]{3,2,1,0:T(8,128)(2,1)S(1)} %get-tuple-element.18), channel_id=1, source_target_pairs={{4,0},{5,1},{6,2},{7,3},{12,8},{13,9},{14,10},{15,11},{20,16},{21,... | collective-permute-start | bytes 589832 | tf_op jit(solution)/shard_map/ppermute | solution.py:467
  10.2 4.6 %collective-permute-start = (bf16[3,16,16,128]{3,2,1,0:T(8,128)(2,1)S(1)}, bf16[3,16,16,128]{3,2,1,0:T(8,128)(2,1)S(1)}, u32[]{:S(2)}, u32[]{:S(2)}) collective-permute-start(bf16[3,16,16,128]{3,2,1,0:T(8,128)(2,1)S(1)} %get-tuple-element.19), channel_id=1, source_target_pairs={{0,4},{1,5},{2,6},{3,7},{8,12},{9,13},{10,14},{11,15},{16,20},{17,... | collective-permute-start | bytes 589832 | tf_op jit(solution)/shard_map/ppermute | solution.py:466
  19.8 1.0 fusion.4
  20.9 1.3 %collective-permute-start.3 = (bf16[14,3,16,128]{3,2,1,0:T(8,128)(2,1)S(1)}, bf16[14,3,16,128]{3,2,1,0:T(8,128)(2,1)S(1)}, u32[]{:S(2)}, u32[]{:S(2)}) collective-permute-start(bf16[14,3,16,128]{3,2,1,0:T(8,128)(2,1)S(1)} %get-tuple-element.16), channel_id=1, source_target_pairs={{1,0},{2,1},{3,2},{5,4},{6,5},{7,6},{9,8},{10,9},{11,10},{13,12},{... | collective-permute-start | bytes 516104 | tf_op jit(solution)/shard_map/ppermute | solution.py:467
  22.2 3.0 %collective-permute-start.2 = (bf16[14,3,16,128]{3,2,1,0:T(8,128)(2,1)S(1)}, bf16[14,3,16,128]{3,2,1,0:T(8,128)(2,1)S(1)}, u32[]{:S(2)}, u32[]{:S(2)}) collective-permute-start(bf16[14,3,16,128]{3,2,1,0:T(8,128)(2,1)S(1)} %get-tuple-element.17), channel_id=1, source_target_pairs={{0,1},{1,2},{2,3},{4,5},{5,6},{6,7},{8,9},{9,10},{10,11},{12,13},{... | collective-permute-start | bytes 516104 | tf_op jit(solution)/shard_map/ppermute | solution.py:466
  25.3 1.0 collective-permute-done.2.left
  26.9 18.9 %shard_map.95 = (bf16[10,18,16,128]{3,2,1,0:T(8,128)(2,1)}, bf16[10,18,16,128]{3,2,1,0:T(8,128)(2,1)}, f32[8,256,128]{2,1,0:T(8,128)}, f32[10,288,128]{2,1,0:T(8,128)}, bf16[8,8,128]{2,1,0:T(8,128)(2,1)}) custom-call(bf16[8,16,16,128]{3,2,1,0:T(8,128)(2,1)} %copy-done.1, bf16[3,16,16,128]{3,2,1,0:T(8,128)(2,1)} %copy-done.4, ...), custom_call_target="tpu_custom_call" | custom-call | tf_op jit(solution)/shard_map/pallas_call | solution.py:541
  45.8 1.5 %broadcast_in_dim.9 = bf16[8,8,8,128]{3,2,1,0:T(8,128)(2,1)} broadcast(bf16[8,8,128]{2,1,0:T(8,128)(2,1)} %get-tuple-element.9), dimensions={1,2,3} | broadcast | bytes 147456 | tf_op jit(solution)/shard_map/broadcast_in_dim | solution.py:474
  47.3 6.6 %all-to-all-start = ((bf16[8,8,8,128]{3,2,1,0:T(8,128)(2,1)}), bf16[8,8,8,128]{3,2,1,0:T(8,128)(2,1)S(1)}, u32[]{:S(2)}, u32[]{:S(2)}) async-start(bf16[8,8,8,128]{3,2,1,0:T(8,128)(2,1)} %broadcast_in_dim.9), calls=%async_computation | async-start | bytes 262144 | tf_op jit(solution)/shard_map/all_to_all | solution.py:473
  55.5 3.3 %rev.15 = bf16[3,9,128,128]{2,0,3,1:T(4,128)(2,1)S(1)} reverse(bf16[3,9,128,128]{2,0,3,1:T(4,128)(2,1)S(1)} %copy.45), dimensions={0,1} | reverse | bytes 1769472 | tf_op jit(solution)/shard_map/rev | solution.py:520
  58.8 1.1 copy.53
  61.3 1.3 %copy.46 = bf16[2,4,8,2,3,16,8]{6,5,4,3,2,1,0:T(8,128)(2,1)S(1)} copy(bf16[2,4,8,2,3,16,8]{5,2,1,0,6,3,4:T(8,128)(2,1)S(1)} %bitcast.76) | data formatting | bytes 196608 | tf_op jit(solution)/shard_map/reshape | solution.py:494
  62.7 1.8 %reshape.78 = bf16[8,8,6,128]{3,2,1,0:T(8,128)(2,1)S(1)} reshape(bf16[2,4,8,2,3,16,8]{6,5,4,3,2,1,0:T(8,128)(2,1)S(1)} %copy.46) | data formatting | bytes 196608 | tf_op jit(solution)/shard_map/reshape | solution.py:494
  65.2 12.6 %shard_map.96 = (f32[16,336,128]{2,1,0:T(8,128)}, f32[8,144,256]{2,1,0:T(8,128)}) custom-call(bf16[8,8,8,128]{3,2,1,0:T(8,128)(2,1)} %pad.60.guides, bf16[128,128]{1,0:T(8,128)(2,1)} %copy-done.7, bf16[1152,128]{1,0:T(8,128)(2,1)} %bitcast.77, bf16[1152,256]{1,0:T(8,128)(2,1)} %bitcast.69), custom_call_target="tpu_custom_call" | custom-call | tf_op jit(solution)/shard_map/pallas_call | solution.py:532
  78.5 35.6 %shard_map.97 = bf16[8,2,108,128]{3,2,1,0:T(8,128)(2,1)} custom-call(bf16[8,8,8,128]{3,2,1,0:T(8,128)(2,1)} %copy-done.6, bf16[8,8,8,128]{3,2,1,0:T(8,128)(2,1)} %pad.60.guides, f32[16,336,128]{2,1,0:T(8,128)} %get-tuple-element.10.guide_2, f32[8,144,256]{2,1,0:T(8,128)} %get-tuple-element.11.guide_3, f32[8,256,128]{2,1,0:T(8,128)} %get-tuple-element.12.slope_first, ...), custom_call_target="tpu_custom_call" | custom-call | tf_op jit(solution)/shard_map/pallas_call | solution.py:568
  114.0 1.0 slice_bitcast_fusion.8
  115.6 2.2 %collective-permute-start.10 = (bf16[2,108,128]{2,1,0:T(8,128)(2,1)S(1)}, bf16[2,108,128]{2,1,0:T(8,128)(2,1)S(1)}, u32[]{:S(2)}, u32[]{:S(2)}) collective-permute-start(bf16[2,108,128]{2,1,0:T(8,128)(2,1)S(1)} %get-tuple-element.21), channel_id=1, source_target_pairs={{0,7},{1,0},{2,1},{3,2},{4,3},{5,4},{6,5},{7,6},{8,15},{9,8},{10,9... | collective-permute-start | bytes 165896 | tf_op jit(solution)/shard_map/ppermute | solution.py:597
  117.8 2.0 %collective-permute-start.9 = (bf16[2,108,128]{2,1,0:T(8,128)(2,1)S(1)}, bf16[2,108,128]{2,1,0:T(8,128)(2,1)S(1)}, u32[]{:S(2)}, u32[]{:S(2)}) collective-permute-start(bf16[2,108,128]{2,1,0:T(8,128)(2,1)S(1)} %get-tuple-element.22), channel_id=1, source_target_pairs={{0,6},{1,7},{2,0},{3,1},{4,2},{5,3},{6,4},{7,5},{8,14},{9,15},{10,... | collective-permute-start | bytes 165896 | tf_op jit(solution)/shard_map/ppermute | solution.py:597
  120.5 1.5 %collective-permute-start.6 = (bf16[2,108,128]{2,1,0:T(8,128)(2,1)S(1)}, bf16[2,108,128]{2,1,0:T(8,128)(2,1)S(1)}, u32[]{:S(2)}, u32[]{:S(2)}) collective-permute-start(bf16[2,108,128]{2,1,0:T(8,128)(2,1)S(1)} %get-tuple-element.25), channel_id=1, source_target_pairs={{0,3},{1,4},{2,5},{3,6},{4,7},{5,0},{6,1},{7,2},{8,11},{9,12},{10,... | collective-permute-start | bytes 165896 | tf_op jit(solution)/shard_map/ppermute | solution.py:597
  122.0 2.1 %collective-permute-start.5 = (bf16[2,108,128]{2,1,0:T(8,128)(2,1)S(1)}, bf16[2,108,128]{2,1,0:T(8,128)(2,1)S(1)}, u32[]{:S(2)}, u32[]{:S(2)}) collective-permute-start(bf16[2,108,128]{2,1,0:T(8,128)(2,1)S(1)} %get-tuple-element.26), channel_id=1, source_target_pairs={{0,2},{1,3},{2,4},{3,5},{4,6},{5,7},{6,0},{7,1},{8,10},{9,11},{10,... | collective-permute-start | bytes 165896 | tf_op jit(solution)/shard_map/ppermute | solution.py:597
  124.2 1.0 collective-permute-done.7
  125.8 1.5 %collective-permute-done.5 = bf16[2,108,128]{2,1,0:T(8,128)(2,1)S(1)} collective-permute-done((bf16[2,108,128]{2,1,0:T(8,128)(2,1)S(1)}, bf16[2,108,128]{2,1,0:T(8,128)(2,1)S(1)}, u32[]{:S(2)}, u32[]{:S(2)}) %collective-permute-start.5) | collective-permute-done | bytes 55328 | tf_op jit(solution)/shard_map/ppermute | solution.py:597
  (78 shorter events, 15.2 us)
Async XLA Ops:
  0.6 0.7 copy-start
  1.4 13.4 %copy-start.11 = (bf16[27,64]{1,0:T(8,128)(2,1)S(1)}, bf16[27,64]{1,0:T(8,128)(2,1)}, u32[]{:S(2)}) copy-start(bf16[27,64]{1,0:T(8,128)(2,1)} %param.13) | copy-start | bytes 10372
  1.4 13.5 %copy-start.12 = (bf16[3,128]{1,0:T(4,128)(2,1)S(1)}, bf16[3,128]{1,0:T(4,128)(2,1)}, u32[]{:S(2)}) copy-start(bf16[3,128]{1,0:T(4,128)(2,1)} %param.12) | copy-start | bytes 2308
  1.4 14.8 %copy-start.10 = (bf16[576,64]{0,1:T(8,128)(2,1)S(1)}, bf16[576,64]{0,1:T(8,128)(2,1)}, u32[]{:S(2)}) copy-start(bf16[576,64]{0,1:T(8,128)(2,1)} %param.14) | copy-start | bytes 221188
  2.2 43.6 %all-to-all-start.1 = ((bf16[8,2,2304]{2,1,0:T(2,128)(2,1)}), bf16[8,2,2304]{2,1,0:T(2,128)(2,1)S(1)}, u32[]{:S(2)}, u32[]{:S(2)}) async-start(bf16[8,2,2304]{2,1,0:T(2,128)(2,1)} %reshape.79), calls=%async_computation.1 | async-start | bytes 147456 | tf_op jit(solution)/shard_map/all_to_all | solution.py:473
  8.7 8.5 %copy-start.5 = (bf16[576,128]{1,0:T(8,128)(2,1)S(1)}, bf16[576,128]{1,0:T(8,128)(2,1)}, u32[]{:S(2)}) copy-start(bf16[576,128]{1,0:T(8,128)(2,1)} %param.15) | copy-start | bytes 442372
  8.8 12.0 %collective-permute-start.1 = (bf16[3,16,16,128]{3,2,1,0:T(8,128)(2,1)S(1)}, bf16[3,16,16,128]{3,2,1,0:T(8,128)(2,1)S(1)}, u32[]{:S(2)}, u32[]{:S(2)}) collective-permute-start(bf16[3,16,16,128]{3,2,1,0:T(8,128)(2,1)S(1)} %get-tuple-element.18), channel_id=1, source_target_pairs={{4,0},{5,1},{6,2},{7,3},{12,8},{13,9},{14,10},{15,11},{20,16},{21,... | collective-permute-start | bytes 589832 | tf_op jit(solution)/shard_map/ppermute | solution.py:467
  10.2 10.6 %collective-permute-start = (bf16[3,16,16,128]{3,2,1,0:T(8,128)(2,1)S(1)}, bf16[3,16,16,128]{3,2,1,0:T(8,128)(2,1)S(1)}, u32[]{:S(2)}, u32[]{:S(2)}) collective-permute-start(bf16[3,16,16,128]{3,2,1,0:T(8,128)(2,1)S(1)} %get-tuple-element.19), channel_id=1, source_target_pairs={{0,4},{1,5},{2,6},{3,7},{8,12},{9,13},{10,14},{11,15},{16,20},{17,... | collective-permute-start | bytes 589832 | tf_op jit(solution)/shard_map/ppermute | solution.py:466
  17.3 3.5 %copy-start.1 = (bf16[8,16,16,128]{3,2,1,0:T(8,128)(2,1)}, bf16[8,16,16,128]{3,2,1,0:T(8,128)(2,1)S(1)}, u32[]{:S(2)}) copy-start(bf16[8,16,16,128]{3,2,1,0:T(8,128)(2,1)S(1)} %pad.57.own) | copy-start | bytes 1572868
  18.5 41.4 %copy-start.7 = (bf16[128,128]{1,0:T(8,128)(2,1)}, bf16[128,128]{1,0:T(8,128)(2,1)S(1)}, u32[]{:S(2)}) copy-start(bf16[128,128]{1,0:T(8,128)(2,1)S(1)} %pad.62.weight_1) | copy-start | bytes 98308
  20.8 5.4 %copy-start.3 = (bf16[3,16,16,128]{3,2,1,0:T(8,128)(2,1)}, bf16[3,16,16,128]{3,2,1,0:T(8,128)(2,1)S(1)}, u32[]{:S(2)}) copy-start(bf16[3,16,16,128]{3,2,1,0:T(8,128)(2,1)S(1)} %collective-permute-done.1.down) | copy-start | bytes 589828
  20.8 5.4 %copy-start.4 = (bf16[3,16,16,128]{3,2,1,0:T(8,128)(2,1)}, bf16[3,16,16,128]{3,2,1,0:T(8,128)(2,1)S(1)}, u32[]{:S(2)}) copy-start(bf16[3,16,16,128]{3,2,1,0:T(8,128)(2,1)S(1)} %collective-permute-done.up) | copy-start | bytes 589828
  20.9 4.4 %collective-permute-start.3 = (bf16[14,3,16,128]{3,2,1,0:T(8,128)(2,1)S(1)}, bf16[14,3,16,128]{3,2,1,0:T(8,128)(2,1)S(1)}, u32[]{:S(2)}, u32[]{:S(2)}) collective-permute-start(bf16[14,3,16,128]{3,2,1,0:T(8,128)(2,1)S(1)} %get-tuple-element.16), channel_id=1, source_target_pairs={{1,0},{2,1},{3,2},{5,4},{6,5},{7,6},{9,8},{10,9},{11,10},{13,12},{... | collective-permute-start | bytes 516104 | tf_op jit(solution)/shard_map/ppermute | solution.py:467
  22.2 4.1 %collective-permute-start.2 = (bf16[14,3,16,128]{3,2,1,0:T(8,128)(2,1)S(1)}, bf16[14,3,16,128]{3,2,1,0:T(8,128)(2,1)S(1)}, u32[]{:S(2)}, u32[]{:S(2)}) collective-permute-start(bf16[14,3,16,128]{3,2,1,0:T(8,128)(2,1)S(1)} %get-tuple-element.17), channel_id=1, source_target_pairs={{0,1},{1,2},{2,3},{4,5},{5,6},{6,7},{8,9},{9,10},{10,11},{12,13},{... | collective-permute-start | bytes 516104 | tf_op jit(solution)/shard_map/ppermute | solution.py:466
  25.3 1.0 copy-start.8
  45.8 8.9 %copy-start.2 = (bf16[3456,128]{1,0:T(8,128)(2,1)S(1)}, bf16[3456,128]{1,0:T(8,128)(2,1)}, u32[]{:S(2)}) copy-start(bf16[3456,128]{1,0:T(8,128)(2,1)} %second.1) | copy-start | bytes 2654212
  47.3 30.5 %all-to-all-start = ((bf16[8,8,8,128]{3,2,1,0:T(8,128)(2,1)}), bf16[8,8,8,128]{3,2,1,0:T(8,128)(2,1)S(1)}, u32[]{:S(2)}, u32[]{:S(2)}) async-start(bf16[8,8,8,128]{3,2,1,0:T(8,128)(2,1)} %broadcast_in_dim.9), calls=%async_computation | async-start | bytes 262144 | tf_op jit(solution)/shard_map/all_to_all | solution.py:473
  115.0 5.5 %collective-permute-start.4 = (bf16[2,108,128]{2,1,0:T(8,128)(2,1)S(1)}, bf16[2,108,128]{2,1,0:T(8,128)(2,1)S(1)}, u32[]{:S(2)}, u32[]{:S(2)}) collective-permute-start(bf16[2,108,128]{2,1,0:T(8,128)(2,1)S(1)} %get-tuple-element.20), channel_id=1, source_target_pairs={{0,1},{1,2},{2,3},{3,4},{4,5},{5,6},{6,7},{7,0},{8,9},{9,10},{10,1... | collective-permute-start | bytes 165896 | tf_op jit(solution)/shard_map/ppermute | solution.py:597
  115.6 6.4 %collective-permute-start.10 = (bf16[2,108,128]{2,1,0:T(8,128)(2,1)S(1)}, bf16[2,108,128]{2,1,0:T(8,128)(2,1)S(1)}, u32[]{:S(2)}, u32[]{:S(2)}) collective-permute-start(bf16[2,108,128]{2,1,0:T(8,128)(2,1)S(1)} %get-tuple-element.21), channel_id=1, source_target_pairs={{0,7},{1,0},{2,1},{3,2},{4,3},{5,4},{6,5},{7,6},{8,15},{9,8},{10,9... | collective-permute-start | bytes 165896 | tf_op jit(solution)/shard_map/ppermute | solution.py:597
  117.8 6.4 %collective-permute-start.9 = (bf16[2,108,128]{2,1,0:T(8,128)(2,1)S(1)}, bf16[2,108,128]{2,1,0:T(8,128)(2,1)S(1)}, u32[]{:S(2)}, u32[]{:S(2)}) collective-permute-start(bf16[2,108,128]{2,1,0:T(8,128)(2,1)S(1)} %get-tuple-element.22), channel_id=1, source_target_pairs={{0,6},{1,7},{2,0},{3,1},{4,2},{5,3},{6,4},{7,5},{8,14},{9,15},{10,... | collective-permute-start | bytes 165896 | tf_op jit(solution)/shard_map/ppermute | solution.py:597
  119.8 4.4 %collective-permute-start.8 = (bf16[2,108,128]{2,1,0:T(8,128)(2,1)S(1)}, bf16[2,108,128]{2,1,0:T(8,128)(2,1)S(1)}, u32[]{:S(2)}, u32[]{:S(2)}) collective-permute-start(bf16[2,108,128]{2,1,0:T(8,128)(2,1)S(1)} %get-tuple-element.23), channel_id=1, source_target_pairs={{0,5},{1,6},{2,7},{3,0},{4,1},{5,2},{6,3},{7,4},{8,13},{9,14},{10,... | collective-permute-start | bytes 165896 | tf_op jit(solution)/shard_map/ppermute | solution.py:597
  119.8 5.4 %collective-permute-start.7 = (bf16[2,108,128]{2,1,0:T(8,128)(2,1)S(1)}, bf16[2,108,128]{2,1,0:T(8,128)(2,1)S(1)}, u32[]{:S(2)}, u32[]{:S(2)}) collective-permute-start(bf16[2,108,128]{2,1,0:T(8,128)(2,1)S(1)} %get-tuple-element.24), channel_id=1, source_target_pairs={{0,4},{1,5},{2,6},{3,7},{4,0},{5,1},{6,2},{7,3},{8,12},{9,13},{10,... | collective-permute-start | bytes 165896 | tf_op jit(solution)/shard_map/ppermute | solution.py:597
  120.5 5.2 %collective-permute-start.6 = (bf16[2,108,128]{2,1,0:T(8,128)(2,1)S(1)}, bf16[2,108,128]{2,1,0:T(8,128)(2,1)S(1)}, u32[]{:S(2)}, u32[]{:S(2)}) collective-permute-start(bf16[2,108,128]{2,1,0:T(8,128)(2,1)S(1)} %get-tuple-element.25), channel_id=1, source_target_pairs={{0,3},{1,4},{2,5},{3,6},{4,7},{5,0},{6,1},{7,2},{8,11},{9,12},{10,... | collective-permute-start | bytes 165896 | tf_op jit(solution)/shard_map/ppermute | solution.py:597
  122.0 5.2 %collective-permute-start.5 = (bf16[2,108,128]{2,1,0:T(8,128)(2,1)S(1)}, bf16[2,108,128]{2,1,0:T(8,128)(2,1)S(1)}, u32[]{:S(2)}, u32[]{:S(2)}) collective-permute-start(bf16[2,108,128]{2,1,0:T(8,128)(2,1)S(1)} %get-tuple-element.26), channel_id=1, source_target_pairs={{0,2},{1,3},{2,4},{3,5},{4,6},{5,7},{6,0},{7,1},{8,10},{9,11},{10,... | collective-permute-start | bytes 165896 | tf_op jit(solution)/shard_map/ppermute | solution.py:597
  (2 other events, 1.3 us)
where the time goes:
time: 129 us
  Pallas kernels  67.1 us (52%)
  starting transfers between devices  31.2 us (24%)
  local copies, waits for them, and re-layouts  20.8 us (16%)
  other arithmetic  4.58 us (4%)
  waiting for transfers between devices  4.06 us (3%)
    pallas_call x1, Pallas kernels, local(): call(functools.partial(backward_kernel, frames, out_rows), jax.ShapeDtype...  35.6 us
    pallas_call x1, Pallas kernels, local(): call(functools.partial(forward_kernel, frames), (jax.ShapeDtypeStruct((ro...  18.9 us
    pallas_call x1, Pallas kernels, local(): call(functools.partial(guide_kernel, (rows, cols, half)), (jax.ShapeDtype...  12.6 us
    all_to_all x2, starting transfers between devices, gather_plane(): lax.all_to_all(jnp.broadcast_to(shard[None], (count,) + shard.shape), pla...  11.8 us
    ppermute x7, starting transfers between devices, local(): pieces.append(lax.ppermute(terms[step], plane, ring))  9.11 us
    ppermute x2, starting transfers between devices, exchange(): before = lax.ppermute(last, axis, [(i, i + 1) for i in range(count - 1)])  7.61 us
    unnamed x33, local copies, waits for them, and re-layouts  4.59 us
    rev x1, local copies, waits for them, and re-layouts, local(): back_volume = conv_second.reshape(3, 9, channels, channels)[::-1, ::-1]  3.29 us
  transfers between devices with their start and end apart: 13, of which 4 were waited for; matrix products, arithmetic and copies ran while one was open for 14% of the time, Pallas kernels for 25%

commit v1 on v0

v1 whole, which is shorter than its diff:
```python
import functools

import jax
import jax.numpy as jnp
from jax import lax
from jax.experimental import pallas as pl
from jax.experimental.pallas import tpu as pltpu
from jax.sharding import PartitionSpec as P

gelu_scale = 0.7978845608028654
gelu_cubic = 0.044715
plane = ("row", "col")
vmem_bytes = 62 * 2**20


def repeat(count, body, unroll=1):
    lax.fori_loop(0, count, lambda i, carry: (body(i), carry)[1], 0, unroll=unroll)


def matmul(left, right):
    return jnp.dot(left, right, preferred_element_type=jnp.float32)


def gelu_tanh(z):
    return jnp.tanh(gelu_scale * (z + gelu_cubic * z * z * z))


def gelu_slope(z, t):
    return 0.5 * (1.0 + t) + 0.5 * z * (1.0 - t * t) * gelu_scale * (
        1.0 + 3.0 * gelu_cubic * z * z
    )


def split(rows, frames_own):
    small = frames_own <= 4 and lax.axis_size("row") == 2 and rows % 4 == 0
    return (2, 4) if small else (1, 8)


def corner(rows, cols):
    height, width = rows * lax.axis_size("row"), cols * lax.axis_size("col")
    view_rows, view_cols = min(height, rows + 20), min(width, cols + 20)
    top, left = lax.axis_index("row") * rows, lax.axis_index("col") * cols
    view_top = jnp.clip(top - 10, 0, height - view_rows)
    view_left = jnp.clip(left - 10, 0, width - view_cols)
    return top, left, view_top, view_left


def col_mask(first_col, cols, width, slots, frames):
    at = lax.broadcasted_iota(jnp.int32, (cols * slots, 1), 0)
    col = at // slots + first_col
    return (at % slots < frames) & (col >= 0) & (col < width)


def conv_frames(source, row, cols, weight):
    slots, channels = source.shape[-2:]
    slabs = [
        source[row + dr, pl.ds(dc, cols)].reshape(cols * slots, channels)
        for dr in range(3)
        for dc in range(3)
    ]
    sums = matmul(jnp.concatenate(slabs, axis=1), weight)
    count = cols * slots
    return (
        pltpu.roll(sums[:, :channels], 1, 0)
        + sums[:, channels : 2 * channels]
        + pltpu.roll(sums[:, 2 * channels :], count - 1, 0)
    )


def frame_weight(ref):
    third = ref.shape[0] // 3
    return jnp.concatenate([ref[pl.ds(third * k, third)] for k in range(3)], axis=1)


def weight_kernel(second, third, volume, weight_2, weight_3, back_2, back_3, back_volume):
    v1, v2, channels = second.shape[1], third.shape[1], volume.shape[1]
    zero_2 = jnp.zeros((v1, v1), jnp.bfloat16)
    zero_3 = jnp.zeros((v1, v2), jnp.bfloat16)
    for tap in range(9):
        taken = second[tap * v1 : (tap + 1) * v1]
        weight_2[tap * 2 * v1 : (tap * 2 + 1) * v1] = jnp.concatenate([taken, zero_2], axis=1)
        weight_2[(tap * 2 + 1) * v1 : (tap * 2 + 2) * v1] = jnp.concatenate(
            [zero_2, taken], axis=1
        )
        turned = jnp.concatenate([taken, zero_2], axis=0).astype(jnp.float32)
        at = (8 - tap) * 2 * v1
        turned = jnp.concatenate([turned, jnp.zeros_like(turned)], axis=1).T
        back_2[at : at + 2 * v1] = turned.astype(jnp.bfloat16)
        taken = third[tap * v1 : (tap + 1) * v1]
        weight_3[tap * 2 * v1 : (tap * 2 + 1) * v1] = jnp.concatenate([taken, zero_3], axis=1)
        weight_3[(tap * 2 + 1) * v1 : (tap * 2 + 2) * v1] = jnp.concatenate(
            [zero_3, taken], axis=1
        )
        turned = jnp.concatenate([taken, zero_3], axis=0).astype(jnp.float32).T
        back_3[(8 - tap) * v2 : (9 - tap) * v2] = turned.astype(jnp.bfloat16)
    for dt in range(3):
        for tap in range(9):
            at = (dt * 9 + tap) * channels
            turned = volume[at : at + channels].astype(jnp.float32).T.astype(jnp.bfloat16)
            back_volume[
                (8 - tap) * channels : (9 - tap) * channels,
                (2 - dt) * channels : (3 - dt) * channels,
            ] = turned


def forward_kernel(
    frames, parts, own, near, left, right, first, second, project, target,
    cells_out, hidden_out, slope_first, slope_second, payload,
    cells, hidden, spread_weight, picked, spaced, colour,
):
    rows, cols, slots, channels = own.shape
    groups, group = lax.axis_size("grp"), lax.axis_index("grp")
    height, width = rows * lax.axis_size("row"), cols * lax.axis_size("col")
    top, left_col = lax.axis_index("row") * rows, lax.axis_index("col") * cols
    cells[3 : 3 + rows, 3 : 3 + cols] = own[...]
    cells[0:3, 3 : 3 + cols] = near[0]
    cells[3 + rows :, 3 : 3 + cols] = near[1]
    cells[:, 0:3] = left[...]
    cells[:, 3 + cols :] = right[...]
    cells_out[...] = cells[2 : 4 + rows, 2 : 4 + cols]
    spread_weight[...] = frame_weight(first)

    def first_layer(r):
        pre = conv_frames(cells, r, cols + 4, spread_weight[...])
        row = top - 2 + r
        keep = col_mask(left_col - 2, cols + 4, width, slots, frames) & (
            (row >= 0) & (row < height)
        )
        gate = 0.5 + 0.5 * jnp.tanh(0.5 * pre)
        out = jnp.where(keep, pre * gate, 0.0).astype(jnp.bfloat16)
        hidden[r] = out.reshape(cols + 4, slots, channels)
        slope = jnp.where(keep, gate * (1.0 + pre * (1.0 - gate)), 0.0)

        @pl.when((r >= 2) & (r < 2 + rows))
        def _():
            slope_first[r - 2] = slope[2 * slots : (2 + cols) * slots]

    repeat(rows + 4, first_layer, 2)
    hidden_out[...] = hidden[1 : 3 + rows, 1 : 3 + cols]
    spread_weight[...] = frame_weight(second)
    own_slots = slots // groups
    spaced[...] = jnp.zeros(spaced.shape, jnp.float32)

    def second_layer(r):
        pre = conv_frames(hidden, r, cols + 2, spread_weight[...])
        row = top - 1 + r
        keep = col_mask(left_col - 1, cols + 2, width, slots, frames) & (
            (row >= 0) & (row < height)
        )
        gate = 0.5 + 0.5 * jnp.tanh(0.5 * pre)
        slope_second[r] = jnp.where(keep, gate * (1.0 + pre * (1.0 - gate)), 0.0)
        picked[...] = jnp.where(keep, pre * gate, 0.0)[slots : (1 + cols) * slots]
        mine = picked[pl.ds(group, cols * own_slots, stride=groups)]
        if parts > 1:
            part = lax.axis_index("row")
            spaced[pl.ds(part, cols * own_slots, stride=parts)] = mine
            mine = spaced[...]
        line = lax.dot_general(
            project[...], mine.astype(jnp.bfloat16), (((1,), (1,)), ((), ())),
            preferred_element_type=jnp.float32,
        )
        colour[jnp.clip(r - 1, -1, rows) + 1] = line

    repeat(rows + 2, second_layer, 2)
    lines = jnp.concatenate(
        [colour[1 : 1 + rows].reshape(rows * 8, colour.shape[2]).astype(jnp.bfloat16), target[...]],
        axis=0,
    )
    for k in range(payload.shape[0]):
        payload[k] = lines


def plane_slabs(wide, narrow, row, count, half):
    pieces = []
    for dr in range(3):
        pieces.append(wide[row + dr, pl.ds(0, count)])
        pieces.append(narrow[row + dr])
        pieces.append(wide[row + dr, pl.ds(2 * half, count)])
    return jnp.concatenate(pieces, axis=1)


def store_slab(wide, narrow, row, value, half):
    wide[row] = value.astype(jnp.bfloat16)
    narrow[row] = value[half : value.shape[0] - half].astype(jnp.bfloat16)


def store_wide(wide, narrow, row, value, half):
    edge = jnp.zeros((half, value.shape[1]), jnp.float32)
    store_slab(wide, narrow, row, jnp.concatenate([edge, value, edge], axis=0), half)


def fill_edges(parts, *refs):
    for ref in refs:
        last = ref.shape[0] - 1
        if parts == 1:
            for at in (0, last):
                ref[at] = jnp.zeros(ref.shape[1:], ref.dtype)
            continue
        part = lax.broadcasted_iota(jnp.int32, (ref.shape[1], 1), 0) % parts
        low = pltpu.roll(ref[last - 1].astype(jnp.float32), 1, 0)
        high = pltpu.roll(ref[1].astype(jnp.float32), ref.shape[1] - 1, 0)
        ref[0] = jnp.where(part > 0, low, 0.0).astype(ref.dtype)
        ref[last] = jnp.where(part < parts - 1, high, 0.0).astype(ref.dtype)


def kept_row(row, first, number):
    return jnp.clip(row - first, -1, number) + 1


def perceptual_kernel(
    shape, received, weight_1, weight_2, weight_3, back_3, back_2, back_1, pixels,
    target, strips, lines, wide_1, narrow_1, wide_3, narrow_3, wide_g, narrow_g,
    plane_1, plane_2, spread, wide_b, narrow_b, wide_a, narrow_a,
):
    rows, cols, blocks, block_frames, own, parts, own_slots, frames_own = shape
    f32, bf16 = jnp.float32, jnp.bfloat16
    half = parts * own_slots
    groups, group = lax.axis_size("grp"), lax.axis_index("grp")
    col_parts = lax.axis_size("col")
    width = cols * col_parts
    height = rows * lax.axis_size("row")
    view_rows, view_cols = min(height, rows + 20), min(width, cols + 20)
    top, left, view_top, view_left = corner(rows, cols)
    number = view_rows // parts
    count = view_cols * half
    lanes = lines.shape[2]
    span = width * half
    v1 = weight_2.shape[1] // 2
    v2 = weight_3.shape[1] // 2
    base = rows * 8
    body = pl.ds(3 * half, count)

    for device in range(received.shape[0]):
        target[device] = received[device, base:].astype(f32)
    strips[...] = jnp.zeros(strips.shape, f32)
    for j in range(frames_own):
        frame = groups * j + group
        block, rest = frame // block_frames, frame % block_frames
        for part in range(parts):
            for k in range(3):
                start = ((k * blocks + block) * own + rest % own) * rows

                def take(at, j=j, part=part, k=k, start=start, rest=rest):
                    row = view_top + part * number + at
                    device = (row // rows) * col_parts + rest // own
                    strips[j * parts + part, pl.ds(at * 8 + 3 + k, 1)] = target[
                        device, pl.ds(start + row % rows, 1)
                    ]

                if parts > 1:
                    device = part * col_parts + rest // own
                    strips[j * parts + part, pl.ds(3 + k, rows, stride=8)] = target[
                        device, pl.ds(pl.multiple_of(start, 8) if rows % 8 == 0 else start, rows)
                    ]
                else:
                    repeat(number, take)
    from_col = lax.broadcasted_iota(jnp.int32, (target.shape[2], lanes), 0) - view_left
    to_lane = lax.broadcasted_iota(jnp.int32, (target.shape[2], lanes), 1)
    guide = 0.0
    for j in range(frames_own):
        for part in range(parts):
            place = (from_col * half + (j * parts + part) == to_lane) & (to_lane < count)
            guide = guide + matmul(
                strips[j * parts + part].astype(bf16),
                jnp.where(place, 1.0, 0.0).astype(bf16),
            )
    lane = lax.broadcasted_iota(jnp.int32, (8, lanes), 1)
    strips_line = lines.at[pl.ds(1, number)]
    for at in range(number):
        strips_line[at, pl.ds(8, 8)] = guide[at * 8 : at * 8 + 8]

    def line_step(at):
        line = 0.0
        for part in range(parts):
            row = view_top + part * number + at
            source = pl.ds(pl.multiple_of(row % rows * 8, 8), 8)
            line = line + jnp.concatenate(
                [
                    received[(row // rows) * col_parts + k, source].astype(f32)[:, : cols * half]
                    for k in range(col_parts)
                ],
                axis=1,
            )
        line = pltpu.roll(line, lax.rem(span - view_left * half, span), 1)[:, :lanes]
        line = jnp.where(lane < count, line, 0.0) + lines[at + 1, pl.ds(8, 8)]
        before = jnp.where(lane < half, 0.0, pltpu.roll(line, half, 1))
        after = jnp.where(lane >= count - half, 0.0, pltpu.roll(line, lanes - half, 1))
        lines[at + 1] = jnp.concatenate([before, line, after], axis=0)

    repeat(number, line_step, 2)
    wide_lane = lax.broadcasted_iota(jnp.int32, (24, lanes), 1)
    if parts > 1:
        part = wide_lane % parts
        inside = wide_lane < count
        low = pltpu.roll(lines[number], 1, 1)
        high = pltpu.roll(lines[1], lanes - 1, 1)
        lines[0] = jnp.where((part > 0) & inside, low, 0.0)
        lines[number + 1] = jnp.where((part < parts - 1) & inside, high, 0.0)
    else:
        lines[0] = jnp.zeros((24, lanes), f32)
        lines[number + 1] = jnp.zeros((24, lanes), f32)

    def first_step(at):
        pieces = [lines[at], lines[at + 1], lines[at + 2], jnp.zeros((56, lanes), f32)]
        patches = jnp.concatenate(pieces, axis=0).T[:count].astype(bf16)
        z = matmul(patches, weight_1[...])
        plane_1[at, body] = z
        store_wide(wide_1, narrow_1, at + 1, 0.5 * z * (1.0 + gelu_tanh(z)), half)

    repeat(number, first_step, 4)
    fill_edges(parts, wide_1, narrow_1)

    def second_step(q):
        total = 0.0
        for step in range(2):
            at = 2 * q + step
            z = matmul(plane_slabs(wide_1, narrow_1, at, count, half), weight_2[...])
            plane_2[at, body] = z
            total = total + 0.5 * z * (1.0 + gelu_tanh(z))
        pooled = total.reshape(view_cols // 2, 2, half, 2 * v1)
        pooled = 0.25 * (pooled[:, 0] + pooled[:, 1])
        store_wide(wide_3, narrow_3, q + 1, pooled.reshape(count // 2, 2 * v1), half)

    repeat(number // 2, second_step, 2)
    fill_edges(parts, wide_3, narrow_3)

    def third_step(q):
        z = matmul(plane_slabs(wide_3, narrow_3, q, count // 2, half), weight_3[...])
        t = gelu_tanh(z)
        value = 0.5 * z * (1.0 + t)
        delta = (64.0 / v2) * (value[:, :v2] - value[:, v2:]) * gelu_slope(z[:, :v2], t[:, :v2])
        store_wide(wide_g, narrow_g, q + 1, delta, half)

    repeat(number // 2, third_step, 2)
    fill_edges(parts, wide_g, narrow_g)

    def pool_step(q):
        grad = 0.25 * matmul(plane_slabs(wide_g, narrow_g, q, count // 2, half), back_3[...])
        grad = grad.reshape(view_cols // 2, 1, half, 2 * v1)
        spread[q, body] = jnp.concatenate([grad, grad], axis=1).reshape(count, 2 * v1)

    repeat(number // 2, pool_step, 2)

    def near(reach):
        size = (cols + 2 * reach) * half
        keep = col_mask(left - reach, cols + 2 * reach, width, half, half)
        start = pl.multiple_of((left - view_left + 3 - reach) * half, 8)
        return keep, pl.ds(start, size), size

    def second_delta(at):
        keep, where, _ = near(3)
        z = plane_2[at, where]
        t = gelu_tanh(z)
        value = 0.5 * z * (1.0 + t)
        delta = spread[at // 2, where] + (16.0 / v1) * (value - pltpu.roll(value, v1, 1))
        store_slab(wide_b, narrow_b, at + 1, jnp.where(keep, delta * gelu_slope(z, t), 0.0), half)

    repeat(number, second_delta, 2)
    fill_edges(parts, wide_b, narrow_b)

    def first_delta(at):
        keep, where, size = near(2)
        grad = matmul(plane_slabs(wide_b, narrow_b, at, size, half), back_2[...])
        z = plane_1[at, where]
        delta = jnp.where(keep, grad * gelu_slope(z, gelu_tanh(z)), 0.0)
        store_slab(wide_a, narrow_a, at + 1, delta, half)

    repeat(number, first_delta, 2)
    fill_edges(parts, wide_a, narrow_a)

    def pixel_step(at):
        size = (cols + 2) * half
        grad = lax.dot_general(
            back_1[...], plane_slabs(wide_a, narrow_a, at, size, half), (((1,), (1,)), ((), ())),
            preferred_element_type=f32,
        )
        line = lines[at + 1, pl.ds(8, 8)]
        line = line - pltpu.roll(line, 5, 0)
        shift = lax.rem((view_left - left + 1) * half + 2 * lanes, lanes)
        line = pltpu.roll(line, shift, 1)
        pixels[at] = (grad + (1.0 / 6.0) * line[:, :size]).astype(bf16)

    repeat(number, pixel_step, 2)


def gradient_taps(source, delta, shifted, sums, first_tap):
    rows = delta.shape[0]
    slots, channels = source.shape[-2:]
    cols = source.shape[1] - 2
    count = cols * slots

    def turn(r):
        block = delta[r].astype(jnp.float32)
        for dt in range(3):
            moved = block if dt == 1 else pltpu.roll(block, (dt - 1) % count, 0)
            shifted[dt, r] = moved.T.astype(jnp.bfloat16)

    repeat(rows, turn, 2)

    def tap_step(step):
        tap = jnp.minimum(first_tap + step, 26)
        dt, dr, dc = tap // 9, tap // 3 % 3, tap % 3
        total = 0.0
        for r in range(rows):
            slab = source[r + dr, pl.ds(dc, cols)].reshape(count, channels)
            total = total + matmul(shifted[dt, r], slab)
        sums[pl.ds(pl.multiple_of(step * channels, channels), channels)] = total.T

    repeat(sums.shape[0] // channels, tap_step, 4)


def backward_kernel(*refs, parts, out_rows, groups):
    pixels = refs[:groups]
    (
        slope_first, slope_second, cells, hidden, paint, back_second, terms,
        painted, hidden_grad, delta_second, delta_own, shifted, sums,
    ) = refs[groups:]
    slots, channels = cells.shape[-2:]
    rows, cols = cells.shape[0] - 2, cells.shape[1] - 2
    height = rows * lax.axis_size("row")
    view_rows = min(height, rows + 20)
    number = view_rows // parts
    own_slots = slots // groups
    group = lax.axis_index("grp")
    top, _, view_top, _ = corner(rows, cols)
    kept = (cols + 2) * own_slots

    def paint_step(at):
        for step in range(groups):
            source = lax.rem(group - step + groups, groups)
            slot = painted.at[step]
            slot[...] = lax.dot_general(
                pixels[step][at], paint[...], (((0,), (0,)), ((), ())),
                preferred_element_type=jnp.float32,
            )
            for part in range(parts):
                row = kept_row(view_top + part * number + at, top - 1, rows + 2)
                value = slot[pl.ds(part, kept, stride=parts)] if parts > 1 else slot[...]
                hidden_grad[row, pl.ds(source, kept, stride=groups)] = value

    repeat(number, paint_step, 2)

    def delta_step(a):
        row = top - 1 + a
        inside = (row >= 0) & (row < height)
        delta = jnp.where(inside, hidden_grad[a + 1] * slope_second[a], 0.0).astype(jnp.bfloat16)
        delta_second[a] = delta.reshape(cols + 2, slots, channels)

    repeat(rows + 2, delta_step, 2)

    first_row = lax.axis_index("grp") * out_rows
    first_tap = first_row // channels
    skip = pl.multiple_of(first_row - first_tap * channels, 32)
    device = lax.axis_index("row") * lax.axis_size("col") + lax.axis_index("col")

    def put(which):
        value = sums[pl.ds(skip, out_rows)]
        if len(terms.shape) == 3:
            terms[which] = value.astype(jnp.bfloat16)
        else:
            chunks, _, size, _ = terms.shape
            for k in range(chunks):
                piece = value[k * size : (k + 1) * size].astype(jnp.bfloat16)
                terms[lax.rem(k - device + chunks, chunks), which] = piece

    def own_step(r):
        delta_own[r] = delta_second[r + 1, 1 : 1 + cols].reshape(cols * slots, channels)

    repeat(rows, own_step, 2)
    gradient_taps(hidden, delta_own, shifted, sums, first_tap)
    put(1)

    def back_step(r):
        back = conv_frames(delta_second, r, cols, back_second[...])
        delta_own[r] = (back * slope_first[r]).astype(jnp.bfloat16)

    repeat(rows, back_step, 4)
    gradient_taps(cells, delta_own, shifted, sums, first_tap)
    put(0)


def call(kernel, outs, scratch, flops=0):
    return pl.pallas_call(
        kernel,
        out_shape=outs,
        scratch_shapes=[pltpu.VMEM(*shape) for shape in scratch],
        compiler_params=pltpu.CompilerParams(vmem_limit_bytes=vmem_bytes),
        cost_estimate=pl.CostEstimate(flops=flops, bytes_accessed=2**20, transcendentals=0),
    )


def plane_first_weights(vgg_first):
    taps = vgg_first.reshape(9, 3, -1)
    v1 = taps.shape[2]
    first = jnp.concatenate(
        [jnp.pad(taps, ((0, 0), (0, 0), (0, v1))), jnp.pad(taps, ((0, 0), (0, 0), (v1, 0)))], axis=1
    )
    first = jnp.pad(first, ((0, 0), (0, 2), (0, 0))).reshape(72, 2 * v1)
    back = jnp.transpose(taps[::-1], (1, 0, 2))
    back = jnp.pad(back, ((0, 5), (0, 0), (0, v1))).reshape(8, 9 * 2 * v1)
    return jnp.pad(first, ((0, 56), (0, 0))), back


def row_halo(own, width):
    count, length = lax.axis_size("row"), own.shape[0]
    if count == 2:
        second = lax.axis_index("row")
        edge = lax.dynamic_slice_in_dim(own, (1 - second) * (length - width), width, axis=0)
        came = lax.ppermute(edge, "row", [(0, 1), (1, 0)])
        place = (jnp.arange(2) == 1 - second).reshape(2, 1, 1, 1, 1)
        return jnp.where(place, came[None], jnp.zeros_like(came)[None])
    before = lax.ppermute(own[length - width :], "row", [(i, i + 1) for i in range(count - 1)])
    after = lax.ppermute(own[:width], "row", [(i + 1, i) for i in range(count - 1)])
    return jnp.stack([before, after])


def col_halo(tall, width):
    count, length = lax.axis_size("col"), tall.shape[1]
    before = lax.ppermute(
        tall[:, length - width :], "col", [(i, i + 1) for i in range(count - 1)]
    )
    after = lax.ppermute(tall[:, :width], "col", [(i + 1, i) for i in range(count - 1)])
    return before, after


def local(dec_input, target, conv_first, conv_second, rgb_weight, vgg_first, vgg_second, vgg_third):
    f32, bf16 = jnp.float32, jnp.bfloat16
    row_count, col_count = lax.axis_size("row"), lax.axis_size("col")
    groups, devices = lax.axis_size("grp"), row_count * col_count
    blocks, block_frames, rows, cols, channels = dec_input.shape
    frames = blocks * block_frames
    frames_own = frames // groups
    parts, own_slots = split(rows, frames_own)
    slots = own_slots * groups
    half = parts * own_slots
    height, width = rows * row_count, cols * col_count
    view_rows, view_cols = min(height, rows + 20), min(width, cols + 20)
    number, count = view_rows // parts, view_cols * half
    lanes = -(-count // 128) * 128
    v1, v2 = vgg_first.shape[1], vgg_third.shape[1]

    own = jnp.transpose(dec_input.reshape(frames, rows, cols, channels), (1, 2, 0, 3))
    own = jnp.pad(own, ((0, 0), (0, 0), (0, slots - frames), (0, 0)))
    near = row_halo(own, 3)
    tall = jnp.concatenate([near[0], own, near[1]], axis=0)
    before, after = col_halo(tall, 3)

    line = max(cols * half, -(-width // 128) * 128)
    own_target = target.reshape(-1, width)
    target_rows = own_target.shape[0]
    own_target = jnp.pad(own_target, ((0, 0), (0, line - width)))
    project = jnp.pad(rgb_weight, ((0, 5), (0, 0)))
    weight_1, back_1 = plane_first_weights(vgg_first)
    weight_2, weight_3, back_2, back_3, back_volume = call(
        weight_kernel,
        (
            jax.ShapeDtypeStruct((18 * v1, 2 * v1), bf16),
            jax.ShapeDtypeStruct((18 * v1, 2 * v2), bf16),
            jax.ShapeDtypeStruct((18 * v1, 2 * v1), bf16),
            jax.ShapeDtypeStruct((9 * v2, 2 * v1), bf16),
            jax.ShapeDtypeStruct((9 * channels, 3 * channels), bf16),
        ),
        [],
        2**30,
    )(vgg_second, vgg_third, conv_second)

    cells, hidden, slope_first, slope_second, payload = call(
        functools.partial(forward_kernel, frames, parts),
        (
            jax.ShapeDtypeStruct((rows + 2, cols + 2, slots, channels), bf16),
            jax.ShapeDtypeStruct((rows + 2, cols + 2, slots, channels), bf16),
            jax.ShapeDtypeStruct((rows, cols * slots, channels), f32),
            jax.ShapeDtypeStruct((rows + 2, (cols + 2) * slots, channels), f32),
            jax.ShapeDtypeStruct((devices, rows * 8 + target_rows, line), bf16),
        ),
        [
            ((rows + 6, cols + 6, slots, channels), bf16),
            ((rows + 4, cols + 4, slots, channels), bf16),
            ((9 * channels, 3 * channels), bf16),
            ((cols * slots, channels), f32),
            ((cols * half, channels), f32),
            ((rows + 2, 8, cols * half), f32),
        ],
        2**33,
    )(own, near, before, after, conv_first, conv_second, project, own_target)

    received = lax.all_to_all(payload, plane, split_axis=0, concat_axis=0, tiled=True)

    wide_count = count + 6 * half
    pixels = call(
        functools.partial(
            perceptual_kernel,
            (
                rows, cols, blocks, block_frames, target.shape[2], parts, own_slots, frames_own,
            ),
        ),
        jax.ShapeDtypeStruct((number, 8, (cols + 2) * half), bf16),
        [
            ((devices, target_rows, line), f32),
            ((frames_own * parts, number * 8, line), f32),
            ((number + 2, 24, lanes), f32),
            ((number + 2, count + 2 * half, 2 * v1), bf16),
            ((number + 2, count, 2 * v1), bf16),
            ((number // 2 + 2, count // 2 + 2 * half, 2 * v1), bf16),
            ((number // 2 + 2, count // 2, 2 * v1), bf16),
            ((number // 2 + 2, count // 2 + 2 * half, v2), bf16),
            ((number // 2 + 2, count // 2, v2), bf16),
            ((number, wide_count, 2 * v1), f32),
            ((number, wide_count, 2 * v1), f32),
            ((number // 2, wide_count, 2 * v1), f32),
            ((number + 2, (cols + 6) * half, 2 * v1), bf16),
            ((number + 2, (cols + 4) * half, 2 * v1), bf16),
            ((number + 2, (cols + 4) * half, 2 * v1), bf16),
            ((number + 2, (cols + 2) * half, 2 * v1), bf16),
        ],
        2**32,
    )(received, weight_1, weight_2, weight_3, back_3, back_2, back_1)

    gathered = [pixels]
    for step in range(1, groups):
        ring = [(i, (i + step) % groups) for i in range(groups)]
        gathered.append(lax.ppermute(pixels, "grp", ring))

    out_rows = conv_first.shape[0] // groups
    taps = max(
        -(-(g + 1) * out_rows // channels) - g * out_rows // channels for g in range(groups)
    )
    even = out_rows % devices == 0
    out_shape = (
        (devices, 2, out_rows // devices, channels) if even else (2, out_rows, channels)
    )
    terms = call(
        functools.partial(backward_kernel, parts=parts, out_rows=out_rows, groups=groups),
        jax.ShapeDtypeStruct(out_shape, bf16),
        [
            ((groups, (cols + 2) * half, channels), f32),
            ((rows + 4, (cols + 2) * slots, channels), f32),
            ((rows + 2, cols + 2, slots, channels), bf16),
            ((rows, cols * slots, channels), bf16),
            ((3, rows, channels, cols * slots), bf16),
            ((taps * channels, channels), f32),
        ],
        2**32,
    )(*gathered, slope_first, slope_second, cells, hidden, project, back_volume)

    if even:
        pieces = [terms[0]]
        for step in range(1, devices):
            ring = [(i, (i + step) % devices) for i in range(devices)]
            pieces.append(lax.ppermute(terms[step], plane, ring))
        total = sum(piece.astype(f32) for piece in pieces)
    else:
        pieces = jnp.swapaxes(terms.reshape(2, devices, -1), 0, 1)
        pieces = lax.all_to_all(pieces, plane, split_axis=0, concat_axis=0, tiled=True)
        total = jnp.sum(pieces.astype(f32), axis=0)
    return total[0].reshape(-1), total[1].reshape(-1)


def solution(mesh):
    in_specs = (
        P(None, None, "row", "col", None),
        P(None, None, "col", "row", None),
        P(),
        P(),
        P(),
        P(),
        P(),
        P(),
    )
    out_specs = (P(("grp", "row", "col")), P(("grp", "row", "col")))
    return jax.shard_map(local, mesh=mesh, in_specs=in_specs, out_specs=out_specs, check_vma=False)
```

time: 129 us -> 94.7 us (0.73)
  Pallas kernels: 67.1 us -> 44.6 us
  local copies, waits for them, and re-layouts: 20.8 us -> 8.47 us
  waiting for transfers between devices: 4.06 us -> 14.7 us
  starting transfers between devices: 31.2 us -> 24.5 us
  other arithmetic: 4.58 us -> 1.11 us
    pallas_call x3 -> x4, Pallas kernels: 67.1 us -> 44.6 us  [the longest x1 17.7 us: local(): call(functools.partial(forward_kernel, frames, parts), (jax.ShapeDtypeStr...]
    ppermute x4 -> x6, waiting for transfers between devices: 0.96 us -> 9.33 us  [the longest x1 3.94 us: col_halo(): lax.ppermute(tall[:, :width], 'col', [(i + 1, i) for i in range(count - 1)])]
    all_to_all x2 -> x1, starting transfers between devices: 11.8 us -> 6.3 us  [local(): lax.all_to_all(payload, plane, split_axis=0, concat_axis=0, tiled=True)]
    reshape x7 -> x3, local copies, waits for them, and re-layouts: 4.51 us -> 0.63 us  [the longest x1 0.61 us: plane_first_weights(): back = jnp.pad(back, ((0, 5), (0, 0), (0, v1))).reshape(8, 9 * 2 * v1)]
    concatenate x9 -> x2, other arithmetic: 3.67 us -> 0.13 us  [the longest x1 0.08 us: plane_first_weights(): jnp.concatenate([jnp.pad(taps, ((0, 0), (0, 0), (0, v1))), jnp.pad(taps,...]
    rev x1 -> x0, local copies, waits for them, and re-layouts: 3.29 us -> none  [local(): back_volume = conv_second.reshape(3, 9, channels, channels)[::-1, ::-1]]
    all_to_all x2 -> x1, waiting for transfers between devices: 0.01 us -> 2.35 us  [local(): lax.all_to_all(payload, plane, split_axis=0, concat_axis=0, tiled=True)]
    ppermute x7, starting transfers between devices: 9.11 us -> 7.05 us  [local(): pieces.append(lax.ppermute(terms[step], plane, ring))]
  transfers between devices with their start and end apart: 13 -> 14, of which waited for: 4 -> 9; matrix products, arithmetic and copies ran while one was open for 14% -> 4% of each run, Pallas kernels for 25% -> 3%
where the time goes in v1:
time: 94.7 us; the launch traced here: 94.2 us
  Pallas kernels  44.6 us (47%)
  starting transfers between devices  24.5 us (26%)
  waiting for transfers between devices  14.7 us (16%)
  local copies, waits for them, and re-layouts  8.47 us (9%)
  other arithmetic  1.11 us (1%)
    pallas_call x1, Pallas kernels, local(): call(functools.partial(forward_kernel, frames, parts), (jax.ShapeDtypeStr...  17.7 us
    pallas_call x1, Pallas kernels, local(): call(functools.partial(backward_kernel, parts=parts, out_rows=out_rows, g...  12.8 us
    pallas_call x1, Pallas kernels, local(): call(functools.partial(perceptual_kernel, (rows, cols, blocks, block_fram...  11.2 us
    ppermute x7, starting transfers between devices, local(): pieces.append(lax.ppermute(terms[step], plane, ring))  7.05 us
    all_to_all x1, starting transfers between devices, local(): lax.all_to_all(payload, plane, split_axis=0, concat_axis=0, tiled=True)  6.3 us
    ppermute x3, starting transfers between devices, local(): gathered.append(lax.ppermute(pixels, 'grp', ring))  5.52 us
    ppermute x1, waiting for transfers between devices, col_halo(): lax.ppermute(tall[:, :width], 'col', [(i + 1, i) for i in range(count - 1)])  3.94 us
    ppermute x1, starting transfers between devices, row_halo(): came = lax.ppermute(edge, 'row', [(0, 1), (1, 0)])  3.03 us
  transfers between devices with their start and end apart: 14, of which 9 were waited for; matrix products, arithmetic and copies ran while one was open for 4% of the time, Pallas kernels for 3%

profile of v1, /device:TPU:0, one launch (start us, length us, event | category | flops | bytes accessed | tf_op | source)
XLA Modules:
  0.0 94.2 jit_solution(12421861605898811692)
XLA Ops:
  0.7 1.3 %copy.15 = bf16[12,8,16,128]{3,0,2,1:T(8,128)(2,1)S(1)} copy(bf16[12,8,16,128]{3,2,1,0:T(8,128)(2,1)} %bitcast.40) | data formatting | bytes 786432 | tf_op jit(solution)/shard_map/reshape | solution.py:542
  2.0 3.0 %collective-permute-start = (bf16[3,16,16,128]{3,2,1,0:T(8,128)(2,1)S(1)}, bf16[3,16,16,128]{3,2,1,0:T(8,128)(2,1)S(1)}, u32[]{:S(2)}, u32[]{:S(2)}) collective-permute-start(bf16[3,16,16,128]{3,2,1,0:T(8,128)(2,1)S(1)} %constant_dynamic-slice_fusion), channel_id=1, source_target_pairs={{0,4},{4,0},{1,5},{5,1},{2,6},{6,2},{3,7},{7,3},{8,12},{12,8},{9,1... | collective-permute-start | bytes 589832 | tf_op jit(solution)/shard_map/ppermute | solution.py:509
  7.4 2.6 %collective-permute-done = bf16[3,16,16,128]{3,2,1,0:T(8,128)(2,1)S(1)} collective-permute-done((bf16[3,16,16,128]{3,2,1,0:T(8,128)(2,1)S(1)}, bf16[3,16,16,128]{3,2,1,0:T(8,128)(2,1)S(1)}, u32[]{:S(2)}, u32[]{:S(2)}) %collective-permute-start) | collective-permute-done | bytes 196640 | tf_op jit(solution)/shard_map/ppermute | solution.py:509
  10.2 1.3 %collective-permute-start.1 = (bf16[14,3,16,128]{3,2,1,0:T(8,128)(2,1)S(1)}, bf16[14,3,16,128]{3,2,1,0:T(8,128)(2,1)S(1)}, u32[]{:S(2)}, u32[]{:S(2)}) collective-permute-start(bf16[14,3,16,128]{3,2,1,0:T(8,128)(2,1)S(1)} %get-tuple-element.23), channel_id=1, source_target_pairs={{0,1},{1,2},{2,3},{4,5},{5,6},{6,7},{8,9},{9,10},{10,11},{12,13},{... | collective-permute-start | bytes 516104 | tf_op jit(solution)/shard_map/ppermute | solution.py:519
  11.5 1.3 %collective-permute-start.2 = (bf16[14,3,16,128]{3,2,1,0:T(8,128)(2,1)S(1)}, bf16[14,3,16,128]{3,2,1,0:T(8,128)(2,1)S(1)}, u32[]{:S(2)}, u32[]{:S(2)}) collective-permute-start(bf16[14,3,16,128]{3,2,1,0:T(8,128)(2,1)S(1)} %get-tuple-element.22), channel_id=1, source_target_pairs={{1,0},{2,1},{3,2},{5,4},{6,5},{7,6},{9,8},{10,9},{11,10},{13,12},{... | collective-permute-start | bytes 516104 | tf_op jit(solution)/shard_map/ppermute | solution.py:522
  12.8 3.9 %collective-permute-done.2.right = bf16[14,3,16,128]{3,2,1,0:T(8,128)(2,1)S(1)} collective-permute-done((bf16[14,3,16,128]{3,2,1,0:T(8,128)(2,1)S(1)}, bf16[14,3,16,128]{3,2,1,0:T(8,128)(2,1)S(1)}, u32[]{:S(2)}, u32[]{:S(2)}) %collective-permute-start.2) | collective-permute-done | bytes 172064 | tf_op jit(solution)/shard_map/ppermute | solution.py:522
  17.5 17.7 %shard_map.95 = (bf16[10,18,16,128]{3,2,1,0:T(8,128)(2,1)}, bf16[10,18,16,128]{3,2,1,0:T(8,128)(2,1)}, f32[8,256,128]{2,1,0:T(8,128)}, f32[10,288,128]{2,1,0:T(8,128)}, bf16[8,136,128]{2,1,0:T(8,128)(2,1)}) custom-call(bf16[8,16,16,128]{3,2,1,0:T(8,128)(2,1)} %copy-done, bf16[2,3,16,16,128]{4,3,2,1,0:T(8,128)(2,1)} %copy-done.1, ...), custom_call_target="tpu_custom_call" | custom-call | flops 8589934592 | bytes 1048576 | tf_op jit(solution)/shard_map/pallas_call | solution.py:567
  35.2 6.3 %all-to-all-start = ((bf16[8,136,128]{2,1,0:T(8,128)(2,1)}), bf16[8,136,128]{2,1,0:T(8,128)(2,1)S(1)}, u32[]{:S(2)}, u32[]{:S(2)}) async-start(bf16[8,136,128]{2,1,0:T(8,128)(2,1)} %get-tuple-element.12), calls=%async_computation | async-start | bytes 557056 | tf_op jit(solution)/shard_map/all_to_all | solution.py:587
  41.5 2.9 %shard_map.96 = (bf16[1152,128]{1,0:T(8,128)(2,1)}, bf16[1152,256]{1,0:T(8,128)(2,1)}, bf16[1152,128]{1,0:T(8,128)(2,1)}, bf16[1152,128]{1,0:T(8,128)(2,1)}, bf16[1152,384]{1,0:T(8,128)(2,1)}) custom-call(bf16[576,64]{1,0:T(8,128)(2,1)} %copy.13.second, bf16[576,128]{1,0:T(8,128)(2,1)} %third.1, bf16[3456,128]{1,0:T(8,128)(2,1)} %volume.1), custom_call_target="tpu_custom_call" | custom-call | flops 1073741824 | bytes 1048576 | tf_op jit(solution)/shard_map/pallas_call | solution.py:554
  45.6 2.4 %all-to-all-done.received = bf16[8,136,128]{2,1,0:T(8,128)(2,1)S(1)} async-done(((bf16[8,136,128]{2,1,0:T(8,128)(2,1)}), bf16[8,136,128]{2,1,0:T(8,128)(2,1)S(1)}, u32[]{:S(2)}, u32[]{:S(2)}) %all-to-all-start) | async-done | bytes 278560 | tf_op jit(solution)/shard_map/all_to_all | solution.py:587
  48.7 11.2 %shard_map.97.refs_0_ = bf16[8,8,144]{2,1,0:T(8,128)(2,1)} custom-call(bf16[8,136,128]{2,1,0:T(8,128)(2,1)} %copy-done.2, bf16[128,128]{1,0:T(8,128)(2,1)} %pad.38.weight_1, bf16[1152,128]{1,0:T(8,128)(2,1)} %get-tuple-element.13.weight_2, bf16[1152,256]{1,0:T(8,128)(2,1)} %get-tuple-element.14.weight_3, bf16[1152,128]{1,0:T(8,128)(2,1)} %get-tuple-element.15.back_3, ...), custom_call_target="tpu_custom_call" | custom-call | flops 4294967296 | bytes 1048576 | tf_op jit(solution)/shard_map/pallas_call | solution.py:590
  59.8 1.6 %collective-permute-start.3 = (bf16[8,8,144]{2,1,0:T(8,128)(2,1)}, bf16[8,8,144]{2,1,0:T(8,128)(2,1)S(1)}, u32[]{:S(2)}, u32[]{:S(2)}) collective-permute-start(bf16[8,8,144]{2,1,0:T(8,128)(2,1)} %shard_map.97.refs_0_), channel_id=1, source_target_pairs={{0,8},{8,16},{16,24},{24,0},{1,9},{9,17},{17,25},{25,1},{2,10},{10... | collective-permute-start | bytes 55304 | tf_op jit(solution)/shard_map/ppermute | solution.py:622
  61.4 2.6 %collective-permute-start.4 = (bf16[8,8,144]{2,1,0:T(8,128)(2,1)}, bf16[8,8,144]{2,1,0:T(8,128)(2,1)S(1)}, u32[]{:S(2)}, u32[]{:S(2)}) collective-permute-start(bf16[8,8,144]{2,1,0:T(8,128)(2,1)} %shard_map.97.refs_0_), channel_id=1, source_target_pairs={{0,16},{8,24},{16,0},{24,8},{1,17},{9,25},{17,1},{25,9},{2,18},{10... | collective-permute-start | bytes 55304 | tf_op jit(solution)/shard_map/ppermute | solution.py:622
  64.0 1.3 %collective-permute-start.5 = (bf16[8,8,144]{2,1,0:T(8,128)(2,1)}, bf16[8,8,144]{2,1,0:T(8,128)(2,1)S(1)}, u32[]{:S(2)}, u32[]{:S(2)}) collective-permute-start(bf16[8,8,144]{2,1,0:T(8,128)(2,1)} %shard_map.97.refs_0_), channel_id=1, source_target_pairs={{0,24},{8,0},{16,8},{24,16},{1,25},{9,1},{17,9},{25,17},{2,26},{10... | collective-permute-start | bytes 55304 | tf_op jit(solution)/shard_map/ppermute | solution.py:622
  65.8 1.0 %collective-permute-done.4.refs_2_ = bf16[8,8,144]{2,1,0:T(8,128)(2,1)S(1)} collective-permute-done((bf16[8,8,144]{2,1,0:T(8,128)(2,1)}, bf16[8,8,144]{2,1,0:T(8,128)(2,1)S(1)}, u32[]{:S(2)}, u32[]{:S(2)}) %collective-permute-start.4) | collective-permute-done | bytes 18464 | tf_op jit(solution)/shard_map/ppermute | solution.py:622
  66.8 1.3 %collective-permute-done.5.refs_3_ = bf16[8,8,144]{2,1,0:T(8,128)(2,1)S(1)} collective-permute-done((bf16[8,8,144]{2,1,0:T(8,128)(2,1)}, bf16[8,8,144]{2,1,0:T(8,128)(2,1)S(1)}, u32[]{:S(2)}, u32[]{:S(2)}) %collective-permute-start.5) | collective-permute-done | bytes 18464 | tf_op jit(solution)/shard_map/ppermute | solution.py:622
  68.7 12.8 %shard_map.98 = bf16[8,2,108,128]{3,2,1,0:T(8,128)(2,1)} custom-call(bf16[8,8,144]{2,1,0:T(8,128)(2,1)} %shard_map.97.refs_0_, bf16[8,8,144]{2,1,0:T(8,128)(2,1)} %copy-done.9, bf16[8,8,144]{2,1,0:T(8,128)(2,1)} %copy-done.10, bf16[8,8,144]{2,1,0:T(8,128)(2,1)} %copy-done.11, f32[8,256,128]{2,1,0:T(8,128)} %get-tuple-element.17.refs_4_, ...), custom_call_target="tpu_custom_call" | custom-call | flops 4294967296 | bytes 1048576 | tf_op jit(solution)/shard_map/pallas_call | solution.py:632
  81.5 1.0 %slice_bitcast_fusion.10 = (bf16[2,108,128]{2,1,0:T(8,128)(2,1)S(1)}, bf16[2,108,128]{2,1,0:T(8,128)(2,1)S(1)}, bf16[2,108,128]{2,1,0:T(8,128)(2,1)S(1)}, bf16[2...) fusion(bf16[8,2,108,128]{3,2,1,0:T(8,128)(2,1)} %shard_map.98), kind=kLoop, calls=%fused_computation.22 | loop fusion | bytes 774144 | tf_op jit(solution)/shard_map/squeeze | solution.py:650
  82.6 1.3 %collective-permute-start.11 = (bf16[2,108,128]{2,1,0:T(8,128)(2,1)S(1)}, bf16[2,108,128]{2,1,0:T(8,128)(2,1)S(1)}, u32[]{:S(2)}, u32[]{:S(2)}) collective-permute-start(bf16[2,108,128]{2,1,0:T(8,128)(2,1)S(1)} %get-tuple-element.26), channel_id=1, source_target_pairs={{0,6},{1,7},{2,0},{3,1},{4,2},{5,3},{6,4},{7,5},{8,14},{9,15},{10,... | collective-permute-start | bytes 165896 | tf_op jit(solution)/shard_map/ppermute | solution.py:650
  83.9 2.3 %collective-permute-start.12 = (bf16[2,108,128]{2,1,0:T(8,128)(2,1)S(1)}, bf16[2,108,128]{2,1,0:T(8,128)(2,1)S(1)}, u32[]{:S(2)}, u32[]{:S(2)}) collective-permute-start(bf16[2,108,128]{2,1,0:T(8,128)(2,1)S(1)} %get-tuple-element.25), channel_id=1, source_target_pairs={{0,7},{1,0},{2,1},{3,2},{4,3},{5,4},{6,5},{7,6},{8,15},{9,8},{10,9... | collective-permute-start | bytes 165896 | tf_op jit(solution)/shard_map/ppermute | solution.py:650
  86.7 1.8 %collective-permute-start.8 = (bf16[2,108,128]{2,1,0:T(8,128)(2,1)S(1)}, bf16[2,108,128]{2,1,0:T(8,128)(2,1)S(1)}, u32[]{:S(2)}, u32[]{:S(2)}) collective-permute-start(bf16[2,108,128]{2,1,0:T(8,128)(2,1)S(1)} %get-tuple-element.29), channel_id=1, source_target_pairs={{0,3},{1,4},{2,5},{3,6},{4,7},{5,0},{6,1},{7,2},{8,11},{9,12},{10,... | collective-permute-start | bytes 165896 | tf_op jit(solution)/shard_map/ppermute | solution.py:650
  88.5 1.2 %collective-permute-start.9 = (bf16[2,108,128]{2,1,0:T(8,128)(2,1)S(1)}, bf16[2,108,128]{2,1,0:T(8,128)(2,1)S(1)}, u32[]{:S(2)}, u32[]{:S(2)}) collective-permute-start(bf16[2,108,128]{2,1,0:T(8,128)(2,1)S(1)} %get-tuple-element.28), channel_id=1, source_target_pairs={{0,4},{1,5},{2,6},{3,7},{4,0},{5,1},{6,2},{7,3},{8,12},{9,13},{10,... | collective-permute-start | bytes 165896 | tf_op jit(solution)/shard_map/ppermute | solution.py:650
  89.6 1.1 %collective-permute-done.6 = bf16[2,108,128]{2,1,0:T(8,128)(2,1)S(1)} collective-permute-done((bf16[2,108,128]{2,1,0:T(8,128)(2,1)S(1)}, bf16[2,108,128]{2,1,0:T(8,128)(2,1)S(1)}, u32[]{:S(2)}, u32[]{:S(2)}) %collective-permute-start.6) | collective-permute-done | bytes 55328 | tf_op jit(solution)/shard_map/ppermute | solution.py:650
  90.7 1.2 %collective-permute-done.7 = bf16[2,108,128]{2,1,0:T(8,128)(2,1)S(1)} collective-permute-done((bf16[2,108,128]{2,1,0:T(8,128)(2,1)S(1)}, bf16[2,108,128]{2,1,0:T(8,128)(2,1)S(1)}, u32[]{:S(2)}, u32[]{:S(2)}) %collective-permute-start.7) | collective-permute-done | bytes 55328 | tf_op jit(solution)/shard_map/ppermute | solution.py:650
  (51 shorter events, 9.0 us)
Async XLA Ops:
  0.6 4.5 %copy-start.6 = (bf16[3,128]{1,0:T(4,128)(2,1)S(1)}, bf16[3,128]{1,0:T(4,128)(2,1)}, u32[]{:S(2)}) copy-start(bf16[3,128]{1,0:T(4,128)(2,1)} %param.12) | copy-start | bytes 2308
  0.6 5.2 %copy-start.4 = (bf16[3,3,1,8,64]{4,3,2,1,0:T(8,128)(2,1)S(1)}, bf16[3,3,1,8,64]{4,3,2,1,0:T(8,128)(2,1)}, u32[]{:S(2)}) copy-start(bf16[3,3,1,8,64]{4,3,2,1,0:T(8,128)(2,1)} %param.9) | copy-start | bytes 27652
  0.7 5.8 %copy-start.3 = (bf16[576,64]{0,1:T(8,128)(2,1)S(1)}, bf16[576,64]{0,1:T(8,128)(2,1)}, u32[]{:S(2)}) copy-start(bf16[576,64]{0,1:T(8,128)(2,1)} %param.14) | copy-start | bytes 221188
  0.7 6.6 %copy-start.5 = (bf16[27,64]{1,0:T(8,128)(2,1)S(1)}, bf16[27,64]{1,0:T(8,128)(2,1)}, u32[]{:S(2)}) copy-start(bf16[27,64]{1,0:T(8,128)(2,1)} %param.13) | copy-start | bytes 10372
  2.0 7.9 %collective-permute-start = (bf16[3,16,16,128]{3,2,1,0:T(8,128)(2,1)S(1)}, bf16[3,16,16,128]{3,2,1,0:T(8,128)(2,1)S(1)}, u32[]{:S(2)}, u32[]{:S(2)}) collective-permute-start(bf16[3,16,16,128]{3,2,1,0:T(8,128)(2,1)S(1)} %constant_dynamic-slice_fusion), channel_id=1, source_target_pairs={{0,4},{4,0},{1,5},{5,1},{2,6},{6,2},{3,7},{7,3},{8,12},{12,8},{9,1... | collective-permute-start | bytes 589832 | tf_op jit(solution)/shard_map/ppermute | solution.py:509
  5.2 5.0 %copy-start = (bf16[8,16,16,128]{3,2,1,0:T(8,128)(2,1)}, bf16[8,16,16,128]{3,2,1,0:T(8,128)(2,1)S(1)}, u32[]{:S(2)}) copy-start(bf16[8,16,16,128]{3,2,1,0:T(8,128)(2,1)S(1)} %pad.32.own) | copy-start | bytes 1572868
  10.1 6.7 %copy-start.1 = (bf16[2,3,16,16,128]{4,3,2,1,0:T(8,128)(2,1)}, bf16[2,3,16,16,128]{4,3,2,1,0:T(8,128)(2,1)S(1)}, u32[]{:S(2)}) copy-start(bf16[2,3,16,16,128]{4,3,2,1,0:T(8,128)(2,1)S(1)} %broadcast_select_fusion.near) | copy-start | bytes 1179652
  10.2 2.6 %collective-permute-start.1 = (bf16[14,3,16,128]{3,2,1,0:T(8,128)(2,1)S(1)}, bf16[14,3,16,128]{3,2,1,0:T(8,128)(2,1)S(1)}, u32[]{:S(2)}, u32[]{:S(2)}) collective-permute-start(bf16[14,3,16,128]{3,2,1,0:T(8,128)(2,1)S(1)} %get-tuple-element.23), channel_id=1, source_target_pairs={{0,1},{1,2},{2,3},{4,5},{5,6},{6,7},{8,9},{9,10},{10,11},{12,13},{... | collective-permute-start | bytes 516104 | tf_op jit(solution)/shard_map/ppermute | solution.py:519
  11.5 5.3 %collective-permute-start.2 = (bf16[14,3,16,128]{3,2,1,0:T(8,128)(2,1)S(1)}, bf16[14,3,16,128]{3,2,1,0:T(8,128)(2,1)S(1)}, u32[]{:S(2)}, u32[]{:S(2)}) collective-permute-start(bf16[14,3,16,128]{3,2,1,0:T(8,128)(2,1)S(1)} %get-tuple-element.22), channel_id=1, source_target_pairs={{1,0},{2,1},{3,2},{5,4},{6,5},{7,6},{9,8},{10,9},{11,10},{13,12},{... | collective-permute-start | bytes 516104 | tf_op jit(solution)/shard_map/ppermute | solution.py:522
  12.8 4.0 %copy-start.7 = (bf16[14,3,16,128]{3,2,1,0:T(8,128)(2,1)}, bf16[14,3,16,128]{3,2,1,0:T(8,128)(2,1)S(1)}, u32[]{:S(2)}) copy-start(bf16[14,3,16,128]{3,2,1,0:T(8,128)(2,1)S(1)} %collective-permute-done.1.left) | copy-start | bytes 516100
  35.2 12.8 %all-to-all-start = ((bf16[8,136,128]{2,1,0:T(8,128)(2,1)}), bf16[8,136,128]{2,1,0:T(8,128)(2,1)S(1)}, u32[]{:S(2)}, u32[]{:S(2)}) async-start(bf16[8,136,128]{2,1,0:T(8,128)(2,1)} %get-tuple-element.12), calls=%async_computation | async-start | bytes 557056 | tf_op jit(solution)/shard_map/all_to_all | solution.py:587
  48.0 0.7 copy-start.2
  59.8 6.0 %collective-permute-start.3 = (bf16[8,8,144]{2,1,0:T(8,128)(2,1)}, bf16[8,8,144]{2,1,0:T(8,128)(2,1)S(1)}, u32[]{:S(2)}, u32[]{:S(2)}) collective-permute-start(bf16[8,8,144]{2,1,0:T(8,128)(2,1)} %shard_map.97.refs_0_), channel_id=1, source_target_pairs={{0,8},{8,16},{16,24},{24,0},{1,9},{9,17},{17,25},{25,1},{2,10},{10... | collective-permute-start | bytes 55304 | tf_op jit(solution)/shard_map/ppermute | solution.py:622
  61.4 5.4 %collective-permute-start.4 = (bf16[8,8,144]{2,1,0:T(8,128)(2,1)}, bf16[8,8,144]{2,1,0:T(8,128)(2,1)S(1)}, u32[]{:S(2)}, u32[]{:S(2)}) collective-permute-start(bf16[8,8,144]{2,1,0:T(8,128)(2,1)} %shard_map.97.refs_0_), channel_id=1, source_target_pairs={{0,16},{8,24},{16,0},{24,8},{1,17},{9,25},{17,1},{25,9},{2,18},{10... | collective-permute-start | bytes 55304 | tf_op jit(solution)/shard_map/ppermute | solution.py:622
  64.0 4.1 %collective-permute-start.5 = (bf16[8,8,144]{2,1,0:T(8,128)(2,1)}, bf16[8,8,144]{2,1,0:T(8,128)(2,1)S(1)}, u32[]{:S(2)}, u32[]{:S(2)}) collective-permute-start(bf16[8,8,144]{2,1,0:T(8,128)(2,1)} %shard_map.97.refs_0_), channel_id=1, source_target_pairs={{0,24},{8,0},{16,8},{24,16},{1,25},{9,1},{17,9},{25,17},{2,26},{10... | collective-permute-start | bytes 55304 | tf_op jit(solution)/shard_map/ppermute | solution.py:622
  65.8 2.3 %copy-start.9 = (bf16[8,8,144]{2,1,0:T(8,128)(2,1)}, bf16[8,8,144]{2,1,0:T(8,128)(2,1)S(1)}, u32[]{:S(2)}) copy-start(bf16[8,8,144]{2,1,0:T(8,128)(2,1)S(1)} %collective-permute-done.3.refs_1_) | copy-start | bytes 55300
  66.8 1.3 %copy-start.10 = (bf16[8,8,144]{2,1,0:T(8,128)(2,1)}, bf16[8,8,144]{2,1,0:T(8,128)(2,1)S(1)}, u32[]{:S(2)}) copy-start(bf16[8,8,144]{2,1,0:T(8,128)(2,1)S(1)} %collective-permute-done.4.refs_2_) | copy-start | bytes 55300
  82.5 4.1 %collective-permute-start.10 = (bf16[2,108,128]{2,1,0:T(8,128)(2,1)S(1)}, bf16[2,108,128]{2,1,0:T(8,128)(2,1)S(1)}, u32[]{:S(2)}, u32[]{:S(2)}) collective-permute-start(bf16[2,108,128]{2,1,0:T(8,128)(2,1)S(1)} %get-tuple-element.27), channel_id=1, source_target_pairs={{0,5},{1,6},{2,7},{3,0},{4,1},{5,2},{6,3},{7,4},{8,13},{9,14},{10,... | collective-permute-start | bytes 165896 | tf_op jit(solution)/shard_map/ppermute | solution.py:650
  82.6 5.9 %collective-permute-start.11 = (bf16[2,108,128]{2,1,0:T(8,128)(2,1)S(1)}, bf16[2,108,128]{2,1,0:T(8,128)(2,1)S(1)}, u32[]{:S(2)}, u32[]{:S(2)}) collective-permute-start(bf16[2,108,128]{2,1,0:T(8,128)(2,1)S(1)} %get-tuple-element.26), channel_id=1, source_target_pairs={{0,6},{1,7},{2,0},{3,1},{4,2},{5,3},{6,4},{7,5},{8,14},{9,15},{10,... | collective-permute-start | bytes 165896 | tf_op jit(solution)/shard_map/ppermute | solution.py:650
  83.9 5.7 %collective-permute-start.12 = (bf16[2,108,128]{2,1,0:T(8,128)(2,1)S(1)}, bf16[2,108,128]{2,1,0:T(8,128)(2,1)S(1)}, u32[]{:S(2)}, u32[]{:S(2)}) collective-permute-start(bf16[2,108,128]{2,1,0:T(8,128)(2,1)S(1)} %get-tuple-element.25), channel_id=1, source_target_pairs={{0,7},{1,0},{2,1},{3,2},{4,3},{5,4},{6,5},{7,6},{8,15},{9,8},{10,9... | collective-permute-start | bytes 165896 | tf_op jit(solution)/shard_map/ppermute | solution.py:650
  86.2 4.5 %collective-permute-start.6 = (bf16[2,108,128]{2,1,0:T(8,128)(2,1)S(1)}, bf16[2,108,128]{2,1,0:T(8,128)(2,1)S(1)}, u32[]{:S(2)}, u32[]{:S(2)}) collective-permute-start(bf16[2,108,128]{2,1,0:T(8,128)(2,1)S(1)} %get-tuple-element.24), channel_id=1, source_target_pairs={{0,1},{1,2},{2,3},{3,4},{4,5},{5,6},{6,7},{7,0},{8,9},{9,10},{10,1... | collective-permute-start | bytes 165896 | tf_op jit(solution)/shard_map/ppermute | solution.py:650
  86.2 5.7 %collective-permute-start.7 = (bf16[2,108,128]{2,1,0:T(8,128)(2,1)S(1)}, bf16[2,108,128]{2,1,0:T(8,128)(2,1)S(1)}, u32[]{:S(2)}, u32[]{:S(2)}) collective-permute-start(bf16[2,108,128]{2,1,0:T(8,128)(2,1)S(1)} %get-tuple-element.30), channel_id=1, source_target_pairs={{0,2},{1,3},{2,4},{3,5},{4,6},{5,7},{6,0},{7,1},{8,10},{9,11},{10,... | collective-permute-start | bytes 165896 | tf_op jit(solution)/shard_map/ppermute | solution.py:650
  86.7 5.2 %collective-permute-start.8 = (bf16[2,108,128]{2,1,0:T(8,128)(2,1)S(1)}, bf16[2,108,128]{2,1,0:T(8,128)(2,1)S(1)}, u32[]{:S(2)}, u32[]{:S(2)}) collective-permute-start(bf16[2,108,128]{2,1,0:T(8,128)(2,1)S(1)} %get-tuple-element.29), channel_id=1, source_target_pairs={{0,3},{1,4},{2,5},{3,6},{4,7},{5,0},{6,1},{7,2},{8,11},{9,12},{10,... | collective-permute-start | bytes 165896 | tf_op jit(solution)/shard_map/ppermute | solution.py:650
  88.5 4.2 %collective-permute-start.9 = (bf16[2,108,128]{2,1,0:T(8,128)(2,1)S(1)}, bf16[2,108,128]{2,1,0:T(8,128)(2,1)S(1)}, u32[]{:S(2)}, u32[]{:S(2)}) collective-permute-start(bf16[2,108,128]{2,1,0:T(8,128)(2,1)S(1)} %get-tuple-element.28), channel_id=1, source_target_pairs={{0,4},{1,5},{2,6},{3,7},{4,0},{5,1},{6,2},{7,3},{8,12},{9,13},{10,... | collective-permute-start | bytes 165896 | tf_op jit(solution)/shard_map/ppermute | solution.py:650
  (2 other events, 1.3 us)

commit v2 on v1

--- a/solution.py
+++ b/solution.py
@@ -10,7 +10,6 @@
 gelu_scale = 0.7978845608028654
 gelu_cubic = 0.044715
 plane = ("row", "col")
-vmem_bytes = 62 * 2**20
 
 
 def repeat(count, body, unroll=1):
@@ -51,64 +50,40 @@
     return (at % slots < frames) & (col >= 0) & (col < width)
 
 
-def conv_frames(source, row, cols, weight):
-    slots, channels = source.shape[-2:]
-    slabs = [
-        source[row + dr, pl.ds(dc, cols)].reshape(cols * slots, channels)
-        for dr in range(3)
-        for dc in range(3)
-    ]
-    sums = matmul(jnp.concatenate(slabs, axis=1), weight)
-    count = cols * slots
-    return (
-        pltpu.roll(sums[:, :channels], 1, 0)
-        + sums[:, channels : 2 * channels]
-        + pltpu.roll(sums[:, 2 * channels :], count - 1, 0)
-    )
-
-
 def frame_weight(ref):
     third = ref.shape[0] // 3
     return jnp.concatenate([ref[pl.ds(third * k, third)] for k in range(3)], axis=1)
 
 
-def weight_kernel(second, third, volume, weight_2, weight_3, back_2, back_3, back_volume):
-    v1, v2, channels = second.shape[1], third.shape[1], volume.shape[1]
-    zero_2 = jnp.zeros((v1, v1), jnp.bfloat16)
-    zero_3 = jnp.zeros((v1, v2), jnp.bfloat16)
-    for tap in range(9):
-        taken = second[tap * v1 : (tap + 1) * v1]
-        weight_2[tap * 2 * v1 : (tap * 2 + 1) * v1] = jnp.concatenate([taken, zero_2], axis=1)
-        weight_2[(tap * 2 + 1) * v1 : (tap * 2 + 2) * v1] = jnp.concatenate(
-            [zero_2, taken], axis=1
+def conv_pairs(source, rows, cols, weight, use):
+    slots, channels = source.shape[-2:]
+    count = cols * slots
+
+    def step(q):
+        slabs = [
+            source[pl.ds(2 * q + dr, 2), pl.ds(dc, cols)].reshape(2 * count, channels)
+            for dr in range(3)
+            for dc in range(3)
+        ]
+        sums = matmul(jnp.concatenate(slabs, axis=1), weight[...])
+        total = (
+            pltpu.roll(sums[:, :channels], 1, 0)
+            + sums[:, channels : 2 * channels]
+            + pltpu.roll(sums[:, 2 * channels :], 2 * count - 1, 0)
         )
-        turned = jnp.concatenate([taken, zero_2], axis=0).astype(jnp.float32)
-        at = (8 - tap) * 2 * v1
-        turned = jnp.concatenate([turned, jnp.zeros_like(turned)], axis=1).T
-        back_2[at : at + 2 * v1] = turned.astype(jnp.bfloat16)
-        taken = third[tap * v1 : (tap + 1) * v1]
-        weight_3[tap * 2 * v1 : (tap * 2 + 1) * v1] = jnp.concatenate([taken, zero_3], axis=1)
-        weight_3[(tap * 2 + 1) * v1 : (tap * 2 + 2) * v1] = jnp.concatenate(
-            [zero_3, taken], axis=1
-        )
-        turned = jnp.concatenate([taken, zero_3], axis=0).astype(jnp.float32).T
-        back_3[(8 - tap) * v2 : (9 - tap) * v2] = turned.astype(jnp.bfloat16)
-    for dt in range(3):
-        for tap in range(9):
-            at = (dt * 9 + tap) * channels
-            turned = volume[at : at + channels].astype(jnp.float32).T.astype(jnp.bfloat16)
-            back_volume[
-                (8 - tap) * channels : (9 - tap) * channels,
-                (2 - dt) * channels : (3 - dt) * channels,
-            ] = turned
+        for k in range(2):
+            use(2 * q + k, total[k * count : (k + 1) * count])
+
+    repeat(rows // 2, step, rows // 2)
 
 
 def forward_kernel(
-    frames, parts, own, near, left, right, first, second, project, target,
-    cells_out, hidden_out, slope_first, slope_second, payload,
-    cells, hidden, spread_weight, picked, spaced, colour,
+    frames, parts, pack, own, near, left, right, first, second, rgb, target,
+    cells_out, hidden_out, first_out, second_out, payload,
+    cells, hidden, slope_first, slope_second, spread_weight, picked, spaced, colour, project, sems,
 ):
     rows, cols, slots, channels = own.shape
+    f32, bf16 = jnp.float32, jnp.bfloat16
     groups, group = lax.axis_size("grp"), lax.axis_index("grp")
     height, width = rows * lax.axis_size("row"), cols * lax.axis_size("col")
     top, left_col = lax.axis_index("row") * rows, lax.axis_index("col") * cols
@@ -117,17 +92,26 @@
     cells[3 + rows :, 3 : 3 + cols] = near[1]
     cells[:, 0:3] = left[...]
     cells[:, 3 + cols :] = right[...]
-    cells_out[...] = cells[2 : 4 + rows, 2 : 4 + cols]
+    copies = [
+        pltpu.make_async_copy(
+            cells.at[pl.ds(2, rows + 2), pl.ds(2, cols + 2)], cells_out, sems.at[0]
+        ),
+        pltpu.make_async_copy(
+            hidden.at[pl.ds(1, rows + 2), pl.ds(1, cols + 2)], hidden_out, sems.at[1]
+        ),
+        pltpu.make_async_copy(slope_first, first_out, sems.at[2]),
+        pltpu.make_async_copy(slope_second, second_out, sems.at[3]),
+    ]
+    copies[0].start()
     spread_weight[...] = frame_weight(first)
 
-    def first_layer(r):
-        pre = conv_frames(cells, r, cols + 4, spread_weight[...])
+    def first_layer(r, pre):
         row = top - 2 + r
         keep = col_mask(left_col - 2, cols + 4, width, slots, frames) & (
             (row >= 0) & (row < height)
         )
         gate = 0.5 + 0.5 * jnp.tanh(0.5 * pre)
-        out = jnp.where(keep, pre * gate, 0.0).astype(jnp.bfloat16)
+        out = jnp.where(keep, pre * gate, 0.0).astype(bf16)
         hidden[r] = out.reshape(cols + 4, slots, channels)
         slope = jnp.where(keep, gate * (1.0 + pre * (1.0 - gate)), 0.0)
 
@@ -135,39 +119,57 @@
         def _():
             slope_first[r - 2] = slope[2 * slots : (2 + cols) * slots]
 
-    repeat(rows + 4, first_layer, 2)
-    hidden_out[...] = hidden[1 : 3 + rows, 1 : 3 + cols]
+    conv_pairs(cells, rows + 4, cols + 4, spread_weight, first_layer)
+    copies[1].start()
+    copies[2].start()
     spread_weight[...] = frame_weight(second)
     own_slots = slots // groups
-    spaced[...] = jnp.zeros(spaced.shape, jnp.float32)
-
-    def second_layer(r):
-        pre = conv_frames(hidden, r, cols + 2, spread_weight[...])
+    spaced[...] = jnp.zeros(spaced.shape, f32)
+    project[...] = jnp.zeros(project.shape, f32)
+    project[0:3] = rgb[...].astype(f32)
+
+    def second_layer(r, pre):
         row = top - 1 + r
         keep = col_mask(left_col - 1, cols + 2, width, slots, frames) & (
             (row >= 0) & (row < height)
         )
         gate = 0.5 + 0.5 * jnp.tanh(0.5 * pre)
         slope_second[r] = jnp.where(keep, gate * (1.0 + pre * (1.0 - gate)), 0.0)
-        picked[...] = jnp.where(keep, pre * gate, 0.0)[slots : (1 + cols) * slots]
-        mine = picked[pl.ds(group, cols * own_slots, stride=groups)]
+        picked[r] = jnp.where(keep, pre * gate, 0.0)[slots : (1 + cols) * slots]
+        mine = picked.at[r][pl.ds(group, cols * own_slots, stride=groups)]
         if parts > 1:
             part = lax.axis_index("row")
-            spaced[pl.ds(part, cols * own_slots, stride=parts)] = mine
-            mine = spaced[...]
+            spaced.at[r][pl.ds(part, cols * own_slots, stride=parts)] = mine
+            mine = spaced[r]
         line = lax.dot_general(
-            project[...], mine.astype(jnp.bfloat16), (((1,), (1,)), ((), ())),
-            preferred_element_type=jnp.float32,
+            project[...].astype(bf16), mine.astype(bf16), (((1,), (1,)), ((), ())),
+            preferred_element_type=f32,
         )
-        colour[jnp.clip(r - 1, -1, rows) + 1] = line
-
-    repeat(rows + 2, second_layer, 2)
-    lines = jnp.concatenate(
-        [colour[1 : 1 + rows].reshape(rows * 8, colour.shape[2]).astype(jnp.bfloat16), target[...]],
-        axis=0,
-    )
+        at = jnp.clip(r - 1, -1, rows) + 1
+        colour[pl.ds(pl.multiple_of(at * 8, 8), 8)] = line
+
+    conv_pairs(hidden, rows + 2, cols + 2, spread_weight, second_layer)
+    copies[3].start()
+    size, line = payload.shape[1:]
+    pieces = [colour[pl.ds(8 + k, rows, stride=8)] for k in range(3)]
+    goal = target[...].reshape(-1, rows, width).astype(f32)
+    if pack > 1:
+        short = rows // pack
+        goal = jnp.concatenate([goal[:, k * short : (k + 1) * short] for k in range(pack)], axis=2)
+    goal = goal.reshape(-1, pack * width)
+    if pack * width < line:
+        goal = jnp.concatenate(
+            [goal, jnp.zeros((goal.shape[0], line - pack * width), f32)], axis=1
+        )
+    pieces.append(goal)
+    filled = 3 * rows + goal.shape[0]
+    if filled < size:
+        pieces.append(jnp.zeros((size - filled, line), f32))
+    lines = jnp.concatenate(pieces, axis=0).astype(bf16)
     for k in range(payload.shape[0]):
         payload[k] = lines
+    for copy in copies:
+        copy.wait()
 
 
 def plane_slabs(wide, narrow, row, count, half):
@@ -207,12 +209,48 @@
     return jnp.clip(row - first, -1, number) + 1
 
 
+def unrolled(number):
+    return number if number <= 8 else 4 if number % 4 == 0 else 2
+
+
+def plane_weights(
+    first, second, third, weight_1, weight_2, weight_3, back_3, back_2, back_1
+):
+    f32, bf16 = jnp.float32, jnp.bfloat16
+    v1, v2 = second.shape[1], third.shape[1]
+    zero_2 = jnp.zeros((v1, v1), bf16)
+    zero_3 = jnp.zeros((v1, v2), bf16)
+    weight_1[...] = jnp.zeros(weight_1.shape, f32)
+    back_1[...] = jnp.zeros(back_1.shape, f32)
+    for tap in range(9):
+        taken = first[...].astype(f32)[tap * 3 : tap * 3 + 3]
+        weight_1[tap * 8 : tap * 8 + 3, 0:v1] = taken
+        weight_1[tap * 8 + 3 : tap * 8 + 6, v1 : 2 * v1] = taken
+        back_1[0:3, (8 - tap) * 2 * v1 : (8 - tap) * 2 * v1 + v1] = taken
+        taken = second[tap * v1 : (tap + 1) * v1]
+        weight_2[tap * 2 * v1 : (tap * 2 + 1) * v1] = jnp.concatenate([taken, zero_2], axis=1)
+        weight_2[(tap * 2 + 1) * v1 : (tap * 2 + 2) * v1] = jnp.concatenate(
+            [zero_2, taken], axis=1
+        )
+        turned = jnp.concatenate([taken, zero_2], axis=0).astype(f32)
+        turned = jnp.concatenate([turned, jnp.zeros_like(turned)], axis=1).T
+        back_2[(8 - tap) * 2 * v1 : (9 - tap) * 2 * v1] = turned.astype(bf16)
+        taken = third[tap * v1 : (tap + 1) * v1]
+        weight_3[tap * 2 * v1 : (tap * 2 + 1) * v1] = jnp.concatenate([taken, zero_3], axis=1)
+        weight_3[(tap * 2 + 1) * v1 : (tap * 2 + 2) * v1] = jnp.concatenate(
+            [zero_3, taken], axis=1
+        )
+        turned = jnp.concatenate([taken, zero_3], axis=0).astype(f32).T
+        back_3[(8 - tap) * v2 : (9 - tap) * v2] = turned.astype(bf16)
+
+
 def perceptual_kernel(
-    shape, received, weight_1, weight_2, weight_3, back_3, back_2, back_1, pixels,
+    shape, received, vgg_first, vgg_second, vgg_third, pixels,
+    weight_1, weight_2, weight_3, back_3, back_2, back_1, shown, grads,
     target, strips, lines, wide_1, narrow_1, wide_3, narrow_3, wide_g, narrow_g,
     plane_1, plane_2, spread, wide_b, narrow_b, wide_a, narrow_a,
 ):
-    rows, cols, blocks, block_frames, own, parts, own_slots, frames_own = shape
+    rows, cols, blocks, block_frames, own, parts, own_slots, frames_own, pack = shape
     f32, bf16 = jnp.float32, jnp.bfloat16
     half = parts * own_slots
     groups, group = lax.axis_size("grp"), lax.axis_index("grp")
@@ -227,18 +265,25 @@
     span = width * half
     v1 = weight_2.shape[1] // 2
     v2 = weight_3.shape[1] // 2
-    base = rows * 8
     body = pl.ds(3 * half, count)
+    plane_weights(
+        vgg_first, vgg_second, vgg_third, weight_1, weight_2, weight_3, back_3, back_2, back_1
+    )
 
     for device in range(received.shape[0]):
-        target[device] = received[device, base:].astype(f32)
+        arrived = received[device].astype(f32)
+        target[device] = arrived[3 * rows :]
+        shown[device] = jnp.zeros(shown.shape[1:], f32)
+        for k in range(3):
+            shown.at[device][pl.ds(k, rows, stride=8)] = arrived[k * rows : (k + 1) * rows]
     strips[...] = jnp.zeros(strips.shape, f32)
     for j in range(frames_own):
         frame = groups * j + group
         block, rest = frame // block_frames, frame % block_frames
         for part in range(parts):
             for k in range(3):
-                start = ((k * blocks + block) * own + rest % own) * rows
+                short = rows // pack
+                start = ((k * blocks + block) * own + rest % own) * short
 
                 def take(at, j=j, part=part, k=k, start=start, rest=rest):
                     row = view_top + part * number + at
@@ -249,9 +294,11 @@
 
                 if parts > 1:
                     device = part * col_parts + rest // own
-                    strips[j * parts + part, pl.ds(3 + k, rows, stride=8)] = target[
-                        device, pl.ds(pl.multiple_of(start, 8) if rows % 8 == 0 else start, rows)
-                    ]
+                    value = target[device, pl.ds(start, short)]
+                    for turn in range(pack):
+                        strips[j * parts + part, pl.ds(3 + k + turn * short * 8, short, stride=8)] = (
+                            pltpu.roll(value, (pack - turn) * width % value.shape[1], 1)
+                        )
                 else:
                     repeat(number, take)
     from_col = lax.broadcasted_iota(jnp.int32, (target.shape[2], lanes), 0) - view_left
@@ -276,7 +323,7 @@
             source = pl.ds(pl.multiple_of(row % rows * 8, 8), 8)
             line = line + jnp.concatenate(
                 [
-                    received[(row // rows) * col_parts + k, source].astype(f32)[:, : cols * half]
+                    shown[(row // rows) * col_parts + k, source][:, : cols * half]
                     for k in range(col_parts)
                 ],
                 axis=1,
@@ -287,7 +334,7 @@
         after = jnp.where(lane >= count - half, 0.0, pltpu.roll(line, lanes - half, 1))
         lines[at + 1] = jnp.concatenate([before, line, after], axis=0)
 
-    repeat(number, line_step, 2)
+    repeat(number, line_step, unrolled(number))
     wide_lane = lax.broadcasted_iota(jnp.int32, (24, lanes), 1)
     if parts > 1:
         part = wide_lane % parts
@@ -303,11 +350,11 @@
     def first_step(at):
         pieces = [lines[at], lines[at + 1], lines[at + 2], jnp.zeros((56, lanes), f32)]
         patches = jnp.concatenate(pieces, axis=0).T[:count].astype(bf16)
-        z = matmul(patches, weight_1[...])
+        z = matmul(patches, weight_1[...].astype(bf16))
         plane_1[at, body] = z
         store_wide(wide_1, narrow_1, at + 1, 0.5 * z * (1.0 + gelu_tanh(z)), half)
 
-    repeat(number, first_step, 4)
+    repeat(number, first_step, unrolled(number))
     fill_edges(parts, wide_1, narrow_1)
 
     def second_step(q):
@@ -321,7 +368,7 @@
         pooled = 0.25 * (pooled[:, 0] + pooled[:, 1])
         store_wide(wide_3, narrow_3, q + 1, pooled.reshape(count // 2, 2 * v1), half)
 
-    repeat(number // 2, second_step, 2)
+    repeat(number // 2, second_step, unrolled(number // 2))
     fill_edges(parts, wide_3, narrow_3)
 
     def third_step(q):
@@ -331,7 +378,7 @@
         delta = (64.0 / v2) * (value[:, :v2] - value[:, v2:]) * gelu_slope(z[:, :v2], t[:, :v2])
         store_wide(wide_g, narrow_g, q + 1, delta, half)
 
-    repeat(number // 2, third_step, 2)
+    repeat(number // 2, third_step, unrolled(number // 2))
     fill_edges(parts, wide_g, narrow_g)
 
     def pool_step(q):
@@ -339,7 +386,7 @@
         grad = grad.reshape(view_cols // 2, 1, half, 2 * v1)
         spread[q, body] = jnp.concatenate([grad, grad], axis=1).reshape(count, 2 * v1)
 
-    repeat(number // 2, pool_step, 2)
+    repeat(number // 2, pool_step, unrolled(number // 2))
 
     def near(reach):
         size = (cols + 2 * reach) * half
@@ -355,7 +402,7 @@
         delta = spread[at // 2, where] + (16.0 / v1) * (value - pltpu.roll(value, v1, 1))
         store_slab(wide_b, narrow_b, at + 1, jnp.where(keep, delta * gelu_slope(z, t), 0.0), half)
 
-    repeat(number, second_delta, 2)
+    repeat(number, second_delta, unrolled(number))
     fill_edges(parts, wide_b, narrow_b)
 
     def first_delta(at):
@@ -365,22 +412,26 @@
         delta = jnp.where(keep, grad * gelu_slope(z, gelu_tanh(z)), 0.0)
         store_slab(wide_a, narrow_a, at + 1, delta, half)
 
-    repeat(number, first_delta, 2)
+    repeat(number, first_delta, unrolled(number))
     fill_edges(parts, wide_a, narrow_a)
 
     def pixel_step(at):
         size = (cols + 2) * half
         grad = lax.dot_general(
-            back_1[...], plane_slabs(wide_a, narrow_a, at, size, half), (((1,), (1,)), ((), ())),
+            back_1[...].astype(bf16), plane_slabs(wide_a, narrow_a, at, size, half), (((1,), (1,)), ((), ())),
             preferred_element_type=f32,
         )
         line = lines[at + 1, pl.ds(8, 8)]
         line = line - pltpu.roll(line, 5, 0)
         shift = lax.rem((view_left - left + 1) * half + 2 * lanes, lanes)
         line = pltpu.roll(line, shift, 1)
-        pixels[at] = (grad + (1.0 / 6.0) * line[:, :size]).astype(bf16)
-
-    repeat(number, pixel_step, 2)
+        grad = grad + (1.0 / 6.0) * line[:, :size]
+        for k in range(3):
+            grads[pl.ds(k * number + at, 1)] = grad[k : k + 1]
+
+    repeat(number, pixel_step, unrolled(number))
+    for k in range(3):
+        pixels[k] = grads[k * number : (k + 1) * number].astype(bf16)
 
 
 def gradient_taps(source, delta, shifted, sums, first_tap):
@@ -395,7 +446,7 @@
             moved = block if dt == 1 else pltpu.roll(block, (dt - 1) % count, 0)
             shifted[dt, r] = moved.T.astype(jnp.bfloat16)
 
-    repeat(rows, turn, 2)
+    repeat(rows, turn, rows)
 
     def tap_step(step):
         tap = jnp.minimum(first_tap + step, 26)
@@ -406,15 +457,25 @@
             total = total + matmul(shifted[dt, r], slab)
         sums[pl.ds(pl.multiple_of(step * channels, channels), channels)] = total.T
 
-    repeat(sums.shape[0] // channels, tap_step, 4)
+    repeat(sums.shape[0] // channels, tap_step, 8)
 
 
 def backward_kernel(*refs, parts, out_rows, groups):
     pixels = refs[:groups]
     (
-        slope_first, slope_second, cells, hidden, paint, back_second, terms,
-        painted, hidden_grad, delta_second, delta_own, shifted, sums,
+        rgb, conv_second, first_in, second_in, cells_in, hidden_in, terms,
+        slope_first, slope_second, cells, hidden, weight, back_second, paint, shown,
+        painted, hidden_grad, delta_second, delta_own, shifted, sums, sems,
     ) = refs[groups:]
+    copies = [
+        pltpu.make_async_copy(second_in, slope_second, sems.at[0]),
+        pltpu.make_async_copy(hidden_in, hidden, sems.at[1]),
+        pltpu.make_async_copy(conv_second, weight, sems.at[2]),
+        pltpu.make_async_copy(first_in, slope_first, sems.at[3]),
+        pltpu.make_async_copy(cells_in, cells, sems.at[4]),
+    ]
+    for copy in copies:
+        copy.start()
     slots, channels = cells.shape[-2:]
     rows, cols = cells.shape[0] - 2, cells.shape[1] - 2
     height = rows * lax.axis_size("row")
@@ -424,13 +485,23 @@
     group = lax.axis_index("grp")
     top, _, view_top, _ = corner(rows, cols)
     kept = (cols + 2) * own_slots
+    paint[...] = jnp.zeros(paint.shape, jnp.float32)
+    paint[0:3] = rgb[...].astype(jnp.float32)
+    shown[...] = jnp.zeros(shown.shape, jnp.float32)
+    for step in range(groups):
+        for k in range(3):
+            value = pixels[step][k].astype(jnp.float32)
+            for at in range(number):
+                shown[step, at * 8 + k : at * 8 + k + 1] = value[at : at + 1]
 
     def paint_step(at):
         for step in range(groups):
             source = lax.rem(group - step + groups, groups)
-            slot = painted.at[step]
+            slot = painted.at[at, step]
             slot[...] = lax.dot_general(
-                pixels[step][at], paint[...], (((0,), (0,)), ((), ())),
+                shown[step, pl.ds(pl.multiple_of(at * 8, 8), 8)].astype(jnp.bfloat16),
+                paint[...].astype(jnp.bfloat16),
+                (((0,), (0,)), ((), ())),
                 preferred_element_type=jnp.float32,
             )
             for part in range(parts):
@@ -438,7 +509,8 @@
                 value = slot[pl.ds(part, kept, stride=parts)] if parts > 1 else slot[...]
                 hidden_grad[row, pl.ds(source, kept, stride=groups)] = value
 
-    repeat(number, paint_step, 2)
+    repeat(number, paint_step, unrolled(number))
+    copies[0].wait()
 
     def delta_step(a):
         row = top - 1 + a
@@ -446,7 +518,7 @@
         delta = jnp.where(inside, hidden_grad[a + 1] * slope_second[a], 0.0).astype(jnp.bfloat16)
         delta_second[a] = delta.reshape(cols + 2, slots, channels)
 
-    repeat(rows + 2, delta_step, 2)
+    repeat(rows + 2, delta_step, 5)
 
     first_row = lax.axis_index("grp") * out_rows
     first_tap = first_row // channels
@@ -466,39 +538,48 @@
     def own_step(r):
         delta_own[r] = delta_second[r + 1, 1 : 1 + cols].reshape(cols * slots, channels)
 
-    repeat(rows, own_step, 2)
+    repeat(rows, own_step, rows)
+    copies[1].wait()
     gradient_taps(hidden, delta_own, shifted, sums, first_tap)
     put(1)
 
-    def back_step(r):
-        back = conv_frames(delta_second, r, cols, back_second[...])
+    copies[2].wait()
+    copies[3].wait()
+    copies[4].wait()
+    for dt in range(3):
+        for tap in range(9):
+            at = (dt * 9 + tap) * channels
+            turned = weight[at : at + channels].astype(jnp.float32).T.astype(jnp.bfloat16)
+            back_second[
+                (8 - tap) * channels : (9 - tap) * channels,
+                (2 - dt) * channels : (3 - dt) * channels,
+            ] = turned
+
+    def back_row(r, back):
         delta_own[r] = (back * slope_first[r]).astype(jnp.bfloat16)
 
-    repeat(rows, back_step, 4)
+    conv_pairs(delta_second, rows, cols, back_second, back_row)
     gradient_taps(cells, delta_own, shifted, sums, first_tap)
     put(0)
 
 
-def call(kernel, outs, scratch, flops=0):
+def call(kernel, outs, scratch, sems, limit, hbm_in=(), hbm_out=(), operands=0, flops=0):
+    def spec(at, chosen):
+        return pl.BlockSpec(memory_space=pltpu.HBM if at in chosen else pltpu.VMEM)
+
+    scratch = [pltpu.VMEM(*shape) for shape in scratch]
+    if sems:
+        scratch.append(pltpu.SemaphoreType.DMA((sems,)))
+    several = isinstance(outs, tuple)
     return pl.pallas_call(
         kernel,
         out_shape=outs,
-        scratch_shapes=[pltpu.VMEM(*shape) for shape in scratch],
-        compiler_params=pltpu.CompilerParams(vmem_limit_bytes=vmem_bytes),
+        in_specs=[spec(k, hbm_in) for k in range(operands)],
+        out_specs=tuple(spec(k, hbm_out) for k in range(len(outs))) if several else spec(0, hbm_out),
+        scratch_shapes=scratch,
+        compiler_params=pltpu.CompilerParams(vmem_limit_bytes=limit * 2**20),
         cost_estimate=pl.CostEstimate(flops=flops, bytes_accessed=2**20, transcendentals=0),
     )
-
-
-def plane_first_weights(vgg_first):
-    taps = vgg_first.reshape(9, 3, -1)
-    v1 = taps.shape[2]
-    first = jnp.concatenate(
-        [jnp.pad(taps, ((0, 0), (0, 0), (0, v1))), jnp.pad(taps, ((0, 0), (0, 0), (v1, 0)))], axis=1
-    )
-    first = jnp.pad(first, ((0, 0), (0, 2), (0, 0))).reshape(72, 2 * v1)
-    back = jnp.transpose(taps[::-1], (1, 0, 2))
-    back = jnp.pad(back, ((0, 5), (0, 0), (0, v1))).reshape(8, 9 * 2 * v1)
-    return jnp.pad(first, ((0, 56), (0, 0))), back
 
 
 def row_halo(own, width):
@@ -546,43 +627,37 @@
     before, after = col_halo(tall, 3)
 
     line = max(cols * half, -(-width // 128) * 128)
-    own_target = target.reshape(-1, width)
-    target_rows = own_target.shape[0]
-    own_target = jnp.pad(own_target, ((0, 0), (0, line - width)))
-    project = jnp.pad(rgb_weight, ((0, 5), (0, 0)))
-    weight_1, back_1 = plane_first_weights(vgg_first)
-    weight_2, weight_3, back_2, back_3, back_volume = call(
-        weight_kernel,
-        (
-            jax.ShapeDtypeStruct((18 * v1, 2 * v1), bf16),
-            jax.ShapeDtypeStruct((18 * v1, 2 * v2), bf16),
-            jax.ShapeDtypeStruct((18 * v1, 2 * v1), bf16),
-            jax.ShapeDtypeStruct((9 * v2, 2 * v1), bf16),
-            jax.ShapeDtypeStruct((9 * channels, 3 * channels), bf16),
-        ),
-        [],
-        2**30,
-    )(vgg_second, vgg_third, conv_second)
+    pack = line // width if parts > 1 and rows % (line // width) == 0 else 1
+    target_rows = 3 * blocks * target.shape[2] * rows // pack
+    size = -(-(3 * rows + target_rows) // 16) * 16
+    big = 16 if parts > 1 else 40
 
     cells, hidden, slope_first, slope_second, payload = call(
-        functools.partial(forward_kernel, frames, parts),
+        functools.partial(forward_kernel, frames, parts, pack),
         (
             jax.ShapeDtypeStruct((rows + 2, cols + 2, slots, channels), bf16),
             jax.ShapeDtypeStruct((rows + 2, cols + 2, slots, channels), bf16),
             jax.ShapeDtypeStruct((rows, cols * slots, channels), f32),
             jax.ShapeDtypeStruct((rows + 2, (cols + 2) * slots, channels), f32),
-            jax.ShapeDtypeStruct((devices, rows * 8 + target_rows, line), bf16),
+            jax.ShapeDtypeStruct((devices, size, line), bf16),
         ),
         [
             ((rows + 6, cols + 6, slots, channels), bf16),
             ((rows + 4, cols + 4, slots, channels), bf16),
+            ((rows, cols * slots, channels), f32),
+            ((rows + 2, (cols + 2) * slots, channels), f32),
             ((9 * channels, 3 * channels), bf16),
-            ((cols * slots, channels), f32),
-            ((cols * half, channels), f32),
-            ((rows + 2, 8, cols * half), f32),
+            ((rows + 2, cols * slots, channels), f32),
+            ((rows + 2, cols * half, channels), f32),
+            (((rows + 2) * 8, cols * half), f32),
+            ((8, channels), f32),
         ],
-        2**33,
-    )(own, near, before, after, conv_first, conv_second, project, own_target)
+        4,
+        big,
+        hbm_out=(0, 1, 2, 3),
+        operands=8,
+        flops=2**33,
+    )(own, near, before, after, conv_first, conv_second, rgb_weight, target)
 
     received = lax.all_to_all(payload, plane, split_axis=0, concat_axis=0, tiled=True)
 
@@ -592,11 +667,20 @@
             perceptual_kernel,
             (
                 rows, cols, blocks, block_frames, target.shape[2], parts, own_slots, frames_own,
+                pack,
             ),
         ),
-        jax.ShapeDtypeStruct((number, 8, (cols + 2) * half), bf16),
+        jax.ShapeDtypeStruct((3, number, (cols + 2) * half), bf16),
         [
-            ((devices, target_rows, line), f32),
+            ((128, 2 * v1), f32),
+            ((18 * v1, 2 * v1), bf16),
+            ((18 * v1, 2 * v2), bf16),
+            ((9 * v2, 2 * v1), bf16),
+            ((18 * v1, 2 * v1), bf16),
+            ((8, 18 * v1), f32),
+            ((devices, rows * 8, line), f32),
+            ((number * 3, (cols + 2) * half), f32),
+            ((devices, size - 3 * rows, line), f32),
             ((frames_own * parts, number * 8, line), f32),
             ((number + 2, 24, lanes), f32),
             ((number + 2, count + 2 * half, 2 * v1), bf16),
@@ -613,8 +697,11 @@
             ((number + 2, (cols + 4) * half, 2 * v1), bf16),
             ((number + 2, (cols + 2) * half, 2 * v1), bf16),
         ],
-        2**32,
-    )(received, weight_1, weight_2, weight_3, back_3, back_2, back_1)
+        0,
+        big,
+        operands=4,
+        flops=2**32,
+    )(received, vgg_first, vgg_second, vgg_third)
 
     gathered = [pixels]
     for step in range(1, groups):
@@ -633,15 +720,29 @@
         functools.partial(backward_kernel, parts=parts, out_rows=out_rows, groups=groups),
         jax.ShapeDtypeStruct(out_shape, bf16),
         [
-            ((groups, (cols + 2) * half, channels), f32),
+            ((rows, cols * slots, channels), f32),
+            ((rows + 2, (cols + 2) * slots, channels), f32),
+            ((rows + 2, cols + 2, slots, channels), bf16),
+            ((rows + 2, cols + 2, slots, channels), bf16),
+            (conv_second.shape, bf16),
+            ((9 * channels, 3 * channels), bf16),
+            ((8, channels), f32),
+            ((groups, number * 8, (cols + 2) * half), f32),
+            ((number, groups, (cols + 2) * half, channels), f32),
             ((rows + 4, (cols + 2) * slots, channels), f32),
             ((rows + 2, cols + 2, slots, channels), bf16),
             ((rows, cols * slots, channels), bf16),
             ((3, rows, channels, cols * slots), bf16),
             ((taps * channels, channels), f32),
         ],
-        2**32,
-    )(*gathered, slope_first, slope_second, cells, hidden, project, back_volume)
+        5,
+        big + 8,
+        hbm_in=tuple(range(groups + 1, groups + 6)),
+        operands=groups + 6,
+        flops=2**32,
+    )(
+        *gathered, rgb_weight, conv_second, slope_first, slope_second, cells, hidden,
+    )
 
     if even:
         pieces = [terms[0]]

time: 94.7 us -> 76 us (0.80)
  Pallas kernels: 44.6 us -> 26.7 us
  waiting for transfers between devices: 14.7 us -> 18.5 us
  local copies, waits for them, and re-layouts: 8.47 us -> 5.04 us
    pallas_call x2 -> x1, Pallas kernels: 20.6 us -> 11.7 us  [local(): call(functools.partial(forward_kernel, frames, parts, pack), (jax.ShapeDt...]
    pallas_call x1, Pallas kernels: 11.2 us -> 6.17 us  [local(): call(functools.partial(perceptual_kernel, (rows, cols, blocks, block_fram...]
    pallas_call x1, Pallas kernels: 12.8 us -> 8.83 us  [local(): call(functools.partial(backward_kernel, parts=parts, out_rows=out_rows, g...]
    ppermute x1, waiting for transfers between devices: 2.61 us -> 4.74 us  [row_halo(): came = lax.ppermute(edge, 'row', [(0, 1), (1, 0)])]
    pad x3 -> x0, local copies, waits for them, and re-layouts: 1.87 us -> none  [the longest x1 0.64 us: local(): project = jnp.pad(rgb_weight, ((0, 5), (0, 0)))]
    all_to_all x1, waiting for transfers between devices: 2.35 us -> 4.12 us  [local(): lax.all_to_all(payload, plane, split_axis=0, concat_axis=0, tiled=True)]
    squeeze x1, local copies, waits for them, and re-layouts: 1.01 us -> 0.03 us  [local(): pieces.append(lax.ppermute(terms[step], plane, ring))]
    unnamed x25 -> x21, local copies, waits for them, and re-layouts: 2.82 us -> 2.92 us
  transfers between devices with their start and end apart: 14 -> 14, of which waited for: 9 -> 8; matrix products, arithmetic and copies ran while one was open for 4% -> 1% of each run, Pallas kernels for 3% -> 0%
where the time goes in v2:
time: 76 us; the launch traced here: 75.7 us
  Pallas kernels  26.7 us (35%)
  starting transfers between devices  24.4 us (32%)
  waiting for transfers between devices  18.5 us (24%)
  local copies, waits for them, and re-layouts  5.04 us (7%)
  between operations  0.83 us (1%)
    pallas_call x1, Pallas kernels, local(): call(functools.partial(forward_kernel, frames, parts, pack), (jax.ShapeDt...  11.7 us
    pallas_call x1, Pallas kernels, local(): call(functools.partial(backward_kernel, parts=parts, out_rows=out_rows, g...  8.83 us
    ppermute x7, starting transfers between devices, local(): pieces.append(lax.ppermute(terms[step], plane, ring))  6.81 us
    all_to_all x1, starting transfers between devices, local(): lax.all_to_all(payload, plane, split_axis=0, concat_axis=0, tiled=True)  6.29 us
    pallas_call x1, Pallas kernels, local(): call(functools.partial(perceptual_kernel, (rows, cols, blocks, block_fram...  6.17 us
    ppermute x3, starting transfers between devices, local(): gathered.append(lax.ppermute(pixels, 'grp', ring))  5.55 us
    ppermute x1, waiting for transfers between devices, row_halo(): came = lax.ppermute(edge, 'row', [(0, 1), (1, 0)])  4.74 us
    all_to_all x1, waiting for transfers between devices, local(): lax.all_to_all(payload, plane, split_axis=0, concat_axis=0, tiled=True)  4.12 us
  transfers between devices with their start and end apart: 14, of which 8 were waited for; matrix products, arithmetic and copies ran while one was open for 1% of the time, Pallas kernels for 0%

profile of v2, /device:TPU:0, one launch (start us, length us, event | category | flops | bytes accessed | tf_op | source)
XLA Modules:
  0.0 75.7 jit_solution(10070574415734092070)
XLA Ops:
  0.6 1.3 %copy.15 = bf16[12,8,16,128]{3,0,2,1:T(8,128)(2,1)S(1)} copy(bf16[12,8,16,128]{3,2,1,0:T(8,128)(2,1)} %bitcast.33) | data formatting | bytes 786432 | tf_op jit(solution)/shard_map/reshape | solution.py:623
  2.0 3.0 %collective-permute-start = (bf16[3,16,16,128]{3,2,1,0:T(8,128)(2,1)S(1)}, bf16[3,16,16,128]{3,2,1,0:T(8,128)(2,1)S(1)}, u32[]{:S(2)}, u32[]{:S(2)}) collective-permute-start(bf16[3,16,16,128]{3,2,1,0:T(8,128)(2,1)S(1)} %constant_dynamic-slice_fusion), channel_id=1, source_target_pairs={{0,4},{4,0},{1,5},{5,1},{2,6},{6,2},{3,7},{7,3},{8,12},{12,8},{9,1... | collective-permute-start | bytes 589832 | tf_op jit(solution)/shard_map/ppermute | solution.py:590
  5.2 4.7 %collective-permute-done = bf16[3,16,16,128]{3,2,1,0:T(8,128)(2,1)S(1)} collective-permute-done((bf16[3,16,16,128]{3,2,1,0:T(8,128)(2,1)S(1)}, bf16[3,16,16,128]{3,2,1,0:T(8,128)(2,1)S(1)}, u32[]{:S(2)}, u32[]{:S(2)}) %collective-permute-start) | collective-permute-done | bytes 196640 | tf_op jit(solution)/shard_map/ppermute | solution.py:590
  10.1 1.3 %collective-permute-start.1 = (bf16[14,3,16,128]{3,2,1,0:T(8,128)(2,1)S(1)}, bf16[14,3,16,128]{3,2,1,0:T(8,128)(2,1)S(1)}, u32[]{:S(2)}, u32[]{:S(2)}) collective-permute-start(bf16[14,3,16,128]{3,2,1,0:T(8,128)(2,1)S(1)} %get-tuple-element.13), channel_id=1, source_target_pairs={{0,1},{1,2},{2,3},{4,5},{5,6},{6,7},{8,9},{9,10},{10,11},{12,13},{... | collective-permute-start | bytes 516104 | tf_op jit(solution)/shard_map/ppermute | solution.py:600
  11.4 1.4 %collective-permute-start.2 = (bf16[14,3,16,128]{3,2,1,0:T(8,128)(2,1)S(1)}, bf16[14,3,16,128]{3,2,1,0:T(8,128)(2,1)S(1)}, u32[]{:S(2)}, u32[]{:S(2)}) collective-permute-start(bf16[14,3,16,128]{3,2,1,0:T(8,128)(2,1)S(1)} %get-tuple-element.12), channel_id=1, source_target_pairs={{1,0},{2,1},{3,2},{5,4},{6,5},{7,6},{9,8},{10,9},{11,10},{13,12},{... | collective-permute-start | bytes 516104 | tf_op jit(solution)/shard_map/ppermute | solution.py:603
  12.9 4.0 %collective-permute-done.2.right = bf16[14,3,16,128]{3,2,1,0:T(8,128)(2,1)S(1)} collective-permute-done((bf16[14,3,16,128]{3,2,1,0:T(8,128)(2,1)S(1)}, bf16[14,3,16,128]{3,2,1,0:T(8,128)(2,1)S(1)}, u32[]{:S(2)}, u32[]{:S(2)}) %collective-permute-start.2) | collective-permute-done | bytes 172064 | tf_op jit(solution)/shard_map/ppermute | solution.py:603
  16.9 11.7 %shard_map.95 = (bf16[10,18,16,128]{3,2,1,0:T(8,128)(2,1)S(1)}, bf16[10,18,16,128]{3,2,1,0:T(8,128)(2,1)S(1)}, f32[8,256,128]{2,1,0:T(8,128)S(1)}, f32[10,288,128]{2,1,0:T(8,128)S(1)}, bf16[8,64,128]{2,1,0:T(8,128)(2,1)}) custom-call(bf16[8,16,16,128]{3,2,1,0:T(8,128)(2,1)S(1)} %pad.4.own, bf16[2,3,16,16,128]{4,3,2,1,0:T(8,128)(2,1)S(1)} %broadcast_select_fusion.near, ...), custom_call_target="tpu_custom_call" | custom-call | flops 8589934592 | bytes 1048576 | tf_op jit(solution)/shard_map/pallas_call | solution.py:635
  28.6 1.0 %copy-done.6 = f32[8,256,128]{2,1,0:T(8,128)} copy-done((f32[8,256,128]{2,1,0:T(8,128)}, f32[8,256,128]{2,1,0:T(8,128)S(1)}, u32[]{:S(2)}) %copy-start.6) | copy-done | bytes 1048600
  30.5 6.3 %all-to-all-start = ((bf16[8,64,128]{2,1,0:T(8,128)(2,1)}), bf16[8,64,128]{2,1,0:T(8,128)(2,1)S(1)}, u32[]{:S(2)}, u32[]{:S(2)}) async-start(bf16[8,64,128]{2,1,0:T(8,128)(2,1)} %get-tuple-element.7), calls=%async_computation | async-start | bytes 262144 | tf_op jit(solution)/shard_map/all_to_all | solution.py:662
  36.7 1.0 %copy.13.vgg_second = bf16[576,64]{1,0:T(8,128)(2,1)S(1)} copy(bf16[576,64]{0,1:T(8,128)(2,1)} %param.14) | data formatting | bytes 147456 | tf_op args[6]
  37.8 4.1 %all-to-all-done.received = bf16[8,64,128]{2,1,0:T(8,128)(2,1)S(1)} async-done(((bf16[8,64,128]{2,1,0:T(8,128)(2,1)}), bf16[8,64,128]{2,1,0:T(8,128)(2,1)S(1)}, u32[]{:S(2)}, u32[]{:S(2)}) %all-to-all-start) | async-done | bytes 131104 | tf_op jit(solution)/shard_map/all_to_all | solution.py:662
  41.9 6.2 %shard_map.96.refs_0_ = bf16[3,8,144]{2,1,0:T(8,128)(2,1)S(1)} custom-call(bf16[8,64,128]{2,1,0:T(8,128)(2,1)S(1)} %all-to-all-done.received, bf16[27,64]{1,0:T(8,128)(2,1)S(1)} %copy-done.4, bf16[576,64]{1,0:T(8,128)(2,1)S(1)} %copy.13.vgg_second, bf16[576,128]{1,0:T(8,128)(2,1)S(1)} %copy-done.2), custom_call_target="tpu_custom_call" | custom-call | flops 4294967296 | bytes 1048576 | tf_op jit(solution)/shard_map/pallas_call | solution.py:665
  48.1 1.6 %collective-permute-start.3 = (bf16[3,8,144]{2,1,0:T(8,128)(2,1)S(1)}, bf16[3,8,144]{2,1,0:T(8,128)(2,1)S(1)}, u32[]{:S(2)}, u32[]{:S(2)}) collective-permute-start(bf16[3,8,144]{2,1,0:T(8,128)(2,1)S(1)} %shard_map.96.refs_0_), channel_id=1, source_target_pairs={{0,8},{8,16},{16,24},{24,0},{1,9},{9,17},{17,25},{25,1},{2,10},{10... | collective-permute-start | bytes 20744 | tf_op jit(solution)/shard_map/ppermute | solution.py:709
  49.7 2.6 %collective-permute-start.4 = (bf16[3,8,144]{2,1,0:T(8,128)(2,1)S(1)}, bf16[3,8,144]{2,1,0:T(8,128)(2,1)S(1)}, u32[]{:S(2)}, u32[]{:S(2)}) collective-permute-start(bf16[3,8,144]{2,1,0:T(8,128)(2,1)S(1)} %shard_map.96.refs_0_), channel_id=1, source_target_pairs={{0,16},{8,24},{16,0},{24,8},{1,17},{9,25},{17,1},{25,9},{2,18},{10... | collective-permute-start | bytes 20744 | tf_op jit(solution)/shard_map/ppermute | solution.py:709
  52.3 1.3 %collective-permute-start.5 = (bf16[3,8,144]{2,1,0:T(8,128)(2,1)S(1)}, bf16[3,8,144]{2,1,0:T(8,128)(2,1)S(1)}, u32[]{:S(2)}, u32[]{:S(2)}) collective-permute-start(bf16[3,8,144]{2,1,0:T(8,128)(2,1)S(1)} %shard_map.96.refs_0_), channel_id=1, source_target_pairs={{0,24},{8,0},{16,8},{24,16},{1,25},{9,1},{17,9},{25,17},{2,26},{10... | collective-permute-start | bytes 20744 | tf_op jit(solution)/shard_map/ppermute | solution.py:709
  54.3 1.7 %collective-permute-done.5.refs_3_ = bf16[3,8,144]{2,1,0:T(8,128)(2,1)S(1)} collective-permute-done((bf16[3,8,144]{2,1,0:T(8,128)(2,1)S(1)}, bf16[3,8,144]{2,1,0:T(8,128)(2,1)S(1)}, u32[]{:S(2)}, u32[]{:S(2)}) %collective-permute-start.5) | collective-permute-done | bytes 6944 | tf_op jit(solution)/shard_map/ppermute | solution.py:709
  56.0 8.8 %shard_map.97 = bf16[8,2,108,128]{3,2,1,0:T(8,128)(2,1)S(1)} custom-call(bf16[3,8,144]{2,1,0:T(8,128)(2,1)S(1)} %shard_map.96.refs_0_, bf16[3,8,144]{2,1,0:T(8,128)(2,1)S(1)} %collective-permute-done.3.refs_1_, bf16[3,8,144]{2,1,0:T(8,128)(2,1)S(1)} %collective-permute-done.4.refs_2_, bf16[3,8,144]{2,1,0:T(8,128)(2,1)S(1)} %collective-permute-done.5.refs_3_, ...), custom_call_target="tpu_custom_call" | custom-call | flops 4294967296 | bytes 1048576 | tf_op jit(solution)/shard_map/pallas_call | solution.py:719
  64.9 1.1 %collective-permute-start.11 = (bf16[2,108,128]{2,1,0:T(8,128)(2,1)S(1)}, bf16[2,108,128]{2,1,0:T(8,128)(2,1)S(1)}, u32[]{:S(2)}, u32[]{:S(2)}) collective-permute-start(bf16[2,108,128]{2,1,0:T(8,128)(2,1)S(1)} %get-tuple-element.16), channel_id=1, source_target_pairs={{0,6},{1,7},{2,0},{3,1},{4,2},{5,3},{6,4},{7,5},{8,14},{9,15},{10,... | collective-permute-start | bytes 165896 | tf_op jit(solution)/shard_map/ppermute | solution.py:751
  66.0 2.2 %collective-permute-start.12 = (bf16[2,108,128]{2,1,0:T(8,128)(2,1)S(1)}, bf16[2,108,128]{2,1,0:T(8,128)(2,1)S(1)}, u32[]{:S(2)}, u32[]{:S(2)}) collective-permute-start(bf16[2,108,128]{2,1,0:T(8,128)(2,1)S(1)} %get-tuple-element.15), channel_id=1, source_target_pairs={{0,7},{1,0},{2,1},{3,2},{4,3},{5,4},{6,5},{7,6},{8,15},{9,8},{10,9... | collective-permute-start | bytes 165896 | tf_op jit(solution)/shard_map/ppermute | solution.py:751
  68.8 2.0 %collective-permute-start.8 = (bf16[2,108,128]{2,1,0:T(8,128)(2,1)S(1)}, bf16[2,108,128]{2,1,0:T(8,128)(2,1)S(1)}, u32[]{:S(2)}, u32[]{:S(2)}) collective-permute-start(bf16[2,108,128]{2,1,0:T(8,128)(2,1)S(1)} %get-tuple-element.19), channel_id=1, source_target_pairs={{0,3},{1,4},{2,5},{3,6},{4,7},{5,0},{6,1},{7,2},{8,11},{9,12},{10,... | collective-permute-start | bytes 165896 | tf_op jit(solution)/shard_map/ppermute | solution.py:751
  70.8 0.9 %collective-permute-start.9 = (bf16[2,108,128]{2,1,0:T(8,128)(2,1)S(1)}, bf16[2,108,128]{2,1,0:T(8,128)(2,1)S(1)}, u32[]{:S(2)}, u32[]{:S(2)}) collective-permute-start(bf16[2,108,128]{2,1,0:T(8,128)(2,1)S(1)} %get-tuple-element.18), channel_id=1, source_target_pairs={{0,4},{1,5},{2,6},{3,7},{4,0},{5,1},{6,2},{7,3},{8,12},{9,13},{10,... | collective-permute-start | bytes 165896 | tf_op jit(solution)/shard_map/ppermute | solution.py:751
  71.7 1.0 %collective-permute-done.6 = bf16[2,108,128]{2,1,0:T(8,128)(2,1)S(1)} collective-permute-done((bf16[2,108,128]{2,1,0:T(8,128)(2,1)S(1)}, bf16[2,108,128]{2,1,0:T(8,128)(2,1)S(1)}, u32[]{:S(2)}, u32[]{:S(2)}) %collective-permute-start.6) | collective-permute-done | bytes 55328 | tf_op jit(solution)/shard_map/ppermute | solution.py:751
  72.7 1.2 %collective-permute-done.7 = bf16[2,108,128]{2,1,0:T(8,128)(2,1)S(1)} collective-permute-done((bf16[2,108,128]{2,1,0:T(8,128)(2,1)S(1)}, bf16[2,108,128]{2,1,0:T(8,128)(2,1)S(1)}, u32[]{:S(2)}, u32[]{:S(2)}) %collective-permute-start.7) | collective-permute-done | bytes 55328 | tf_op jit(solution)/shard_map/ppermute | solution.py:751
  73.9 1.1 %collective-permute-done.9 = bf16[2,108,128]{2,1,0:T(8,128)(2,1)S(1)} collective-permute-done((bf16[2,108,128]{2,1,0:T(8,128)(2,1)S(1)}, bf16[2,108,128]{2,1,0:T(8,128)(2,1)S(1)}, u32[]{:S(2)}, u32[]{:S(2)}) %collective-permute-start.9) | collective-permute-done | bytes 55328 | tf_op jit(solution)/shard_map/ppermute | solution.py:751
  (38 shorter events, 3.3 us)
Async XLA Ops:
  2.0 7.9 %collective-permute-start = (bf16[3,16,16,128]{3,2,1,0:T(8,128)(2,1)S(1)}, bf16[3,16,16,128]{3,2,1,0:T(8,128)(2,1)S(1)}, u32[]{:S(2)}, u32[]{:S(2)}) collective-permute-start(bf16[3,16,16,128]{3,2,1,0:T(8,128)(2,1)S(1)} %constant_dynamic-slice_fusion), channel_id=1, source_target_pairs={{0,4},{4,0},{1,5},{5,1},{2,6},{6,2},{3,7},{7,3},{8,12},{12,8},{9,1... | collective-permute-start | bytes 589832 | tf_op jit(solution)/shard_map/ppermute | solution.py:590
  5.1 11.7 %copy-start = (bf16[3456,128]{1,0:T(8,128)(2,1)S(1)}, bf16[3456,128]{1,0:T(8,128)(2,1)}, u32[]{:S(2)}) copy-start(bf16[3456,128]{1,0:T(8,128)(2,1)} %first.1) | copy-start | bytes 2654212
  5.1 11.7 %copy-start.1 = (bf16[3456,128]{1,0:T(8,128)(2,1)S(1)}, bf16[3456,128]{1,0:T(8,128)(2,1)}, u32[]{:S(2)}) copy-start(bf16[3456,128]{1,0:T(8,128)(2,1)} %refs_5_.1) | copy-start | bytes 2654212
  5.1 11.7 %copy-start.3 = (bf16[3,3,1,8,64]{4,3,2,1,0:T(8,128)(2,1)S(1)}, bf16[3,3,1,8,64]{4,3,2,1,0:T(8,128)(2,1)}, u32[]{:S(2)}) copy-start(bf16[3,3,1,8,64]{4,3,2,1,0:T(8,128)(2,1)} %target.1) | copy-start | bytes 27652
  5.1 11.7 %copy-start.5 = (bf16[3,128]{1,0:T(4,128)(2,1)S(1)}, bf16[3,128]{1,0:T(4,128)(2,1)}, u32[]{:S(2)}) copy-start(bf16[3,128]{1,0:T(4,128)(2,1)} %refs_4_.1) | copy-start | bytes 2308
  10.1 2.8 %collective-permute-start.1 = (bf16[14,3,16,128]{3,2,1,0:T(8,128)(2,1)S(1)}, bf16[14,3,16,128]{3,2,1,0:T(8,128)(2,1)S(1)}, u32[]{:S(2)}, u32[]{:S(2)}) collective-permute-start(bf16[14,3,16,128]{3,2,1,0:T(8,128)(2,1)S(1)} %get-tuple-element.13), channel_id=1, source_target_pairs={{0,1},{1,2},{2,3},{4,5},{5,6},{6,7},{8,9},{9,10},{10,11},{12,13},{... | collective-permute-start | bytes 516104 | tf_op jit(solution)/shard_map/ppermute | solution.py:600
  11.4 30.5 %copy-start.2 = (bf16[576,128]{1,0:T(8,128)(2,1)S(1)}, bf16[576,128]{1,0:T(8,128)(2,1)}, u32[]{:S(2)}) copy-start(bf16[576,128]{1,0:T(8,128)(2,1)} %vgg_third.1) | copy-start | bytes 442372
  11.4 30.5 %copy-start.4 = (bf16[27,64]{1,0:T(8,128)(2,1)S(1)}, bf16[27,64]{1,0:T(8,128)(2,1)}, u32[]{:S(2)}) copy-start(bf16[27,64]{1,0:T(8,128)(2,1)} %vgg_first.1) | copy-start | bytes 10372
  11.4 5.4 %collective-permute-start.2 = (bf16[14,3,16,128]{3,2,1,0:T(8,128)(2,1)S(1)}, bf16[14,3,16,128]{3,2,1,0:T(8,128)(2,1)S(1)}, u32[]{:S(2)}, u32[]{:S(2)}) collective-permute-start(bf16[14,3,16,128]{3,2,1,0:T(8,128)(2,1)S(1)} %get-tuple-element.12), channel_id=1, source_target_pairs={{1,0},{2,1},{3,2},{5,4},{6,5},{7,6},{9,8},{10,9},{11,10},{13,12},{... | collective-permute-start | bytes 516104 | tf_op jit(solution)/shard_map/ppermute | solution.py:603
  28.6 1.0 %copy-start.6 = (f32[8,256,128]{2,1,0:T(8,128)}, f32[8,256,128]{2,1,0:T(8,128)S(1)}, u32[]{:S(2)}) copy-start(f32[8,256,128]{2,1,0:T(8,128)S(1)} %get-tuple-element.8.refs_6_) | copy-start | bytes 3145732
  29.6 0.9 %copy-start.8 = (bf16[10,18,16,128]{3,2,1,0:T(8,128)(2,1)}, bf16[10,18,16,128]{3,2,1,0:T(8,128)(2,1)S(1)}, u32[]{:S(2)}) copy-start(bf16[10,18,16,128]{3,2,1,0:T(8,128)(2,1)S(1)} %get-tuple-element.11.refs_9_) | copy-start | bytes 2211844
  30.5 11.4 %all-to-all-start = ((bf16[8,64,128]{2,1,0:T(8,128)(2,1)}), bf16[8,64,128]{2,1,0:T(8,128)(2,1)S(1)}, u32[]{:S(2)}, u32[]{:S(2)}) async-start(bf16[8,64,128]{2,1,0:T(8,128)(2,1)} %get-tuple-element.7), calls=%async_computation | async-start | bytes 262144 | tf_op jit(solution)/shard_map/all_to_all | solution.py:662
  41.9 14.1 %copy-start.7 = (f32[8,256,128]{2,1,0:T(8,128)S(1)}, f32[8,256,128]{2,1,0:T(8,128)}, u32[]{:S(2)}) copy-start(f32[8,256,128]{2,1,0:T(8,128)} %copy-done.6) | copy-start | bytes 3145732
  41.9 14.1 %copy-start.9 = (bf16[10,18,16,128]{3,2,1,0:T(8,128)(2,1)S(1)}, bf16[10,18,16,128]{3,2,1,0:T(8,128)(2,1)}, u32[]{:S(2)}) copy-start(bf16[10,18,16,128]{3,2,1,0:T(8,128)(2,1)} %copy-done.8) | copy-start | bytes 2211844
  48.1 5.6 %collective-permute-start.3 = (bf16[3,8,144]{2,1,0:T(8,128)(2,1)S(1)}, bf16[3,8,144]{2,1,0:T(8,128)(2,1)S(1)}, u32[]{:S(2)}, u32[]{:S(2)}) collective-permute-start(bf16[3,8,144]{2,1,0:T(8,128)(2,1)S(1)} %shard_map.96.refs_0_), channel_id=1, source_target_pairs={{0,8},{8,16},{16,24},{24,0},{1,9},{9,17},{17,25},{25,1},{2,10},{10... | collective-permute-start | bytes 20744 | tf_op jit(solution)/shard_map/ppermute | solution.py:709
  49.7 4.6 %collective-permute-start.4 = (bf16[3,8,144]{2,1,0:T(8,128)(2,1)S(1)}, bf16[3,8,144]{2,1,0:T(8,128)(2,1)S(1)}, u32[]{:S(2)}, u32[]{:S(2)}) collective-permute-start(bf16[3,8,144]{2,1,0:T(8,128)(2,1)S(1)} %shard_map.96.refs_0_), channel_id=1, source_target_pairs={{0,16},{8,24},{16,0},{24,8},{1,17},{9,25},{17,1},{25,9},{2,18},{10... | collective-permute-start | bytes 20744 | tf_op jit(solution)/shard_map/ppermute | solution.py:709
  52.3 3.7 %collective-permute-start.5 = (bf16[3,8,144]{2,1,0:T(8,128)(2,1)S(1)}, bf16[3,8,144]{2,1,0:T(8,128)(2,1)S(1)}, u32[]{:S(2)}, u32[]{:S(2)}) collective-permute-start(bf16[3,8,144]{2,1,0:T(8,128)(2,1)S(1)} %shard_map.96.refs_0_), channel_id=1, source_target_pairs={{0,24},{8,0},{16,8},{24,16},{1,25},{9,1},{17,9},{25,17},{2,26},{10... | collective-permute-start | bytes 20744 | tf_op jit(solution)/shard_map/ppermute | solution.py:709
  64.9 3.9 %collective-permute-start.10 = (bf16[2,108,128]{2,1,0:T(8,128)(2,1)S(1)}, bf16[2,108,128]{2,1,0:T(8,128)(2,1)S(1)}, u32[]{:S(2)}, u32[]{:S(2)}) collective-permute-start(bf16[2,108,128]{2,1,0:T(8,128)(2,1)S(1)} %get-tuple-element.17), channel_id=1, source_target_pairs={{0,5},{1,6},{2,7},{3,0},{4,1},{5,2},{6,3},{7,4},{8,13},{9,14},{10,... | collective-permute-start | bytes 165896 | tf_op jit(solution)/shard_map/ppermute | solution.py:751
  64.9 5.9 %collective-permute-start.11 = (bf16[2,108,128]{2,1,0:T(8,128)(2,1)S(1)}, bf16[2,108,128]{2,1,0:T(8,128)(2,1)S(1)}, u32[]{:S(2)}, u32[]{:S(2)}) collective-permute-start(bf16[2,108,128]{2,1,0:T(8,128)(2,1)S(1)} %get-tuple-element.16), channel_id=1, source_target_pairs={{0,6},{1,7},{2,0},{3,1},{4,2},{5,3},{6,4},{7,5},{8,14},{9,15},{10,... | collective-permute-start | bytes 165896 | tf_op jit(solution)/shard_map/ppermute | solution.py:751
  66.0 5.7 %collective-permute-start.12 = (bf16[2,108,128]{2,1,0:T(8,128)(2,1)S(1)}, bf16[2,108,128]{2,1,0:T(8,128)(2,1)S(1)}, u32[]{:S(2)}, u32[]{:S(2)}) collective-permute-start(bf16[2,108,128]{2,1,0:T(8,128)(2,1)S(1)} %get-tuple-element.15), channel_id=1, source_target_pairs={{0,7},{1,0},{2,1},{3,2},{4,3},{5,4},{6,5},{7,6},{8,15},{9,8},{10,9... | collective-permute-start | bytes 165896 | tf_op jit(solution)/shard_map/ppermute | solution.py:751
  68.2 4.5 %collective-permute-start.6 = (bf16[2,108,128]{2,1,0:T(8,128)(2,1)S(1)}, bf16[2,108,128]{2,1,0:T(8,128)(2,1)S(1)}, u32[]{:S(2)}, u32[]{:S(2)}) collective-permute-start(bf16[2,108,128]{2,1,0:T(8,128)(2,1)S(1)} %get-tuple-element.14), channel_id=1, source_target_pairs={{0,1},{1,2},{2,3},{3,4},{4,5},{5,6},{6,7},{7,0},{8,9},{9,10},{10,1... | collective-permute-start | bytes 165896 | tf_op jit(solution)/shard_map/ppermute | solution.py:751
  68.2 5.7 %collective-permute-start.7 = (bf16[2,108,128]{2,1,0:T(8,128)(2,1)S(1)}, bf16[2,108,128]{2,1,0:T(8,128)(2,1)S(1)}, u32[]{:S(2)}, u32[]{:S(2)}) collective-permute-start(bf16[2,108,128]{2,1,0:T(8,128)(2,1)S(1)} %get-tuple-element.20), channel_id=1, source_target_pairs={{0,2},{1,3},{2,4},{3,5},{4,6},{5,7},{6,0},{7,1},{8,10},{9,11},{10,... | collective-permute-start | bytes 165896 | tf_op jit(solution)/shard_map/ppermute | solution.py:751
  68.8 5.1 %collective-permute-start.8 = (bf16[2,108,128]{2,1,0:T(8,128)(2,1)S(1)}, bf16[2,108,128]{2,1,0:T(8,128)(2,1)S(1)}, u32[]{:S(2)}, u32[]{:S(2)}) collective-permute-start(bf16[2,108,128]{2,1,0:T(8,128)(2,1)S(1)} %get-tuple-element.19), channel_id=1, source_target_pairs={{0,3},{1,4},{2,5},{3,6},{4,7},{5,0},{6,1},{7,2},{8,11},{9,12},{10,... | collective-permute-start | bytes 165896 | tf_op jit(solution)/shard_map/ppermute | solution.py:751
  70.8 4.2 %collective-permute-start.9 = (bf16[2,108,128]{2,1,0:T(8,128)(2,1)S(1)}, bf16[2,108,128]{2,1,0:T(8,128)(2,1)S(1)}, u32[]{:S(2)}, u32[]{:S(2)}) collective-permute-start(bf16[2,108,128]{2,1,0:T(8,128)(2,1)S(1)} %get-tuple-element.18), channel_id=1, source_target_pairs={{0,4},{1,5},{2,6},{3,7},{4,0},{5,1},{6,2},{7,3},{8,12},{9,13},{10,... | collective-permute-start | bytes 165896 | tf_op jit(solution)/shard_map/ppermute | solution.py:751

commit v3 on v2

--- a/solution.py
+++ b/solution.py
@@ -77,21 +77,32 @@
     repeat(rows // 2, step, rows // 2)
 
 
-def forward_kernel(
-    frames, parts, pack, own, near, left, right, first, second, rgb, target,
-    cells_out, hidden_out, first_out, second_out, payload,
-    cells, hidden, slope_first, slope_second, spread_weight, picked, spaced, colour, project, sems,
-):
+def forward_kernel(frames, parts, pack, places, own, *refs):
+    near = refs[: len(places)]
+    (
+        first, second, rgb, target, cells_out, hidden_out, first_out, second_out, payload,
+        cells, hidden, slope_first, slope_second, spread_weight, picked, spaced, colour, project,
+        sems,
+    ) = refs[len(places) :]
     rows, cols, slots, channels = own.shape
     f32, bf16 = jnp.float32, jnp.bfloat16
     groups, group = lax.axis_size("grp"), lax.axis_index("grp")
     height, width = rows * lax.axis_size("row"), cols * lax.axis_size("col")
     top, left_col = lax.axis_index("row") * rows, lax.axis_index("col") * cols
     cells[3 : 3 + rows, 3 : 3 + cols] = own[...]
-    cells[0:3, 3 : 3 + cols] = near[0]
-    cells[3 + rows :, 3 : 3 + cols] = near[1]
-    cells[:, 0:3] = left[...]
-    cells[:, 3 + cols :] = right[...]
+    if lax.axis_size("row") == 2:
+        start = jnp.where(lax.axis_index("row") == 0, 0, 3 + rows)
+        cells[pl.ds(start, 3)] = jnp.zeros((3,) + cells.shape[1:], bf16)
+    if lax.axis_size("col") == 2:
+        start = jnp.where(lax.axis_index("col") == 0, 0, 3 + cols)
+        cells[:, pl.ds(start, 3)] = jnp.zeros((rows + 6, 3) + cells.shape[2:], bf16)
+    for (row_at, col_at), piece in zip(places, near):
+        row, col = 3, 3
+        if row_at is not None:
+            row = jnp.where(lax.axis_index("row") % 2 == row_at, 3 + rows, 0)
+        if col_at is not None:
+            col = jnp.where(lax.axis_index("col") % 2 == col_at, 3 + cols, 0)
+        cells[pl.ds(row, piece.shape[0]), pl.ds(col, piece.shape[1])] = piece[...]
     copies = [
         pltpu.make_async_copy(
             cells.at[pl.ds(2, rows + 2), pl.ds(2, cols + 2)], cells_out, sems.at[0]
@@ -150,7 +161,7 @@
 
     conv_pairs(hidden, rows + 2, cols + 2, spread_weight, second_layer)
     copies[3].start()
-    size, line = payload.shape[1:]
+    size, line = payload.shape
     pieces = [colour[pl.ds(8 + k, rows, stride=8)] for k in range(3)]
     goal = target[...].reshape(-1, rows, width).astype(f32)
     if pack > 1:
@@ -166,8 +177,7 @@
     if filled < size:
         pieces.append(jnp.zeros((size - filled, line), f32))
     lines = jnp.concatenate(pieces, axis=0).astype(bf16)
-    for k in range(payload.shape[0]):
-        payload[k] = lines
+    payload[...] = lines
     for copy in copies:
         copy.wait()
 
@@ -217,8 +227,7 @@
     first, second, third, weight_1, weight_2, weight_3, back_3, back_2, back_1
 ):
     f32, bf16 = jnp.float32, jnp.bfloat16
-    v1, v2 = second.shape[1], third.shape[1]
-    zero_2 = jnp.zeros((v1, v1), bf16)
+    v1, v2 = second.shape[0], third.shape[1]
     zero_3 = jnp.zeros((v1, v2), bf16)
     weight_1[...] = jnp.zeros(weight_1.shape, f32)
     back_1[...] = jnp.zeros(back_1.shape, f32)
@@ -227,14 +236,14 @@
         weight_1[tap * 8 : tap * 8 + 3, 0:v1] = taken
         weight_1[tap * 8 + 3 : tap * 8 + 6, v1 : 2 * v1] = taken
         back_1[0:3, (8 - tap) * 2 * v1 : (8 - tap) * 2 * v1 + v1] = taken
-        taken = second[tap * v1 : (tap + 1) * v1]
-        weight_2[tap * 2 * v1 : (tap * 2 + 1) * v1] = jnp.concatenate([taken, zero_2], axis=1)
-        weight_2[(tap * 2 + 1) * v1 : (tap * 2 + 2) * v1] = jnp.concatenate(
-            [zero_2, taken], axis=1
-        )
-        turned = jnp.concatenate([taken, zero_2], axis=0).astype(f32)
-        turned = jnp.concatenate([turned, jnp.zeros_like(turned)], axis=1).T
-        back_2[(8 - tap) * 2 * v1 : (9 - tap) * 2 * v1] = turned.astype(bf16)
+        taken = second[...].astype(f32)[:, tap * v1 : (tap + 1) * v1]
+        beside = jnp.concatenate([taken, jnp.zeros_like(taken)], axis=1)
+        under = jnp.concatenate([jnp.zeros_like(taken), taken], axis=1)
+        both = jnp.concatenate([beside, under], axis=0)
+        weight_2[tap * 2 * v1 : (tap + 1) * 2 * v1] = both.T.astype(bf16)
+        back_2[(8 - tap) * 2 * v1 : (9 - tap) * 2 * v1] = jnp.concatenate(
+            [beside, jnp.zeros_like(beside)], axis=0
+        ).astype(bf16)
         taken = third[tap * v1 : (tap + 1) * v1]
         weight_3[tap * 2 * v1 : (tap * 2 + 1) * v1] = jnp.concatenate([taken, zero_3], axis=1)
         weight_3[(tap * 2 + 1) * v1 : (tap * 2 + 2) * v1] = jnp.concatenate(
@@ -244,12 +253,14 @@
         back_3[(8 - tap) * v2 : (9 - tap) * v2] = turned.astype(bf16)
 
 
-def perceptual_kernel(
-    shape, received, vgg_first, vgg_second, vgg_third, pixels,
-    weight_1, weight_2, weight_3, back_3, back_2, back_1, shown, grads,
-    target, strips, lines, wide_1, narrow_1, wide_3, narrow_3, wide_g, narrow_g,
-    plane_1, plane_2, spread, wide_b, narrow_b, wide_a, narrow_a,
-):
+def perceptual_kernel(shape, sources, paired, *refs):
+    received = refs[:sources]
+    (
+        vgg_first, vgg_second, vgg_third, pixels,
+        weight_1, weight_2, weight_3, back_3, back_2, back_1, shown, grads,
+        target, strips, lines, wide_1, narrow_1, wide_3, narrow_3, wide_g, narrow_g,
+        plane_1, plane_2, spread, wide_b, narrow_b, wide_a, narrow_a,
+    ) = refs[sources:]
     rows, cols, blocks, block_frames, own, parts, own_slots, frames_own, pack = shape
     f32, bf16 = jnp.float32, jnp.bfloat16
     half = parts * own_slots
@@ -270,8 +281,11 @@
         vgg_first, vgg_second, vgg_third, weight_1, weight_2, weight_3, back_3, back_2, back_1
     )
 
-    for device in range(received.shape[0]):
-        arrived = received[device].astype(f32)
+    place = lax.axis_index("row") * col_parts + lax.axis_index("col")
+    for at in range(shown.shape[0]):
+        per_source = received[0].shape[0]
+        device = place ^ at if paired else at
+        arrived = received[at // per_source][at % per_source].astype(f32)
         target[device] = arrived[3 * rows :]
         shown[device] = jnp.zeros(shown.shape[1:], f32)
         for k in range(3):
@@ -496,7 +510,7 @@
 
     def paint_step(at):
         for step in range(groups):
-            source = lax.rem(group - step + groups, groups)
+            source = partner(group, step, groups)
             slot = painted.at[at, step]
             slot[...] = lax.dot_general(
                 shown[step, pl.ds(pl.multiple_of(at * 8, 8), 8)].astype(jnp.bfloat16),
@@ -533,7 +547,11 @@
             chunks, _, size, _ = terms.shape
             for k in range(chunks):
                 piece = value[k * size : (k + 1) * size].astype(jnp.bfloat16)
-                terms[lax.rem(k - device + chunks, chunks), which] = piece
+                if chunks & (chunks - 1):
+                    at = lax.rem(k - device + chunks, chunks)
+                else:
+                    at = device ^ k
+                terms[at, which] = piece
 
     def own_step(r):
         delta_own[r] = delta_second[r + 1, 1 : 1 + cols].reshape(cols * slots, channels)
@@ -582,26 +600,56 @@
     )
 
 
-def row_halo(own, width):
-    count, length = lax.axis_size("row"), own.shape[0]
-    if count == 2:
-        second = lax.axis_index("row")
-        edge = lax.dynamic_slice_in_dim(own, (1 - second) * (length - width), width, axis=0)
-        came = lax.ppermute(edge, "row", [(0, 1), (1, 0)])
-        place = (jnp.arange(2) == 1 - second).reshape(2, 1, 1, 1, 1)
-        return jnp.where(place, came[None], jnp.zeros_like(came)[None])
-    before = lax.ppermute(own[length - width :], "row", [(i, i + 1) for i in range(count - 1)])
-    after = lax.ppermute(own[:width], "row", [(i + 1, i) for i in range(count - 1)])
-    return jnp.stack([before, after])
-
-
-def col_halo(tall, width):
-    count, length = lax.axis_size("col"), tall.shape[1]
-    before = lax.ppermute(
-        tall[:, length - width :], "col", [(i, i + 1) for i in range(count - 1)]
-    )
-    after = lax.ppermute(tall[:, :width], "col", [(i + 1, i) for i in range(count - 1)])
-    return before, after
+def partners(step, count):
+    if count & (count - 1):
+        return [(i, (i + step) % count) for i in range(count)]
+    return [(i, i ^ step) for i in range(count)]
+
+
+def partner(index, step, count):
+    if count & (count - 1):
+        return lax.rem(index - step + count, count)
+    return index ^ step
+
+
+def matchings(axis):
+    count = lax.axis_size(axis)
+    pairs = []
+    for first in range(2 if count > 2 else 1):
+        pairs.append([(i, i + 1) for i in range(first, count - 1, 2)])
+    return pairs
+
+
+def exchange_pieces(field, width):
+    row_pairs, col_pairs = matchings("row"), matchings("col")
+    col_count = lax.axis_size("col")
+    rows, cols = field.shape[1:3]
+    pieces = []
+    for row_at in (None, *range(len(row_pairs))):
+        for col_at in (None, *range(len(col_pairs))):
+            if row_at is None and col_at is None:
+                continue
+            edge, moves = field, []
+            for axis, dim, at, length in (("row", 1, row_at, rows), ("col", 2, col_at, cols)):
+                if at is not None:
+                    after = (lax.axis_index(axis) % 2 == at).astype(jnp.int32)
+                    edge = lax.dynamic_slice_in_dim(edge, after * (length - width), width, axis=dim)
+            row_moves = [(i, i) for i in range(lax.axis_size("row"))]
+            col_moves = [(i, i) for i in range(col_count)]
+            if row_at is not None:
+                row_moves = [pair for a, b in row_pairs[row_at] for pair in ((a, b), (b, a))]
+            if col_at is not None:
+                col_moves = [pair for a, b in col_pairs[col_at] for pair in ((a, b), (b, a))]
+            moves = [
+                (a * col_count + c, b * col_count + d) for a, b in row_moves for c, d in col_moves
+            ]
+            pieces.append(((row_at, col_at), edge, moves))
+    return pieces
+
+
+def slotted(field, slots):
+    field = jnp.transpose(field, (1, 2, 0, 3))
+    return jnp.pad(field, ((0, 0), (0, 0), (0, slots - field.shape[2]), (0, 0)))
 
 
 def local(dec_input, target, conv_first, conv_second, rgb_weight, vgg_first, vgg_second, vgg_third):
@@ -620,11 +668,11 @@
     lanes = -(-count // 128) * 128
     v1, v2 = vgg_first.shape[1], vgg_third.shape[1]
 
-    own = jnp.transpose(dec_input.reshape(frames, rows, cols, channels), (1, 2, 0, 3))
-    own = jnp.pad(own, ((0, 0), (0, 0), (0, slots - frames), (0, 0)))
-    near = row_halo(own, 3)
-    tall = jnp.concatenate([near[0], own, near[1]], axis=0)
-    before, after = col_halo(tall, 3)
+    raw = dec_input.reshape(frames, rows, cols, channels)
+    pieces = exchange_pieces(raw, 3)
+    places = tuple(place for place, _, _ in pieces)
+    near = [lax.ppermute(slotted(edge, slots), plane, moves) for _, edge, moves in pieces]
+    own = slotted(raw, slots)
 
     line = max(cols * half, -(-width // 128) * 128)
     pack = line // width if parts > 1 and rows % (line // width) == 0 else 1
@@ -633,13 +681,13 @@
     big = 16 if parts > 1 else 40
 
     cells, hidden, slope_first, slope_second, payload = call(
-        functools.partial(forward_kernel, frames, parts, pack),
+        functools.partial(forward_kernel, frames, parts, pack, places),
         (
-            jax.ShapeDtypeStruct((rows + 2, cols + 2, slots, channels), bf16),
-            jax.ShapeDtypeStruct((rows + 2, cols + 2, slots, channels), bf16),
-            jax.ShapeDtypeStruct((rows, cols * slots, channels), f32),
-            jax.ShapeDtypeStruct((rows + 2, (cols + 2) * slots, channels), f32),
-            jax.ShapeDtypeStruct((devices, size, line), bf16),
+            pltpu.HBM((rows + 2, cols + 2, slots, channels), bf16),
+            pltpu.HBM((rows + 2, cols + 2, slots, channels), bf16),
+            pltpu.HBM((rows, cols * slots, channels), f32),
+            pltpu.HBM((rows + 2, (cols + 2) * slots, channels), f32),
+            jax.ShapeDtypeStruct((size, line), bf16),
         ),
         [
             ((rows + 6, cols + 6, slots, channels), bf16),
@@ -655,11 +703,28 @@
         4,
         big,
         hbm_out=(0, 1, 2, 3),
-        operands=8,
+        operands=5 + len(near),
         flops=2**33,
-    )(own, near, before, after, conv_first, conv_second, rgb_weight, target)
-
-    received = lax.all_to_all(payload, plane, split_axis=0, concat_axis=0, tiled=True)
+    )(own, *near, conv_first, conv_second, rgb_weight, target)
+
+    paired = devices == 8 and col_count % 2 == 0
+    if paired:
+        other = lax.ppermute(payload, plane, [(i, i ^ 1) for i in range(devices)])
+        both = jnp.stack([payload, other])
+        received = [both] + [
+            lax.ppermute(both, plane, [(i, i ^ step) for i in range(devices)])
+            for step in range(2, devices, 2)
+        ]
+    else:
+        received = [
+            lax.all_to_all(
+                jnp.broadcast_to(payload[None], (devices,) + payload.shape),
+                plane,
+                split_axis=0,
+                concat_axis=0,
+                tiled=True,
+            )
+        ]
 
     wide_count = count + 6 * half
     pixels = call(
@@ -669,6 +734,8 @@
                 rows, cols, blocks, block_frames, target.shape[2], parts, own_slots, frames_own,
                 pack,
             ),
+            len(received),
+            paired,
         ),
         jax.ShapeDtypeStruct((3, number, (cols + 2) * half), bf16),
         [
@@ -699,14 +766,13 @@
         ],
         0,
         big,
-        operands=4,
+        operands=3 + len(received),
         flops=2**32,
-    )(received, vgg_first, vgg_second, vgg_third)
+    )(*received, vgg_first, vgg_second.T, vgg_third)
 
     gathered = [pixels]
     for step in range(1, groups):
-        ring = [(i, (i + step) % groups) for i in range(groups)]
-        gathered.append(lax.ppermute(pixels, "grp", ring))
+        gathered.append(lax.ppermute(pixels, "grp", partners(step, groups)))
 
     out_rows = conv_first.shape[0] // groups
     taps = max(
@@ -747,8 +813,7 @@
     if even:
         pieces = [terms[0]]
         for step in range(1, devices):
-            ring = [(i, (i + step) % devices) for i in range(devices)]
-            pieces.append(lax.ppermute(terms[step], plane, ring))
+            pieces.append(lax.ppermute(terms[step], plane, partners(step, devices)))
         total = sum(piece.astype(f32) for piece in pieces)
     else:
         pieces = jnp.swapaxes(terms.reshape(2, devices, -1), 0, 1)

time: 76 us -> 68.6 us (0.903)
  waiting for transfers between devices: 18.5 us -> 11.6 us
  local copies, waits for them, and re-layouts: 5.04 us -> 2.27 us
  starting transfers between devices: 24.4 us -> 26.5 us
    ppermute x13 -> x19, starting transfers between devices: 18.1 us -> 26.5 us  [the longest x5 7.51 us: local(): lax.ppermute(slotted(edge, slots), plane, moves)]
    all_to_all x1 -> x0, starting transfers between devices: 6.29 us -> none  [local(): lax.all_to_all(payload, plane, split_axis=0, concat_axis=0, tiled=True)]
    all_to_all x1 -> x0, waiting for transfers between devices: 4.12 us -> none  [local(): lax.all_to_all(payload, plane, split_axis=0, concat_axis=0, tiled=True)]
    unnamed x21 -> x22, local copies, waits for them, and re-layouts: 2.92 us -> 0.06 us
    ppermute x13 -> x19, waiting for transfers between devices: 14.3 us -> 11.6 us  [the longest x3 3.8 us: local(): gathered.append(lax.ppermute(pixels, 'grp', partners(step, groups)))]
  transfers between devices with their start and end apart: 14 -> 19, of which waited for: 8 -> 9; matrix products, arithmetic and copies ran while one was open for 1% -> 0% of each run, Pallas kernels for 0% -> 0%
where the time goes in v3:
time: 68.6 us; the launch traced here: 68.4 us
  Pallas kernels  27.1 us (40%)
  starting transfers between devices  26.5 us (39%)
  waiting for transfers between devices  11.6 us (17%)
  local copies, waits for them, and re-layouts  2.27 us (3%)
  between operations  0.96 us (1%)
    pallas_call x1, Pallas kernels, local(): call(functools.partial(forward_kernel, frames, parts, pack, places), (plt...  11.7 us
    pallas_call x1, Pallas kernels, local(): call(functools.partial(backward_kernel, parts=parts, out_rows=out_rows, g...  8.84 us
    ppermute x5, starting transfers between devices, local(): lax.ppermute(slotted(edge, slots), plane, moves)  7.51 us
    ppermute x7, starting transfers between devices, local(): pieces.append(lax.ppermute(terms[step], plane, partners(step, devices)))  6.59 us
    pallas_call x1, Pallas kernels, local(): call(functools.partial(perceptual_kernel, (rows, cols, blocks, block_fram...  6.58 us
    ppermute x1, starting transfers between devices, local(): other = lax.ppermute(payload, plane, [(i, i ^ 1) for i in range(devices)])  4.47 us
    ppermute x3, starting transfers between devices, local(): gathered.append(lax.ppermute(pixels, 'grp', partners(step, groups)))  4.42 us
    ppermute x3, waiting for transfers between devices, local(): gathered.append(lax.ppermute(pixels, 'grp', partners(step, groups)))  3.8 us
  transfers between devices with their start and end apart: 19, of which 9 were waited for; matrix products, arithmetic and copies ran while one was open for 0% of the time, Pallas kernels for 0%

profile of v3, /device:TPU:0, one launch (start us, length us, event | category | flops | bytes accessed | tf_op | source)
XLA Modules:
  0.0 68.4 jit_solution(3838240930518550686)
XLA Ops:
  0.6 1.3 %copy.19 = bf16[12,8,16,128]{3,0,2,1:T(8,128)(2,1)S(1)} copy(bf16[12,8,16,128]{3,2,1,0:T(8,128)(2,1)} %bitcast.42) | data formatting | bytes 786432 | tf_op jit(solution)/shard_map/reshape | solution.py:671
  2.0 3.0 %collective-permute-start.2 = (bf16[3,16,16,128]{3,2,1,0:T(8,128)(2,1)S(1)}, bf16[3,16,16,128]{3,2,1,0:T(8,128)(2,1)S(1)}, u32[]{:S(2)}, u32[]{:S(2)}) collective-permute-start(bf16[3,16,16,128]{3,2,1,0:T(8,128)(2,1)S(1)} %pad.25), channel_id=1, source_target_pairs={{0,4},{1,5},{2,6},{3,7},{4,0},{5,1},{6,2},{7,3},{8,12},{9,13},{10,... | collective-permute-start | bytes 589832 | tf_op jit(solution)/shard_map/ppermute | solution.py:674
  6.0 3.1 %collective-permute-start.3 = (bf16[3,3,16,128]{3,2,1,0:T(8,128)(2,1)S(1)}, bf16[3,3,16,128]{3,2,1,0:T(8,128)(2,1)S(1)}, u32[]{:S(2)}, u32[]{:S(2)}) collective-permute-start(bf16[3,3,16,128]{3,2,1,0:T(8,128)(2,1)S(1)} %pad.26), channel_id=1, source_target_pairs={{0,5},{1,4},{2,7},{3,6},{4,1},{5,0},{6,3},{7,2},{8,13},{9,12},{10,... | collective-permute-start | bytes 110600 | tf_op jit(solution)/shard_map/ppermute | solution.py:674
  9.9 0.8 %collective-permute-done.3.refs_3_ = bf16[3,3,16,128]{3,2,1,0:T(8,128)(2,1)S(1)} collective-permute-done((bf16[3,3,16,128]{3,2,1,0:T(8,128)(2,1)S(1)}, bf16[3,3,16,128]{3,2,1,0:T(8,128)(2,1)S(1)}, u32[]{:S(2)}, u32[]{:S(2)}) %collective-permute-start.3) | collective-permute-done | bytes 36896 | tf_op jit(solution)/shard_map/ppermute | solution.py:674
  10.8 11.7 %shard_map.95 = (bf16[10,18,16,128]{3,2,1,0:T(8,128)(2,1)}, bf16[10,18,16,128]{3,2,1,0:T(8,128)(2,1)}, f32[8,256,128]{2,1,0:T(8,128)}, f32[10,288,128]{2,1,0:T(8,128)}, bf16[64,128]{1,0:T(8,128)(2,1)S(1)}) custom-call(bf16[8,16,16,128]{3,2,1,0:T(8,128)(2,1)S(1)} %pad.22.own, bf16[8,3,16,128]{3,2,1,0:T(8,128)(2,1)S(1)} %collective-permute-done.refs_0_, ...), custom_call_target="tpu_custom_call" | custom-call | flops 8589934592 | bytes 1048576 | tf_op jit(solution)/shard_map/pallas_call | solution.py:683
  22.4 4.5 %collective-permute-start.5 = (bf16[64,128]{1,0:T(8,128)(2,1)S(1)}, bf16[64,128]{1,0:T(8,128)(2,1)S(1)}, u32[]{:S(2)}, u32[]{:S(2)}) collective-permute-start(bf16[64,128]{1,0:T(8,128)(2,1)S(1)} %get-tuple-element.7), channel_id=1, source_target_pairs={{0,1},{1,0},{2,3},{3,2},{4,5},{5,4},{6,7},{7,6},{8,9},{9,8},{10,11... | collective-permute-start | bytes 49160 | tf_op jit(solution)/shard_map/ppermute | solution.py:712
  26.9 0.8 %collective-permute-done.5 = bf16[64,128]{1,0:T(8,128)(2,1)S(1)} collective-permute-done((bf16[64,128]{1,0:T(8,128)(2,1)S(1)}, bf16[64,128]{1,0:T(8,128)(2,1)S(1)}, u32[]{:S(2)}, u32[]{:S(2)}) %collective-permute-start.5) | collective-permute-done | bytes 16416 | tf_op jit(solution)/shard_map/ppermute | solution.py:712
  28.3 1.8 %collective-permute-start.7 = (bf16[2,64,128]{2,1,0:T(8,128)(2,1)S(1)}, bf16[2,64,128]{2,1,0:T(8,128)(2,1)S(1)}, u32[]{:S(2)}, u32[]{:S(2)}) collective-permute-start(bf16[2,64,128]{2,1,0:T(8,128)(2,1)S(1)} %pad_maximum_fusion.refs_0_), channel_id=1, source_target_pairs={{0,4},{1,5},{2,6},{3,7},{4,0},{5,1},{6,2},{7,3},{8,12},{9,13},{10,... | collective-permute-start | bytes 98312 | tf_op jit(solution)/shard_map/ppermute | solution.py:715
  30.0 1.2 %collective-permute-start.6 = (bf16[2,64,128]{2,1,0:T(8,128)(2,1)S(1)}, bf16[2,64,128]{2,1,0:T(8,128)(2,1)S(1)}, u32[]{:S(2)}, u32[]{:S(2)}) collective-permute-start(bf16[2,64,128]{2,1,0:T(8,128)(2,1)S(1)} %pad_maximum_fusion.refs_0_), channel_id=1, source_target_pairs={{0,2},{1,3},{2,0},{3,1},{4,6},{5,7},{6,4},{7,5},{8,10},{9,11},{10,... | collective-permute-start | bytes 98312 | tf_op jit(solution)/shard_map/ppermute | solution.py:715
  31.2 1.5 %collective-permute-done.8.refs_3_ = bf16[2,64,128]{2,1,0:T(8,128)(2,1)S(1)} collective-permute-done((bf16[2,64,128]{2,1,0:T(8,128)(2,1)S(1)}, bf16[2,64,128]{2,1,0:T(8,128)(2,1)S(1)}, u32[]{:S(2)}, u32[]{:S(2)}) %collective-permute-start.8) | collective-permute-done | bytes 32800 | tf_op jit(solution)/shard_map/ppermute | solution.py:715
  32.7 1.2 %collective-permute-done.6.refs_1_ = bf16[2,64,128]{2,1,0:T(8,128)(2,1)S(1)} collective-permute-done((bf16[2,64,128]{2,1,0:T(8,128)(2,1)S(1)}, bf16[2,64,128]{2,1,0:T(8,128)(2,1)S(1)}, u32[]{:S(2)}, u32[]{:S(2)}) %collective-permute-start.6) | collective-permute-done | bytes 32800 | tf_op jit(solution)/shard_map/ppermute | solution.py:715
  34.0 6.6 %shard_map.96.refs_0_ = bf16[3,8,144]{2,1,0:T(8,128)(2,1)S(1)} custom-call(bf16[2,64,128]{2,1,0:T(8,128)(2,1)S(1)} %pad_maximum_fusion.refs_0_, bf16[2,64,128]{2,1,0:T(8,128)(2,1)S(1)} %collective-permute-done.6.refs_1_, bf16[2,64,128]{2,1,0:T(8,128)(2,1)S(1)} %collective-permute-done.7.refs_2_, bf16[2,64,128]{2,1,0:T(8,128)(2,1)S(1)} %collective-permute-done.8.refs_3_, ...), custom_call_target="tpu_custom_call" | custom-call | flops 4294967296 | bytes 1048576 | tf_op jit(solution)/shard_map/pallas_call | solution.py:730
  40.6 3.6 %collective-permute-start.11 = (bf16[3,8,144]{2,1,0:T(8,128)(2,1)S(1)}, bf16[3,8,144]{2,1,0:T(8,128)(2,1)S(1)}, u32[]{:S(2)}, u32[]{:S(2)}) collective-permute-start(bf16[3,8,144]{2,1,0:T(8,128)(2,1)S(1)} %shard_map.96.refs_0_), channel_id=1, source_target_pairs={{0,24},{8,16},{16,8},{24,0},{1,25},{9,17},{17,9},{25,1},{2,26},{10... | collective-permute-start | bytes 20744 | tf_op jit(solution)/shard_map/ppermute | solution.py:775
  44.2 0.8 %collective-permute-start.9 = (bf16[3,8,144]{2,1,0:T(8,128)(2,1)S(1)}, bf16[3,8,144]{2,1,0:T(8,128)(2,1)S(1)}, u32[]{:S(2)}, u32[]{:S(2)}) collective-permute-start(bf16[3,8,144]{2,1,0:T(8,128)(2,1)S(1)} %shard_map.96.refs_0_), channel_id=1, source_target_pairs={{0,8},{8,0},{16,24},{24,16},{1,9},{9,1},{17,25},{25,17},{2,10},{10... | collective-permute-start | bytes 20744 | tf_op jit(solution)/shard_map/ppermute | solution.py:775
  45.0 1.1 %collective-permute-done.11.refs_3_ = bf16[3,8,144]{2,1,0:T(8,128)(2,1)S(1)} collective-permute-done((bf16[3,8,144]{2,1,0:T(8,128)(2,1)S(1)}, bf16[3,8,144]{2,1,0:T(8,128)(2,1)S(1)}, u32[]{:S(2)}, u32[]{:S(2)}) %collective-permute-start.11) | collective-permute-done | bytes 6944 | tf_op jit(solution)/shard_map/ppermute | solution.py:775
  46.1 2.7 %collective-permute-done.10.refs_2_ = bf16[3,8,144]{2,1,0:T(8,128)(2,1)S(1)} collective-permute-done((bf16[3,8,144]{2,1,0:T(8,128)(2,1)S(1)}, bf16[3,8,144]{2,1,0:T(8,128)(2,1)S(1)}, u32[]{:S(2)}, u32[]{:S(2)}) %collective-permute-start.10) | collective-permute-done | bytes 6944 | tf_op jit(solution)/shard_map/ppermute | solution.py:775
  48.8 8.8 %shard_map.97 = bf16[8,2,108,128]{3,2,1,0:T(8,128)(2,1)S(1)} custom-call(bf16[3,8,144]{2,1,0:T(8,128)(2,1)S(1)} %shard_map.96.refs_0_, bf16[3,8,144]{2,1,0:T(8,128)(2,1)S(1)} %collective-permute-done.9.refs_1_, bf16[3,8,144]{2,1,0:T(8,128)(2,1)S(1)} %collective-permute-done.10.refs_2_, bf16[3,8,144]{2,1,0:T(8,128)(2,1)S(1)} %collective-permute-done.11.refs_3_, ...), custom_call_target="tpu_custom_call" | custom-call | flops 4294967296 | bytes 1048576 | tf_op jit(solution)/shard_map/pallas_call | solution.py:785
  57.8 1.2 %collective-permute-start.18 = (bf16[2,108,128]{2,1,0:T(8,128)(2,1)S(1)}, bf16[2,108,128]{2,1,0:T(8,128)(2,1)S(1)}, u32[]{:S(2)}, u32[]{:S(2)}) collective-permute-start(bf16[2,108,128]{2,1,0:T(8,128)(2,1)S(1)} %get-tuple-element.17), channel_id=1, source_target_pairs={{0,7},{1,6},{2,5},{3,4},{4,3},{5,2},{6,1},{7,0},{8,15},{9,14},{10,... | collective-permute-start | bytes 165896 | tf_op jit(solution)/shard_map/ppermute | solution.py:816
  59.1 1.8 %collective-permute-start.17 = (bf16[2,108,128]{2,1,0:T(8,128)(2,1)S(1)}, bf16[2,108,128]{2,1,0:T(8,128)(2,1)S(1)}, u32[]{:S(2)}, u32[]{:S(2)}) collective-permute-start(bf16[2,108,128]{2,1,0:T(8,128)(2,1)S(1)} %get-tuple-element.18), channel_id=1, source_target_pairs={{0,6},{1,7},{2,4},{3,5},{4,2},{5,3},{6,0},{7,1},{8,14},{9,15},{10,... | collective-permute-start | bytes 165896 | tf_op jit(solution)/shard_map/ppermute | solution.py:816
  60.8 1.4 %collective-permute-start.15 = (bf16[2,108,128]{2,1,0:T(8,128)(2,1)S(1)}, bf16[2,108,128]{2,1,0:T(8,128)(2,1)S(1)}, u32[]{:S(2)}, u32[]{:S(2)}) collective-permute-start(bf16[2,108,128]{2,1,0:T(8,128)(2,1)S(1)} %get-tuple-element.20), channel_id=1, source_target_pairs={{0,4},{1,5},{2,6},{3,7},{4,0},{5,1},{6,2},{7,3},{8,12},{9,13},{10,... | collective-permute-start | bytes 165896 | tf_op jit(solution)/shard_map/ppermute | solution.py:816
  62.3 1.2 %collective-permute-start.14 = (bf16[2,108,128]{2,1,0:T(8,128)(2,1)S(1)}, bf16[2,108,128]{2,1,0:T(8,128)(2,1)S(1)}, u32[]{:S(2)}, u32[]{:S(2)}) collective-permute-start(bf16[2,108,128]{2,1,0:T(8,128)(2,1)S(1)} %get-tuple-element.21), channel_id=1, source_target_pairs={{0,3},{1,2},{2,1},{3,0},{4,7},{5,6},{6,5},{7,4},{8,11},{9,10},{10,... | collective-permute-start | bytes 165896 | tf_op jit(solution)/shard_map/ppermute | solution.py:816
  63.5 0.9 %collective-permute-start.13 = (bf16[2,108,128]{2,1,0:T(8,128)(2,1)S(1)}, bf16[2,108,128]{2,1,0:T(8,128)(2,1)S(1)}, u32[]{:S(2)}, u32[]{:S(2)}) collective-permute-start(bf16[2,108,128]{2,1,0:T(8,128)(2,1)S(1)} %get-tuple-element.22), channel_id=1, source_target_pairs={{0,2},{1,3},{2,0},{3,1},{4,6},{5,7},{6,4},{7,5},{8,10},{9,11},{10,... | collective-permute-start | bytes 165896 | tf_op jit(solution)/shard_map/ppermute | solution.py:816
  65.0 1.3 %collective-permute-done.15 = bf16[2,108,128]{2,1,0:T(8,128)(2,1)S(1)} collective-permute-done((bf16[2,108,128]{2,1,0:T(8,128)(2,1)S(1)}, bf16[2,108,128]{2,1,0:T(8,128)(2,1)S(1)}, u32[]{:S(2)}, u32[]{:S(2)}) %collective-permute-start.15) | collective-permute-done | bytes 55328 | tf_op jit(solution)/shard_map/ppermute | solution.py:816
  66.4 1.3 %collective-permute-done.13 = bf16[2,108,128]{2,1,0:T(8,128)(2,1)S(1)} collective-permute-done((bf16[2,108,128]{2,1,0:T(8,128)(2,1)S(1)}, bf16[2,108,128]{2,1,0:T(8,128)(2,1)S(1)}, u32[]{:S(2)}, u32[]{:S(2)}) %collective-permute-start.13) | collective-permute-done | bytes 55328 | tf_op jit(solution)/shard_map/ppermute | solution.py:816
  (53 shorter events, 3.8 us)
Async XLA Ops:
  2.0 8.7 %collective-permute-start.2 = (bf16[3,16,16,128]{3,2,1,0:T(8,128)(2,1)S(1)}, bf16[3,16,16,128]{3,2,1,0:T(8,128)(2,1)S(1)}, u32[]{:S(2)}, u32[]{:S(2)}) collective-permute-start(bf16[3,16,16,128]{3,2,1,0:T(8,128)(2,1)S(1)} %pad.25), channel_id=1, source_target_pairs={{0,4},{1,5},{2,6},{3,7},{4,0},{5,1},{6,2},{7,3},{8,12},{9,13},{10,... | collective-permute-start | bytes 589832 | tf_op jit(solution)/shard_map/ppermute | solution.py:674
  5.1 5.6 %collective-permute-start = (bf16[8,3,16,128]{3,2,1,0:T(8,128)(2,1)S(1)}, bf16[8,3,16,128]{3,2,1,0:T(8,128)(2,1)S(1)}, u32[]{:S(2)}, u32[]{:S(2)}) collective-permute-start(bf16[8,3,16,128]{3,2,1,0:T(8,128)(2,1)S(1)} %pad.23), channel_id=1, source_target_pairs={{0,1},{1,0},{2,3},{3,2},{4,5},{5,4},{6,7},{7,6},{8,9},{9,8},{10,11... | collective-permute-start | bytes 294920 | tf_op jit(solution)/shard_map/ppermute | solution.py:674
  5.2 5.5 %collective-permute-start.1 = (bf16[8,3,16,128]{3,2,1,0:T(8,128)(2,1)S(1)}, bf16[8,3,16,128]{3,2,1,0:T(8,128)(2,1)S(1)}, u32[]{:S(2)}, u32[]{:S(2)}) collective-permute-start(bf16[8,3,16,128]{3,2,1,0:T(8,128)(2,1)S(1)} %pad.24), channel_id=1, source_target_pairs={{1,2},{2,1},{5,6},{6,5},{9,10},{10,9},{13,14},{14,13},{17,18},{18,... | collective-permute-start | bytes 294920 | tf_op jit(solution)/shard_map/ppermute | solution.py:674
  6.0 4.7 %collective-permute-start.3 = (bf16[3,3,16,128]{3,2,1,0:T(8,128)(2,1)S(1)}, bf16[3,3,16,128]{3,2,1,0:T(8,128)(2,1)S(1)}, u32[]{:S(2)}, u32[]{:S(2)}) collective-permute-start(bf16[3,3,16,128]{3,2,1,0:T(8,128)(2,1)S(1)} %pad.26), channel_id=1, source_target_pairs={{0,5},{1,4},{2,7},{3,6},{4,1},{5,0},{6,3},{7,2},{8,13},{9,12},{10,... | collective-permute-start | bytes 110600 | tf_op jit(solution)/shard_map/ppermute | solution.py:674
  9.1 1.6 %collective-permute-start.4 = (bf16[3,3,16,128]{3,2,1,0:T(8,128)(2,1)S(1)}, bf16[3,3,16,128]{3,2,1,0:T(8,128)(2,1)S(1)}, u32[]{:S(2)}, u32[]{:S(2)}) collective-permute-start(bf16[3,3,16,128]{3,2,1,0:T(8,128)(2,1)S(1)} %pad.27), channel_id=1, source_target_pairs={{1,6},{2,5},{5,2},{6,1},{9,14},{10,13},{13,10},{14,9},{17,22},{18,... | collective-permute-start | bytes 110600 | tf_op jit(solution)/shard_map/ppermute | solution.py:674
  9.9 24.1 %copy-start.2 = (bf16[576,128]{1,0:T(8,128)(2,1)S(1)}, bf16[576,128]{1,0:T(8,128)(2,1)}, u32[]{:S(2)}) copy-start(bf16[576,128]{1,0:T(8,128)(2,1)} %refs_6_.3) | copy-start | bytes 442372
  9.9 24.1 %copy-start.3 = (bf16[576,64]{0,1:T(8,128)(2,1)S(1)}, bf16[576,64]{0,1:T(8,128)(2,1)}, u32[]{:S(2)}) copy-start(bf16[576,64]{0,1:T(8,128)(2,1)} %param.14) | copy-start | bytes 221188
  9.9 24.1 %copy-start.5 = (bf16[27,64]{1,0:T(8,128)(2,1)S(1)}, bf16[27,64]{1,0:T(8,128)(2,1)}, u32[]{:S(2)}) copy-start(bf16[27,64]{1,0:T(8,128)(2,1)} %refs_4_.2) | copy-start | bytes 10372
  22.4 5.3 %collective-permute-start.5 = (bf16[64,128]{1,0:T(8,128)(2,1)S(1)}, bf16[64,128]{1,0:T(8,128)(2,1)S(1)}, u32[]{:S(2)}, u32[]{:S(2)}) collective-permute-start(bf16[64,128]{1,0:T(8,128)(2,1)S(1)} %get-tuple-element.7), channel_id=1, source_target_pairs={{0,1},{1,0},{2,3},{3,2},{4,5},{5,4},{6,7},{7,6},{8,9},{9,8},{10,11... | collective-permute-start | bytes 49160 | tf_op jit(solution)/shard_map/ppermute | solution.py:712
  27.7 5.0 %collective-permute-start.8 = (bf16[2,64,128]{2,1,0:T(8,128)(2,1)S(1)}, bf16[2,64,128]{2,1,0:T(8,128)(2,1)S(1)}, u32[]{:S(2)}, u32[]{:S(2)}) collective-permute-start(bf16[2,64,128]{2,1,0:T(8,128)(2,1)S(1)} %pad_maximum_fusion.refs_0_), channel_id=1, source_target_pairs={{0,6},{1,7},{2,4},{3,5},{4,2},{5,3},{6,0},{7,1},{8,14},{9,15},{10,... | collective-permute-start | bytes 98312 | tf_op jit(solution)/shard_map/ppermute | solution.py:715
  28.3 4.5 %collective-permute-start.7 = (bf16[2,64,128]{2,1,0:T(8,128)(2,1)S(1)}, bf16[2,64,128]{2,1,0:T(8,128)(2,1)S(1)}, u32[]{:S(2)}, u32[]{:S(2)}) collective-permute-start(bf16[2,64,128]{2,1,0:T(8,128)(2,1)S(1)} %pad_maximum_fusion.refs_0_), channel_id=1, source_target_pairs={{0,4},{1,5},{2,6},{3,7},{4,0},{5,1},{6,2},{7,3},{8,12},{9,13},{10,... | collective-permute-start | bytes 98312 | tf_op jit(solution)/shard_map/ppermute | solution.py:715
  30.0 3.9 %collective-permute-start.6 = (bf16[2,64,128]{2,1,0:T(8,128)(2,1)S(1)}, bf16[2,64,128]{2,1,0:T(8,128)(2,1)S(1)}, u32[]{:S(2)}, u32[]{:S(2)}) collective-permute-start(bf16[2,64,128]{2,1,0:T(8,128)(2,1)S(1)} %pad_maximum_fusion.refs_0_), channel_id=1, source_target_pairs={{0,2},{1,3},{2,0},{3,1},{4,6},{5,7},{6,4},{7,5},{8,10},{9,11},{10,... | collective-permute-start | bytes 98312 | tf_op jit(solution)/shard_map/ppermute | solution.py:715
  34.0 14.9 %copy-start.7 = (f32[10,288,128]{2,1,0:T(8,128)S(1)}, f32[10,288,128]{2,1,0:T(8,128)}, u32[]{:S(2)}) copy-start(f32[10,288,128]{2,1,0:T(8,128)} %get-tuple-element.9.refs_7_) | copy-start | bytes 4423684
  34.0 14.8 %copy-start.8 = (f32[8,256,128]{2,1,0:T(8,128)S(1)}, f32[8,256,128]{2,1,0:T(8,128)}, u32[]{:S(2)}) copy-start(f32[8,256,128]{2,1,0:T(8,128)} %get-tuple-element.8.refs_6_) | copy-start | bytes 3145732
  40.6 5.5 %collective-permute-start.11 = (bf16[3,8,144]{2,1,0:T(8,128)(2,1)S(1)}, bf16[3,8,144]{2,1,0:T(8,128)(2,1)S(1)}, u32[]{:S(2)}, u32[]{:S(2)}) collective-permute-start(bf16[3,8,144]{2,1,0:T(8,128)(2,1)S(1)} %shard_map.96.refs_0_), channel_id=1, source_target_pairs={{0,24},{8,16},{16,8},{24,0},{1,25},{9,17},{17,9},{25,1},{2,26},{10... | collective-permute-start | bytes 20744 | tf_op jit(solution)/shard_map/ppermute | solution.py:775
  44.2 4.6 %collective-permute-start.10 = (bf16[3,8,144]{2,1,0:T(8,128)(2,1)S(1)}, bf16[3,8,144]{2,1,0:T(8,128)(2,1)S(1)}, u32[]{:S(2)}, u32[]{:S(2)}) collective-permute-start(bf16[3,8,144]{2,1,0:T(8,128)(2,1)S(1)} %shard_map.96.refs_0_), channel_id=1, source_target_pairs={{0,16},{8,24},{16,0},{24,8},{1,17},{9,25},{17,1},{25,9},{2,18},{10... | collective-permute-start | bytes 20744 | tf_op jit(solution)/shard_map/ppermute | solution.py:775
  44.2 4.6 %collective-permute-start.9 = (bf16[3,8,144]{2,1,0:T(8,128)(2,1)S(1)}, bf16[3,8,144]{2,1,0:T(8,128)(2,1)S(1)}, u32[]{:S(2)}, u32[]{:S(2)}) collective-permute-start(bf16[3,8,144]{2,1,0:T(8,128)(2,1)S(1)} %shard_map.96.refs_0_), channel_id=1, source_target_pairs={{0,8},{8,0},{16,24},{24,16},{1,9},{9,1},{17,25},{25,17},{2,10},{10... | collective-permute-start | bytes 20744 | tf_op jit(solution)/shard_map/ppermute | solution.py:775
  57.7 4.5 %collective-permute-start.12 = (bf16[2,108,128]{2,1,0:T(8,128)(2,1)S(1)}, bf16[2,108,128]{2,1,0:T(8,128)(2,1)S(1)}, u32[]{:S(2)}, u32[]{:S(2)}) collective-permute-start(bf16[2,108,128]{2,1,0:T(8,128)(2,1)S(1)} %get-tuple-element.16), channel_id=1, source_target_pairs={{0,1},{1,0},{2,3},{3,2},{4,5},{5,4},{6,7},{7,6},{8,9},{9,8},{10,11... | collective-permute-start | bytes 165896 | tf_op jit(solution)/shard_map/ppermute | solution.py:816
  57.8 5.7 %collective-permute-start.18 = (bf16[2,108,128]{2,1,0:T(8,128)(2,1)S(1)}, bf16[2,108,128]{2,1,0:T(8,128)(2,1)S(1)}, u32[]{:S(2)}, u32[]{:S(2)}) collective-permute-start(bf16[2,108,128]{2,1,0:T(8,128)(2,1)S(1)} %get-tuple-element.17), channel_id=1, source_target_pairs={{0,7},{1,6},{2,5},{3,4},{4,3},{5,2},{6,1},{7,0},{8,15},{9,14},{10,... | collective-permute-start | bytes 165896 | tf_op jit(solution)/shard_map/ppermute | solution.py:816
  59.1 5.3 %collective-permute-start.17 = (bf16[2,108,128]{2,1,0:T(8,128)(2,1)S(1)}, bf16[2,108,128]{2,1,0:T(8,128)(2,1)S(1)}, u32[]{:S(2)}, u32[]{:S(2)}) collective-permute-start(bf16[2,108,128]{2,1,0:T(8,128)(2,1)S(1)} %get-tuple-element.18), channel_id=1, source_target_pairs={{0,6},{1,7},{2,4},{3,5},{4,2},{5,3},{6,0},{7,1},{8,14},{9,15},{10,... | collective-permute-start | bytes 165896 | tf_op jit(solution)/shard_map/ppermute | solution.py:816
  60.8 4.2 %collective-permute-start.16 = (bf16[2,108,128]{2,1,0:T(8,128)(2,1)S(1)}, bf16[2,108,128]{2,1,0:T(8,128)(2,1)S(1)}, u32[]{:S(2)}, u32[]{:S(2)}) collective-permute-start(bf16[2,108,128]{2,1,0:T(8,128)(2,1)S(1)} %get-tuple-element.19), channel_id=1, source_target_pairs={{0,5},{1,4},{2,7},{3,6},{4,1},{5,0},{6,3},{7,2},{8,13},{9,12},{10,... | collective-permute-start | bytes 165896 | tf_op jit(solution)/shard_map/ppermute | solution.py:816
  60.8 5.5 %collective-permute-start.15 = (bf16[2,108,128]{2,1,0:T(8,128)(2,1)S(1)}, bf16[2,108,128]{2,1,0:T(8,128)(2,1)S(1)}, u32[]{:S(2)}, u32[]{:S(2)}) collective-permute-start(bf16[2,108,128]{2,1,0:T(8,128)(2,1)S(1)} %get-tuple-element.20), channel_id=1, source_target_pairs={{0,4},{1,5},{2,6},{3,7},{4,0},{5,1},{6,2},{7,3},{8,12},{9,13},{10,... | collective-permute-start | bytes 165896 | tf_op jit(solution)/shard_map/ppermute | solution.py:816
  62.3 4.1 %collective-permute-start.14 = (bf16[2,108,128]{2,1,0:T(8,128)(2,1)S(1)}, bf16[2,108,128]{2,1,0:T(8,128)(2,1)S(1)}, u32[]{:S(2)}, u32[]{:S(2)}) collective-permute-start(bf16[2,108,128]{2,1,0:T(8,128)(2,1)S(1)} %get-tuple-element.21), channel_id=1, source_target_pairs={{0,3},{1,2},{2,1},{3,0},{4,7},{5,6},{6,5},{7,4},{8,11},{9,10},{10,... | collective-permute-start | bytes 165896 | tf_op jit(solution)/shard_map/ppermute | solution.py:816
  63.5 4.2 %collective-permute-start.13 = (bf16[2,108,128]{2,1,0:T(8,128)(2,1)S(1)}, bf16[2,108,128]{2,1,0:T(8,128)(2,1)S(1)}, u32[]{:S(2)}, u32[]{:S(2)}) collective-permute-start(bf16[2,108,128]{2,1,0:T(8,128)(2,1)S(1)} %get-tuple-element.22), channel_id=1, source_target_pairs={{0,2},{1,3},{2,0},{3,1},{4,6},{5,7},{6,4},{7,5},{8,10},{9,11},{10,... | collective-permute-start | bytes 165896 | tf_op jit(solution)/shard_map/ppermute | solution.py:816
  (6 other events, 64.9 us)

commit v4 on v3

--- a/solution.py
+++ b/solution.py
@@ -82,8 +82,9 @@
     (
         first, second, rgb, target, cells_out, hidden_out, first_out, second_out, payload,
         cells, hidden, slope_first, slope_second, spread_weight, picked, spaced, colour, project,
-        sems,
+        unpacked, corner_rows, sems,
     ) = refs[len(places) :]
+    unpacked[...] = jnp.zeros(unpacked.shape, jnp.float32)
     rows, cols, slots, channels = own.shape
     f32, bf16 = jnp.float32, jnp.bfloat16
     groups, group = lax.axis_size("grp"), lax.axis_index("grp")
@@ -102,7 +103,30 @@
             row = jnp.where(lax.axis_index("row") % 2 == row_at, 3 + rows, 0)
         if col_at is not None:
             col = jnp.where(lax.axis_index("col") % 2 == col_at, 3 + cols, 0)
-        cells[pl.ds(row, piece.shape[0]), pl.ds(col, piece.shape[1])] = piece[...]
+        if row_at is None:
+            for f in range(frames):
+                for c in range(3):
+                    unpacked[pl.ds(c * rows * slots + f, rows, stride=slots)] = piece[f, c].astype(
+                        f32
+                    )
+            for c in range(3):
+                line = unpacked[c * rows * slots : (c + 1) * rows * slots].astype(bf16)
+                cells[3 : 3 + rows, col + c] = line.reshape(rows, slots, channels)
+        elif col_at is None:
+            for f in range(frames):
+                for r in range(3):
+                    unpacked[pl.ds(r * cols * slots + f, cols, stride=slots)] = piece[f, r].astype(
+                        f32
+                    )
+            for r in range(3):
+                line = unpacked[r * cols * slots : (r + 1) * cols * slots].astype(bf16)
+                cells[row + r, 3 : 3 + cols] = line.reshape(cols, slots, channels)
+        else:
+            corner_rows[...] = piece[...].astype(f32)
+            for r in range(3):
+                for c in range(3):
+                    unpacked[0:frames] = corner_rows[pl.ds(r * 3 + c, frames, stride=9)]
+                    cells[row + r, col + c] = unpacked[0:slots].astype(bf16)
     copies = [
         pltpu.make_async_copy(
             cells.at[pl.ds(2, rows + 2), pl.ds(2, cols + 2)], cells_out, sems.at[0]
@@ -474,13 +498,16 @@
     repeat(sums.shape[0] // channels, tap_step, 8)
 
 
-def backward_kernel(*refs, parts, out_rows, groups):
+def backward_kernel(*refs, parts, out_rows, groups, outs):
     pixels = refs[:groups]
     (
-        rgb, conv_second, first_in, second_in, cells_in, hidden_in, terms,
+        rgb, conv_second, first_in, second_in, cells_in, hidden_in,
+    ) = refs[groups : groups + 6]
+    terms = refs[groups + 6 : groups + 6 + outs]
+    (
         slope_first, slope_second, cells, hidden, weight, back_second, paint, shown,
         painted, hidden_grad, delta_second, delta_own, shifted, sums, sems,
-    ) = refs[groups:]
+    ) = refs[groups + 6 + outs :]
     copies = [
         pltpu.make_async_copy(second_in, slope_second, sems.at[0]),
         pltpu.make_async_copy(hidden_in, hidden, sems.at[1]),
@@ -541,17 +568,27 @@
 
     def put(which):
         value = sums[pl.ds(skip, out_rows)]
-        if len(terms.shape) == 3:
-            terms[which] = value.astype(jnp.bfloat16)
-        else:
-            chunks, _, size, _ = terms.shape
-            for k in range(chunks):
-                piece = value[k * size : (k + 1) * size].astype(jnp.bfloat16)
-                if chunks & (chunks - 1):
-                    at = lax.rem(k - device + chunks, chunks)
-                else:
-                    at = device ^ k
-                terms[at, which] = piece
+        if len(terms[0].shape) == 3:
+            terms[0][which] = value.astype(jnp.bfloat16)
+            return
+        chunks, _, size, _ = terms[0].shape
+        chunks = chunks * outs
+        for k in range(chunks):
+            piece = value[k * size : (k + 1) * size].astype(jnp.bfloat16)
+            if chunks & (chunks - 1):
+                terms[0][lax.rem(k - device + chunks, chunks), which] = piece
+            elif outs == 1:
+                terms[0][device ^ k, which] = piece
+            else:
+                at = device ^ k
+
+                @pl.when(at % 2 == 0)
+                def _():
+                    terms[0][at // 2, which] = piece
+
+                @pl.when(at % 2 == 1)
+                def _():
+                    terms[1][at // 2, which] = piece
 
     def own_step(r):
         delta_own[r] = delta_second[r + 1, 1 : 1 + cols].reshape(cols * slots, channels)
@@ -647,6 +684,15 @@
     return pieces
 
 
+def packed_edge(place, edge):
+    row_at, col_at = place
+    if row_at is None:
+        return jnp.swapaxes(edge, 1, 2)
+    if col_at is None:
+        return edge
+    return edge.reshape(-1, edge.shape[3])
+
+
 def slotted(field, slots):
     field = jnp.transpose(field, (1, 2, 0, 3))
     return jnp.pad(field, ((0, 0), (0, 0), (0, slots - field.shape[2]), (0, 0)))
@@ -671,7 +717,9 @@
     raw = dec_input.reshape(frames, rows, cols, channels)
     pieces = exchange_pieces(raw, 3)
     places = tuple(place for place, _, _ in pieces)
-    near = [lax.ppermute(slotted(edge, slots), plane, moves) for _, edge, moves in pieces]
+    near = [
+        lax.ppermute(packed_edge(place, edge), plane, moves) for place, edge, moves in pieces
+    ]
     own = slotted(raw, slots)
 
     line = max(cols * half, -(-width // 128) * 128)
@@ -699,6 +747,8 @@
             ((rows + 2, cols * half, channels), f32),
             (((rows + 2) * 8, cols * half), f32),
             ((8, channels), f32),
+            ((3 * max(rows, cols) * slots, channels), f32),
+            ((9 * frames, channels), f32),
         ],
         4,
         big,
@@ -779,12 +829,18 @@
         -(-(g + 1) * out_rows // channels) - g * out_rows // channels for g in range(groups)
     )
     even = out_rows % devices == 0
-    out_shape = (
-        (devices, 2, out_rows // devices, channels) if even else (2, out_rows, channels)
-    )
+    out_shape = jax.ShapeDtypeStruct((2, out_rows, channels), bf16)
+    if even:
+        count_out = devices // 2 if paired else devices
+        out_shape = jax.ShapeDtypeStruct((count_out, 2, out_rows // devices, channels), bf16)
+    if even and paired:
+        out_shape = (out_shape, out_shape)
     terms = call(
-        functools.partial(backward_kernel, parts=parts, out_rows=out_rows, groups=groups),
-        jax.ShapeDtypeStruct(out_shape, bf16),
+        functools.partial(
+            backward_kernel, parts=parts, out_rows=out_rows, groups=groups,
+            outs=2 if even and paired else 1,
+        ),
+        out_shape,
         [
             ((rows, cols * slots, channels), f32),
             ((rows + 2, (cols + 2) * slots, channels), f32),
@@ -810,7 +866,15 @@
         *gathered, rgb_weight, conv_second, slope_first, slope_second, cells, hidden,
     )
 
-    if even:
+    if even and paired:
+        kept, given = terms
+        came = lax.ppermute(given, plane, partners(1, devices))
+        halves = [kept[k].astype(f32) + came[k].astype(f32) for k in range(devices // 2)]
+        total = halves[0]
+        for k in range(1, devices // 2):
+            half_sum = lax.ppermute(halves[k].astype(bf16), plane, partners(2 * k, devices))
+            total = total + half_sum.astype(f32)
+    elif even:
         pieces = [terms[0]]
         for step in range(1, devices):
             pieces.append(lax.ppermute(terms[step], plane, partners(step, devices)))

time: 68.6 us -> 70.1 us (1.022)
  starting transfers between devices: 26.5 us -> 22.6 us
  local copies, waits for them, and re-layouts: 2.27 us -> 5.36 us
  waiting for transfers between devices: 11.6 us -> 13.1 us
    ppermute x12 -> x9, starting transfers between devices: 14.1 us -> 11.2 us  [the longest x5 7.58 us: local(): lax.ppermute(packed_edge(place, edge), plane, moves)]
    ppermute x12 -> x9, waiting for transfers between devices: 4.21 us -> 6.29 us  [the longest x3 3.85 us: local(): lax.ppermute(halves[k].astype(bf16), plane, partners(2 * k, devices))]
    dynamic_slice x0 -> x2, local copies, waits for them, and re-layouts: none -> 1.94 us  [exchange_pieces(): lax.dynamic_slice_in_dim(edge, after * (length - width), width, axis=dim)]
    unnamed x22 -> x23, local copies, waits for them, and re-layouts: 0.06 us -> 1.32 us
    reshape x1 -> x2, local copies, waits for them, and re-layouts: 1.27 us -> 0.06 us  [packed_edge(): return edge.reshape(-1, edge.shape[3])]
    transpose x3 -> x1, local copies, waits for them, and re-layouts: 0.06 us -> 1.26 us  [packed_edge(): return jnp.swapaxes(edge, 1, 2)]
    ppermute x1, starting transfers between devices: 4.47 us -> 3.47 us  [local(): other = lax.ppermute(payload, plane, [(i, i ^ 1) for i in range(devices)])]
  transfers between devices with their start and end apart: 19 -> 16, of which waited for: 9 -> 10; matrix products, arithmetic and copies ran while one was open for 0% -> 5% of each run, Pallas kernels for 0% -> 0%
where the time goes in v4:
time: 70.1 us; the launch traced here: 69.8 us
  Pallas kernels  27.8 us (40%)
  starting transfers between devices  22.6 us (32%)
  waiting for transfers between devices  13.1 us (19%)
  local copies, waits for them, and re-layouts  5.36 us (8%)
  between operations  0.88 us (1%)
    pallas_call x1, Pallas kernels, local(): call(functools.partial(forward_kernel, frames, parts, pack, places), (plt...  12.1 us
    pallas_call x1, Pallas kernels, local(): call(functools.partial(backward_kernel, parts=parts, out_rows=out_rows, g...  9.13 us
    ppermute x5, starting transfers between devices, local(): lax.ppermute(packed_edge(place, edge), plane, moves)  7.58 us
    pallas_call x1, Pallas kernels, local(): call(functools.partial(perceptual_kernel, (rows, cols, blocks, block_fram...  6.59 us
    ppermute x3, starting transfers between devices, local(): gathered.append(lax.ppermute(pixels, 'grp', partners(step, groups)))  4.42 us
    ppermute x3, waiting for transfers between devices, local(): lax.ppermute(halves[k].astype(bf16), plane, partners(2 * k, devices))  3.85 us
    ppermute x3, waiting for transfers between devices, local(): gathered.append(lax.ppermute(pixels, 'grp', partners(step, groups)))  3.81 us
    ppermute x3, starting transfers between devices, local(): lax.ppermute(halves[k].astype(bf16), plane, partners(2 * k, devices))  3.55 us
  transfers between devices with their start and end apart: 16, of which 10 were waited for; matrix products, arithmetic and copies ran while one was open for 5% of the time, Pallas kernels for 0%

profile of v4, /device:TPU:0, one launch (start us, length us, event | category | flops | bytes accessed | tf_op | source)
XLA Modules:
  0.0 69.8 jit_solution(5468862402193013566)
XLA Ops:
  0.6 0.9 %constant_dynamic-slice_fusion.2 = bf16[12,3,16,128]{3,2,1,0:T(8,128)(2,1)S(1)} fusion(bf16[12,8,16,128]{3,2,1,0:T(8,128)(2,1)} %bitcast.28, s32[]{:T(128)S(6)} %mul.21), kind=kLoop, calls=%fused_computation.16 | loop fusion | bytes 294916 | tf_op jit(solution)/shard_map/dynamic_slice | solution.py:673
  1.6 3.0 %collective-permute-start.2 = (bf16[12,3,16,128]{3,2,1,0:T(8,128)(2,1)S(1)}, bf16[12,3,16,128]{3,2,1,0:T(8,128)(2,1)S(1)}, u32[]{:S(2)}, u32[]{:S(2)}) collective-permute-start(bf16[12,3,16,128]{3,2,1,0:T(8,128)(2,1)S(1)} %constant_dynamic-slice_fusion.2), channel_id=1, source_target_pairs={{0,4},{1,5},{2,6},{3,7},{4,0},{5,1},{6,2},{7,3},{8,12},{9,13},{10,... | collective-permute-start | bytes 442376 | tf_op jit(solution)/shard_map/ppermute | solution.py:721
  4.6 1.3 %dynamic-slice_bitcast_fusion = (bf16[12,3,8,128]{3,1,2,0:T(4,128)(2,1)S(1)}, bf16[12,3,8,128]{3,1,2,0:T(4,128)(2,1)S(1)}) fusion(bf16[12,8,16,128]{3,2,1,0:T(8,128)(2,1)} %bitcast.29, s32[]{:T(128)S(6)} %mul.20, s32[]{:T(128)S(6)} %mul.19), kind=kLoop, calls=%fused_computation.6 | loop fusion | bytes 294920 | tf_op jit(solution)/shard_map/transpose | solution.py:690
  6.6 2.9 %collective-permute-start = (bf16[12,3,8,128]{3,1,2,0:T(4,128)(2,1)S(1)}, bf16[12,3,8,128]{3,1,2,0:T(4,128)(2,1)S(1)}, u32[]{:S(2)}, u32[]{:S(2)}) collective-permute-start(bf16[12,3,8,128]{3,1,2,0:T(4,128)(2,1)S(1)} %get-tuple-element.22), channel_id=1, source_target_pairs={{0,1},{1,0},{2,3},{3,2},{4,5},{5,4},{6,7},{7,6},{8,9},{9,8},{10,11... | collective-permute-start | bytes 221192 | tf_op jit(solution)/shard_map/ppermute | solution.py:721
  9.5 1.0 %constant_dynamic-slice_fusion = (bf16[12,3,3,128]{3,2,1,0:T(4,128)(2,1)S(1)}, bf16[12,3,3,128]{3,2,1,0:T(4,128)(2,1)S(1)}) fusion(bf16[12,8,16,128]{3,2,1,0:T(8,128)(2,1)} %bitcast.30, s32[]{:T(128)S(6)} %mul.22, s32[]{:T(128)S(6)} %mul.24, s32[]{:T(128)S(6)} %mul.23), kind=kLoop, calls=%fused_computation.14 | loop fusion | bytes 110604 | tf_op jit(solution)/shard_map/dynamic_slice | solution.py:673
  11.5 1.3 %copy.13 = bf16[8,16,12,128]{3,2,1,0:T(8,128)(2,1)S(1)} copy(bf16[8,16,12,128]{3,1,0,2:T(8,128)(2,1)} %bitcast.31) | data formatting | bytes 786432
  13.0 1.0 %collective-permute-done.3.refs_3_ = bf16[108,128]{1,0:T(8,128)(2,1)S(1)} collective-permute-done((bf16[108,128]{1,0:T(8,128)(2,1)S(1)}, bf16[108,128]{1,0:T(8,128)(2,1)S(1)}, u32[]{:S(2)}, u32[]{:S(2)}) %collective-permute-start.3) | collective-permute-done | bytes 27680 | tf_op jit(solution)/shard_map/ppermute | solution.py:721
  14.0 12.1 %shard_map.95 = (bf16[10,18,16,128]{3,2,1,0:T(8,128)(2,1)}, bf16[10,18,16,128]{3,2,1,0:T(8,128)(2,1)}, f32[8,256,128]{2,1,0:T(8,128)}, f32[10,288,128]{2,1,0:T(8,128)}, bf16[64,128]{1,0:T(8,128)(2,1)S(1)}) custom-call(bf16[8,16,16,128]{3,2,1,0:T(8,128)(2,1)S(1)} %pad.4.clone.own, bf16[12,3,8,128]{3,2,1,0:T(8,128)(2,1)S(1)} %copy.11.refs_0_, ...), custom_call_target="tpu_custom_call" | custom-call | flops 8589934592 | bytes 1048576 | tf_op jit(solution)/shard_map/pallas_call | solution.py:731
  26.1 3.5 %collective-permute-start.5 = (bf16[64,128]{1,0:T(8,128)(2,1)S(1)}, bf16[64,128]{1,0:T(8,128)(2,1)S(1)}, u32[]{:S(2)}, u32[]{:S(2)}) collective-permute-start(bf16[64,128]{1,0:T(8,128)(2,1)S(1)} %get-tuple-element.9), channel_id=1, source_target_pairs={{0,1},{1,0},{2,3},{3,2},{4,5},{5,4},{6,7},{7,6},{8,9},{9,8},{10,11... | collective-permute-start | bytes 49160 | tf_op jit(solution)/shard_map/ppermute | solution.py:762
  29.6 0.8 %collective-permute-done.5 = bf16[64,128]{1,0:T(8,128)(2,1)S(1)} collective-permute-done((bf16[64,128]{1,0:T(8,128)(2,1)S(1)}, bf16[64,128]{1,0:T(8,128)(2,1)S(1)}, u32[]{:S(2)}, u32[]{:S(2)}) %collective-permute-start.5) | collective-permute-done | bytes 16416 | tf_op jit(solution)/shard_map/ppermute | solution.py:762
  30.4 1.2 %collective-permute-start.8 = (bf16[2,64,128]{2,1,0:T(8,128)(2,1)S(1)}, bf16[2,64,128]{2,1,0:T(8,128)(2,1)S(1)}, u32[]{:S(2)}, u32[]{:S(2)}) collective-permute-start(bf16[2,64,128]{2,1,0:T(8,128)(2,1)S(1)} %pad_maximum_fusion.refs_0_), channel_id=1, source_target_pairs={{0,6},{1,7},{2,4},{3,5},{4,2},{5,3},{6,0},{7,1},{8,14},{9,15},{10,... | collective-permute-start | bytes 98312 | tf_op jit(solution)/shard_map/ppermute | solution.py:765
  32.2 1.8 %collective-permute-start.6 = (bf16[2,64,128]{2,1,0:T(8,128)(2,1)S(1)}, bf16[2,64,128]{2,1,0:T(8,128)(2,1)S(1)}, u32[]{:S(2)}, u32[]{:S(2)}) collective-permute-start(bf16[2,64,128]{2,1,0:T(8,128)(2,1)S(1)} %pad_maximum_fusion.refs_0_), channel_id=1, source_target_pairs={{0,2},{1,3},{2,0},{3,1},{4,6},{5,7},{6,4},{7,5},{8,10},{9,11},{10,... | collective-permute-start | bytes 98312 | tf_op jit(solution)/shard_map/ppermute | solution.py:765
  33.9 1.4 %collective-permute-done.8.refs_3_ = bf16[2,64,128]{2,1,0:T(8,128)(2,1)S(1)} collective-permute-done((bf16[2,64,128]{2,1,0:T(8,128)(2,1)S(1)}, bf16[2,64,128]{2,1,0:T(8,128)(2,1)S(1)}, u32[]{:S(2)}, u32[]{:S(2)}) %collective-permute-start.8) | collective-permute-done | bytes 32800 | tf_op jit(solution)/shard_map/ppermute | solution.py:765
  36.1 6.6 %shard_map.96.refs_0_ = bf16[3,8,144]{2,1,0:T(8,128)(2,1)S(1)} custom-call(bf16[2,64,128]{2,1,0:T(8,128)(2,1)S(1)} %pad_maximum_fusion.refs_0_, bf16[2,64,128]{2,1,0:T(8,128)(2,1)S(1)} %collective-permute-done.6.refs_1_, bf16[2,64,128]{2,1,0:T(8,128)(2,1)S(1)} %collective-permute-done.7.refs_2_, bf16[2,64,128]{2,1,0:T(8,128)(2,1)S(1)} %collective-permute-done.8.refs_3_, ...), custom_call_target="tpu_custom_call" | custom-call | flops 4294967296 | bytes 1048576 | tf_op jit(solution)/shard_map/pallas_call | solution.py:780
  42.7 3.6 %collective-permute-start.11 = (bf16[3,8,144]{2,1,0:T(8,128)(2,1)S(1)}, bf16[3,8,144]{2,1,0:T(8,128)(2,1)S(1)}, u32[]{:S(2)}, u32[]{:S(2)}) collective-permute-start(bf16[3,8,144]{2,1,0:T(8,128)(2,1)S(1)} %shard_map.96.refs_0_), channel_id=1, source_target_pairs={{0,24},{8,16},{16,8},{24,0},{1,25},{9,17},{17,9},{25,1},{2,26},{10... | collective-permute-start | bytes 20744 | tf_op jit(solution)/shard_map/ppermute | solution.py:825
  46.4 0.8 %collective-permute-start.9 = (bf16[3,8,144]{2,1,0:T(8,128)(2,1)S(1)}, bf16[3,8,144]{2,1,0:T(8,128)(2,1)S(1)}, u32[]{:S(2)}, u32[]{:S(2)}) collective-permute-start(bf16[3,8,144]{2,1,0:T(8,128)(2,1)S(1)} %shard_map.96.refs_0_), channel_id=1, source_target_pairs={{0,8},{8,0},{16,24},{24,16},{1,9},{9,1},{17,25},{25,17},{2,10},{10... | collective-permute-start | bytes 20744 | tf_op jit(solution)/shard_map/ppermute | solution.py:825
  47.2 1.2 %collective-permute-done.11.refs_3_ = bf16[3,8,144]{2,1,0:T(8,128)(2,1)S(1)} collective-permute-done((bf16[3,8,144]{2,1,0:T(8,128)(2,1)S(1)}, bf16[3,8,144]{2,1,0:T(8,128)(2,1)S(1)}, u32[]{:S(2)}, u32[]{:S(2)}) %collective-permute-start.11) | collective-permute-done | bytes 6944 | tf_op jit(solution)/shard_map/ppermute | solution.py:825
  48.3 2.6 %collective-permute-done.10.refs_2_ = bf16[3,8,144]{2,1,0:T(8,128)(2,1)S(1)} collective-permute-done((bf16[3,8,144]{2,1,0:T(8,128)(2,1)S(1)}, bf16[3,8,144]{2,1,0:T(8,128)(2,1)S(1)}, u32[]{:S(2)}, u32[]{:S(2)}) %collective-permute-start.10) | collective-permute-done | bytes 6944 | tf_op jit(solution)/shard_map/ppermute | solution.py:825
  51.0 9.1 %shard_map.97 = (bf16[4,2,108,128]{3,2,1,0:T(8,128)(2,1)S(1)}, bf16[4,2,108,128]{3,2,1,0:T(8,128)(2,1)S(1)}) custom-call(bf16[3,8,144]{2,1,0:T(8,128)(2,1)S(1)} %shard_map.96.refs_0_, bf16[3,8,144]{2,1,0:T(8,128)(2,1)S(1)} %collective-permute-done.9.refs_1_, bf16[3,8,144]{2,1,0:T(8,128)(2,1)S(1)} %collective-permute-done.10.refs_2_, ...), custom_call_target="tpu_custom_call" | custom-call | flops 4294967296 | bytes 1048576 | tf_op jit(solution)/shard_map/pallas_call | solution.py:838
  60.2 1.5 %collective-permute-done.12 = bf16[4,2,108,128]{3,2,1,0:T(8,128)(2,1)S(1)} collective-permute-done((bf16[4,2,108,128]{3,2,1,0:T(8,128)(2,1)S(1)}, bf16[4,2,108,128]{3,2,1,0:T(8,128)(2,1)S(1)}, u32[]{:S(2)}, u32[]{:S(2)}) %collective-permute-start.12) | collective-permute-done | bytes 221216 | tf_op jit(solution)/shard_map/ppermute | solution.py:871
  61.7 1.8 %collective-permute-start.13 = (bf16[2,108,128]{2,1,0:T(8,128)(2,1)S(1)}, bf16[2,108,128]{2,1,0:T(8,128)(2,1)S(1)}, u32[]{:S(2)}, u32[]{:S(2)}) collective-permute-start(bf16[2,108,128]{2,1,0:T(8,128)(2,1)S(1)} %get-tuple-element.16), channel_id=1, source_target_pairs={{0,2},{1,3},{2,0},{3,1},{4,6},{5,7},{6,4},{7,5},{8,10},{9,11},{10,... | collective-permute-start | bytes 165896 | tf_op jit(solution)/shard_map/ppermute | solution.py:875
  63.5 1.2 %collective-permute-start.15 = (bf16[2,108,128]{2,1,0:T(8,128)(2,1)S(1)}, bf16[2,108,128]{2,1,0:T(8,128)(2,1)S(1)}, u32[]{:S(2)}, u32[]{:S(2)}) collective-permute-start(bf16[2,108,128]{2,1,0:T(8,128)(2,1)S(1)} %get-tuple-element.17), channel_id=1, source_target_pairs={{0,6},{1,7},{2,4},{3,5},{4,2},{5,3},{6,0},{7,1},{8,14},{9,15},{10,... | collective-permute-start | bytes 165896 | tf_op jit(solution)/shard_map/ppermute | solution.py:875
  65.3 0.7 collective-permute-done.13
  66.0 3.2 %collective-permute-done.15 = bf16[2,108,128]{2,1,0:T(8,128)(2,1)S(1)} collective-permute-done((bf16[2,108,128]{2,1,0:T(8,128)(2,1)S(1)}, bf16[2,108,128]{2,1,0:T(8,128)(2,1)S(1)}, u32[]{:S(2)}, u32[]{:S(2)}) %collective-permute-start.15) | collective-permute-done | bytes 55328 | tf_op jit(solution)/shard_map/ppermute | solution.py:875
  (46 shorter events, 4.5 us)
Async XLA Ops:
  1.6 12.4 %collective-permute-start.2 = (bf16[12,3,16,128]{3,2,1,0:T(8,128)(2,1)S(1)}, bf16[12,3,16,128]{3,2,1,0:T(8,128)(2,1)S(1)}, u32[]{:S(2)}, u32[]{:S(2)}) collective-permute-start(bf16[12,3,16,128]{3,2,1,0:T(8,128)(2,1)S(1)} %constant_dynamic-slice_fusion.2), channel_id=1, source_target_pairs={{0,4},{1,5},{2,6},{3,7},{4,0},{5,1},{6,2},{7,3},{8,12},{9,13},{10,... | collective-permute-start | bytes 442376 | tf_op jit(solution)/shard_map/ppermute | solution.py:721
  4.6 9.4 %copy-start.6 = (bf16[3,128]{1,0:T(4,128)(2,1)S(1)}, bf16[3,128]{1,0:T(4,128)(2,1)}, u32[]{:S(2)}) copy-start(bf16[3,128]{1,0:T(4,128)(2,1)} %refs_4_.3) | copy-start | bytes 2308
  5.9 7.0 %collective-permute-start.1 = (bf16[12,3,8,128]{3,1,2,0:T(4,128)(2,1)S(1)}, bf16[12,3,8,128]{3,1,2,0:T(4,128)(2,1)S(1)}, u32[]{:S(2)}, u32[]{:S(2)}) collective-permute-start(bf16[12,3,8,128]{3,1,2,0:T(4,128)(2,1)S(1)} %get-tuple-element.21), channel_id=1, source_target_pairs={{1,2},{2,1},{5,6},{6,5},{9,10},{10,9},{13,14},{14,13},{17,18},{18,... | collective-permute-start | bytes 221192 | tf_op jit(solution)/shard_map/ppermute | solution.py:721
  6.6 6.4 %collective-permute-start = (bf16[12,3,8,128]{3,1,2,0:T(4,128)(2,1)S(1)}, bf16[12,3,8,128]{3,1,2,0:T(4,128)(2,1)S(1)}, u32[]{:S(2)}, u32[]{:S(2)}) collective-permute-start(bf16[12,3,8,128]{3,1,2,0:T(4,128)(2,1)S(1)} %get-tuple-element.22), channel_id=1, source_target_pairs={{0,1},{1,0},{2,3},{3,2},{4,5},{5,4},{6,7},{7,6},{8,9},{9,8},{10,11... | collective-permute-start | bytes 221192 | tf_op jit(solution)/shard_map/ppermute | solution.py:721
  10.6 3.4 %collective-permute-start.3 = (bf16[108,128]{1,0:T(8,128)(2,1)S(1)}, bf16[108,128]{1,0:T(8,128)(2,1)S(1)}, u32[]{:S(2)}, u32[]{:S(2)}) collective-permute-start(bf16[108,128]{1,0:T(8,128)(2,1)S(1)} %reshape.29), channel_id=1, source_target_pairs={{0,5},{1,4},{2,7},{3,6},{4,1},{5,0},{6,3},{7,2},{8,13},{9,12},{10,... | collective-permute-start | bytes 82952 | tf_op jit(solution)/shard_map/ppermute | solution.py:721
  10.9 3.1 %collective-permute-start.4 = (bf16[108,128]{1,0:T(8,128)(2,1)S(1)}, bf16[108,128]{1,0:T(8,128)(2,1)S(1)}, u32[]{:S(2)}, u32[]{:S(2)}) collective-permute-start(bf16[108,128]{1,0:T(8,128)(2,1)S(1)} %reshape.30), channel_id=1, source_target_pairs={{1,6},{2,5},{5,2},{6,1},{9,14},{10,13},{13,10},{14,9},{17,22},{18,... | collective-permute-start | bytes 82952 | tf_op jit(solution)/shard_map/ppermute | solution.py:721
  13.0 23.1 %copy-start.2 = (bf16[576,128]{1,0:T(8,128)(2,1)S(1)}, bf16[576,128]{1,0:T(8,128)(2,1)}, u32[]{:S(2)}) copy-start(bf16[576,128]{1,0:T(8,128)(2,1)} %refs_6_.3) | copy-start | bytes 442372
  13.0 23.1 %copy-start.3 = (bf16[576,64]{0,1:T(8,128)(2,1)S(1)}, bf16[576,64]{0,1:T(8,128)(2,1)}, u32[]{:S(2)}) copy-start(bf16[576,64]{0,1:T(8,128)(2,1)} %param.14) | copy-start | bytes 221188
  13.0 23.1 %copy-start.5 = (bf16[27,64]{1,0:T(8,128)(2,1)S(1)}, bf16[27,64]{1,0:T(8,128)(2,1)}, u32[]{:S(2)}) copy-start(bf16[27,64]{1,0:T(8,128)(2,1)} %refs_4_.2) | copy-start | bytes 10372
  26.1 4.3 %collective-permute-start.5 = (bf16[64,128]{1,0:T(8,128)(2,1)S(1)}, bf16[64,128]{1,0:T(8,128)(2,1)S(1)}, u32[]{:S(2)}, u32[]{:S(2)}) collective-permute-start(bf16[64,128]{1,0:T(8,128)(2,1)S(1)} %get-tuple-element.9), channel_id=1, source_target_pairs={{0,1},{1,0},{2,3},{3,2},{4,5},{5,4},{6,7},{7,6},{8,9},{9,8},{10,11... | collective-permute-start | bytes 49160 | tf_op jit(solution)/shard_map/ppermute | solution.py:762
  30.4 4.9 %collective-permute-start.8 = (bf16[2,64,128]{2,1,0:T(8,128)(2,1)S(1)}, bf16[2,64,128]{2,1,0:T(8,128)(2,1)S(1)}, u32[]{:S(2)}, u32[]{:S(2)}) collective-permute-start(bf16[2,64,128]{2,1,0:T(8,128)(2,1)S(1)} %pad_maximum_fusion.refs_0_), channel_id=1, source_target_pairs={{0,6},{1,7},{2,4},{3,5},{4,2},{5,3},{6,0},{7,1},{8,14},{9,15},{10,... | collective-permute-start | bytes 98312 | tf_op jit(solution)/shard_map/ppermute | solution.py:765
  31.6 3.9 %collective-permute-start.7 = (bf16[2,64,128]{2,1,0:T(8,128)(2,1)S(1)}, bf16[2,64,128]{2,1,0:T(8,128)(2,1)S(1)}, u32[]{:S(2)}, u32[]{:S(2)}) collective-permute-start(bf16[2,64,128]{2,1,0:T(8,128)(2,1)S(1)} %pad_maximum_fusion.refs_0_), channel_id=1, source_target_pairs={{0,4},{1,5},{2,6},{3,7},{4,0},{5,1},{6,2},{7,3},{8,12},{9,13},{10,... | collective-permute-start | bytes 98312 | tf_op jit(solution)/shard_map/ppermute | solution.py:765
  32.2 3.9 %collective-permute-start.6 = (bf16[2,64,128]{2,1,0:T(8,128)(2,1)S(1)}, bf16[2,64,128]{2,1,0:T(8,128)(2,1)S(1)}, u32[]{:S(2)}, u32[]{:S(2)}) collective-permute-start(bf16[2,64,128]{2,1,0:T(8,128)(2,1)S(1)} %pad_maximum_fusion.refs_0_), channel_id=1, source_target_pairs={{0,2},{1,3},{2,0},{3,1},{4,6},{5,7},{6,4},{7,5},{8,10},{9,11},{10,... | collective-permute-start | bytes 98312 | tf_op jit(solution)/shard_map/ppermute | solution.py:765
  36.1 14.9 %copy-start.7 = (f32[10,288,128]{2,1,0:T(8,128)S(1)}, f32[10,288,128]{2,1,0:T(8,128)}, u32[]{:S(2)}) copy-start(f32[10,288,128]{2,1,0:T(8,128)} %get-tuple-element.11.refs_7_) | copy-start | bytes 4423684
  36.1 14.9 %copy-start.8 = (f32[8,256,128]{2,1,0:T(8,128)S(1)}, f32[8,256,128]{2,1,0:T(8,128)}, u32[]{:S(2)}) copy-start(f32[8,256,128]{2,1,0:T(8,128)} %get-tuple-element.10.refs_6_) | copy-start | bytes 3145732
  36.1 14.8 %copy-start.9 = (bf16[10,18,16,128]{3,2,1,0:T(8,128)(2,1)S(1)}, bf16[10,18,16,128]{3,2,1,0:T(8,128)(2,1)}, u32[]{:S(2)}) copy-start(bf16[10,18,16,128]{3,2,1,0:T(8,128)(2,1)} %get-tuple-element.12.refs_8_) | copy-start | bytes 2211844
  36.1 14.8 %copy-start.10 = (bf16[10,18,16,128]{3,2,1,0:T(8,128)(2,1)S(1)}, bf16[10,18,16,128]{3,2,1,0:T(8,128)(2,1)}, u32[]{:S(2)}) copy-start(bf16[10,18,16,128]{3,2,1,0:T(8,128)(2,1)} %get-tuple-element.13.refs_9_) | copy-start | bytes 2211844
  42.7 5.6 %collective-permute-start.11 = (bf16[3,8,144]{2,1,0:T(8,128)(2,1)S(1)}, bf16[3,8,144]{2,1,0:T(8,128)(2,1)S(1)}, u32[]{:S(2)}, u32[]{:S(2)}) collective-permute-start(bf16[3,8,144]{2,1,0:T(8,128)(2,1)S(1)} %shard_map.96.refs_0_), channel_id=1, source_target_pairs={{0,24},{8,16},{16,8},{24,0},{1,25},{9,17},{17,9},{25,1},{2,26},{10... | collective-permute-start | bytes 20744 | tf_op jit(solution)/shard_map/ppermute | solution.py:825
  46.4 4.6 %collective-permute-start.10 = (bf16[3,8,144]{2,1,0:T(8,128)(2,1)S(1)}, bf16[3,8,144]{2,1,0:T(8,128)(2,1)S(1)}, u32[]{:S(2)}, u32[]{:S(2)}) collective-permute-start(bf16[3,8,144]{2,1,0:T(8,128)(2,1)S(1)} %shard_map.96.refs_0_), channel_id=1, source_target_pairs={{0,16},{8,24},{16,0},{24,8},{1,17},{9,25},{17,1},{25,9},{2,18},{10... | collective-permute-start | bytes 20744 | tf_op jit(solution)/shard_map/ppermute | solution.py:825
  46.4 4.6 %collective-permute-start.9 = (bf16[3,8,144]{2,1,0:T(8,128)(2,1)S(1)}, bf16[3,8,144]{2,1,0:T(8,128)(2,1)S(1)}, u32[]{:S(2)}, u32[]{:S(2)}) collective-permute-start(bf16[3,8,144]{2,1,0:T(8,128)(2,1)S(1)} %shard_map.96.refs_0_), channel_id=1, source_target_pairs={{0,8},{8,0},{16,24},{24,16},{1,9},{9,1},{17,25},{25,17},{2,10},{10... | collective-permute-start | bytes 20744 | tf_op jit(solution)/shard_map/ppermute | solution.py:825
  60.1 1.6 %collective-permute-start.12 = (bf16[4,2,108,128]{3,2,1,0:T(8,128)(2,1)S(1)}, bf16[4,2,108,128]{3,2,1,0:T(8,128)(2,1)S(1)}, u32[]{:S(2)}, u32[]{:S(2)}) collective-permute-start(bf16[4,2,108,128]{3,2,1,0:T(8,128)(2,1)S(1)} %get-tuple-element.15), channel_id=1, source_target_pairs={{0,1},{1,0},{2,3},{3,2},{4,5},{5,4},{6,7},{7,6},{8,9},{9,8},{10,11... | collective-permute-start | bytes 663560 | tf_op jit(solution)/shard_map/ppermute | solution.py:871
  61.7 4.2 %collective-permute-start.13 = (bf16[2,108,128]{2,1,0:T(8,128)(2,1)S(1)}, bf16[2,108,128]{2,1,0:T(8,128)(2,1)S(1)}, u32[]{:S(2)}, u32[]{:S(2)}) collective-permute-start(bf16[2,108,128]{2,1,0:T(8,128)(2,1)S(1)} %get-tuple-element.16), channel_id=1, source_target_pairs={{0,2},{1,3},{2,0},{3,1},{4,6},{5,7},{6,4},{7,5},{8,10},{9,11},{10,... | collective-permute-start | bytes 165896 | tf_op jit(solution)/shard_map/ppermute | solution.py:875
  63.5 5.6 %collective-permute-start.15 = (bf16[2,108,128]{2,1,0:T(8,128)(2,1)S(1)}, bf16[2,108,128]{2,1,0:T(8,128)(2,1)S(1)}, u32[]{:S(2)}, u32[]{:S(2)}) collective-permute-start(bf16[2,108,128]{2,1,0:T(8,128)(2,1)S(1)} %get-tuple-element.17), channel_id=1, source_target_pairs={{0,6},{1,7},{2,4},{3,5},{4,2},{5,3},{6,0},{7,1},{8,14},{9,15},{10,... | collective-permute-start | bytes 165896 | tf_op jit(solution)/shard_map/ppermute | solution.py:875
  64.8 4.4 %collective-permute-start.14 = (bf16[2,108,128]{2,1,0:T(8,128)(2,1)S(1)}, bf16[2,108,128]{2,1,0:T(8,128)(2,1)S(1)}, u32[]{:S(2)}, u32[]{:S(2)}) collective-permute-start(bf16[2,108,128]{2,1,0:T(8,128)(2,1)S(1)} %get-tuple-element.18), channel_id=1, source_target_pairs={{0,4},{1,5},{2,6},{3,7},{4,0},{5,1},{6,2},{7,3},{8,12},{9,13},{10,... | collective-permute-start | bytes 165896 | tf_op jit(solution)/shard_map/ppermute | solution.py:875
  (3 other events, 28.1 us)

commit v5 on v4

--- a/solution.py
+++ b/solution.py
@@ -82,9 +82,8 @@
     (
         first, second, rgb, target, cells_out, hidden_out, first_out, second_out, payload,
         cells, hidden, slope_first, slope_second, spread_weight, picked, spaced, colour, project,
-        unpacked, corner_rows, sems,
+        sems,
     ) = refs[len(places) :]
-    unpacked[...] = jnp.zeros(unpacked.shape, jnp.float32)
     rows, cols, slots, channels = own.shape
     f32, bf16 = jnp.float32, jnp.bfloat16
     groups, group = lax.axis_size("grp"), lax.axis_index("grp")
@@ -103,30 +102,7 @@
             row = jnp.where(lax.axis_index("row") % 2 == row_at, 3 + rows, 0)
         if col_at is not None:
             col = jnp.where(lax.axis_index("col") % 2 == col_at, 3 + cols, 0)
-        if row_at is None:
-            for f in range(frames):
-                for c in range(3):
-                    unpacked[pl.ds(c * rows * slots + f, rows, stride=slots)] = piece[f, c].astype(
-                        f32
-                    )
-            for c in range(3):
-                line = unpacked[c * rows * slots : (c + 1) * rows * slots].astype(bf16)
-                cells[3 : 3 + rows, col + c] = line.reshape(rows, slots, channels)
-        elif col_at is None:
-            for f in range(frames):
-                for r in range(3):
-                    unpacked[pl.ds(r * cols * slots + f, cols, stride=slots)] = piece[f, r].astype(
-                        f32
-                    )
-            for r in range(3):
-                line = unpacked[r * cols * slots : (r + 1) * cols * slots].astype(bf16)
-                cells[row + r, 3 : 3 + cols] = line.reshape(cols, slots, channels)
-        else:
-            corner_rows[...] = piece[...].astype(f32)
-            for r in range(3):
-                for c in range(3):
-                    unpacked[0:frames] = corner_rows[pl.ds(r * 3 + c, frames, stride=9)]
-                    cells[row + r, col + c] = unpacked[0:slots].astype(bf16)
+        cells[pl.ds(row, piece.shape[0]), pl.ds(col, piece.shape[1])] = piece[...]
     copies = [
         pltpu.make_async_copy(
             cells.at[pl.ds(2, rows + 2), pl.ds(2, cols + 2)], cells_out, sems.at[0]
@@ -684,15 +660,6 @@
     return pieces
 
 
-def packed_edge(place, edge):
-    row_at, col_at = place
-    if row_at is None:
-        return jnp.swapaxes(edge, 1, 2)
-    if col_at is None:
-        return edge
-    return edge.reshape(-1, edge.shape[3])
-
-
 def slotted(field, slots):
     field = jnp.transpose(field, (1, 2, 0, 3))
     return jnp.pad(field, ((0, 0), (0, 0), (0, slots - field.shape[2]), (0, 0)))
@@ -717,9 +684,7 @@
     raw = dec_input.reshape(frames, rows, cols, channels)
     pieces = exchange_pieces(raw, 3)
     places = tuple(place for place, _, _ in pieces)
-    near = [
-        lax.ppermute(packed_edge(place, edge), plane, moves) for place, edge, moves in pieces
-    ]
+    near = [lax.ppermute(slotted(edge, slots), plane, moves) for _, edge, moves in pieces]
     own = slotted(raw, slots)
 
     line = max(cols * half, -(-width // 128) * 128)
@@ -747,8 +712,6 @@
             ((rows + 2, cols * half, channels), f32),
             (((rows + 2) * 8, cols * half), f32),
             ((8, channels), f32),
-            ((3 * max(rows, cols) * slots, channels), f32),
-            ((9 * frames, channels), f32),
         ],
         4,
         big,

time: 70.1 us -> 66.9 us (0.954)
  local copies, waits for them, and re-layouts: 5.36 us -> 2.24 us
  starting transfers between devices: 22.6 us -> 23.5 us
    dynamic_slice x2 -> x0, local copies, waits for them, and re-layouts: 1.94 us -> none  [exchange_pieces(): lax.dynamic_slice_in_dim(edge, after * (length - width), width, axis=dim)]
    unnamed x23 -> x22, local copies, waits for them, and re-layouts: 1.32 us -> 0.06 us
    reshape x2 -> x1, local copies, waits for them, and re-layouts: 0.06 us -> 1.27 us  [local(): raw = dec_input.reshape(frames, rows, cols, channels)]
    transpose x1 -> x3, local copies, waits for them, and re-layouts: 1.26 us -> 0.06 us  [slotted(): field = jnp.transpose(field, (1, 2, 0, 3))]
    ppermute x1, starting transfers between devices: 3.47 us -> 4.47 us  [local(): other = lax.ppermute(payload, plane, [(i, i ^ 1) for i in range(devices)])]
    ppermute x3, waiting for transfers between devices: 3.85 us -> 2.88 us  [local(): lax.ppermute(halves[k].astype(bf16), plane, partners(2 * k, devices))]
  transfers between devices with their start and end apart: 16 -> 16, of which waited for: 10 -> 9; matrix products, arithmetic and copies ran while one was open for 5% -> 0% of each run, Pallas kernels for 0% -> 0%
where the time goes in v5:
time: 66.9 us; the launch traced here: 66.7 us
  Pallas kernels  27.4 us (41%)
  starting transfers between devices  23.5 us (35%)
  waiting for transfers between devices  12.5 us (19%)
  local copies, waits for them, and re-layouts  2.24 us (3%)
  between operations  0.96 us (1%)
    pallas_call x1, Pallas kernels, local(): call(functools.partial(forward_kernel, frames, parts, pack, places), (plt...  11.7 us
    pallas_call x1, Pallas kernels, local(): call(functools.partial(backward_kernel, parts=parts, out_rows=out_rows, g...  9.13 us
    ppermute x5, starting transfers between devices, local(): lax.ppermute(slotted(edge, slots), plane, moves)  7.51 us
    pallas_call x1, Pallas kernels, local(): call(functools.partial(perceptual_kernel, (rows, cols, blocks, block_fram...  6.58 us
    ppermute x1, starting transfers between devices, local(): other = lax.ppermute(payload, plane, [(i, i ^ 1) for i in range(devices)])  4.47 us
    ppermute x3, starting transfers between devices, local(): gathered.append(lax.ppermute(pixels, 'grp', partners(step, groups)))  4.42 us
    ppermute x3, waiting for transfers between devices, local(): gathered.append(lax.ppermute(pixels, 'grp', partners(step, groups)))  3.8 us
    ppermute x3, starting transfers between devices, local(): lax.ppermute(halves[k].astype(bf16), plane, partners(2 * k, devices))  3.55 us
  transfers between devices with their start and end apart: 16, of which 9 were waited for; matrix products, arithmetic and copies ran while one was open for 0% of the time, Pallas kernels for 0%

profile of v5, /device:TPU:0, one launch (start us, length us, event | category | flops | bytes accessed | tf_op | source)
XLA Modules:
  0.0 66.7 jit_solution(13090325235127231924)
XLA Ops:
  0.6 1.3 %copy.19 = bf16[12,8,16,128]{3,0,2,1:T(8,128)(2,1)S(1)} copy(bf16[12,8,16,128]{3,2,1,0:T(8,128)(2,1)} %bitcast.35) | data formatting | bytes 786432 | tf_op jit(solution)/shard_map/reshape | solution.py:684
  2.0 3.0 %collective-permute-start.2 = (bf16[3,16,16,128]{3,2,1,0:T(8,128)(2,1)S(1)}, bf16[3,16,16,128]{3,2,1,0:T(8,128)(2,1)S(1)}, u32[]{:S(2)}, u32[]{:S(2)}) collective-permute-start(bf16[3,16,16,128]{3,2,1,0:T(8,128)(2,1)S(1)} %pad.25), channel_id=1, source_target_pairs={{0,4},{1,5},{2,6},{3,7},{4,0},{5,1},{6,2},{7,3},{8,12},{9,13},{10,... | collective-permute-start | bytes 589832 | tf_op jit(solution)/shard_map/ppermute | solution.py:687
  5.2 0.7 collective-permute-start.1
  6.0 3.1 %collective-permute-start.3 = (bf16[3,3,16,128]{3,2,1,0:T(8,128)(2,1)S(1)}, bf16[3,3,16,128]{3,2,1,0:T(8,128)(2,1)S(1)}, u32[]{:S(2)}, u32[]{:S(2)}) collective-permute-start(bf16[3,3,16,128]{3,2,1,0:T(8,128)(2,1)S(1)} %pad.26), channel_id=1, source_target_pairs={{0,5},{1,4},{2,7},{3,6},{4,1},{5,0},{6,3},{7,2},{8,13},{9,12},{10,... | collective-permute-start | bytes 110600 | tf_op jit(solution)/shard_map/ppermute | solution.py:687
  9.9 0.8 %collective-permute-done.3.refs_3_ = bf16[3,3,16,128]{3,2,1,0:T(8,128)(2,1)S(1)} collective-permute-done((bf16[3,3,16,128]{3,2,1,0:T(8,128)(2,1)S(1)}, bf16[3,3,16,128]{3,2,1,0:T(8,128)(2,1)S(1)}, u32[]{:S(2)}, u32[]{:S(2)}) %collective-permute-start.3) | collective-permute-done | bytes 36896 | tf_op jit(solution)/shard_map/ppermute | solution.py:687
  10.8 11.7 %shard_map.95 = (bf16[10,18,16,128]{3,2,1,0:T(8,128)(2,1)}, bf16[10,18,16,128]{3,2,1,0:T(8,128)(2,1)}, f32[8,256,128]{2,1,0:T(8,128)}, f32[10,288,128]{2,1,0:T(8,128)}, bf16[64,128]{1,0:T(8,128)(2,1)S(1)}) custom-call(bf16[8,16,16,128]{3,2,1,0:T(8,128)(2,1)S(1)} %pad.22.own, bf16[8,3,16,128]{3,2,1,0:T(8,128)(2,1)S(1)} %collective-permute-done.refs_0_, ...), custom_call_target="tpu_custom_call" | custom-call | flops 8589934592 | bytes 1048576 | tf_op jit(solution)/shard_map/pallas_call | solution.py:696
  22.5 4.5 %collective-permute-start.5 = (bf16[64,128]{1,0:T(8,128)(2,1)S(1)}, bf16[64,128]{1,0:T(8,128)(2,1)S(1)}, u32[]{:S(2)}, u32[]{:S(2)}) collective-permute-start(bf16[64,128]{1,0:T(8,128)(2,1)S(1)} %get-tuple-element.9), channel_id=1, source_target_pairs={{0,1},{1,0},{2,3},{3,2},{4,5},{5,4},{6,7},{7,6},{8,9},{9,8},{10,11... | collective-permute-start | bytes 49160 | tf_op jit(solution)/shard_map/ppermute | solution.py:725
  26.9 0.8 %collective-permute-done.5 = bf16[64,128]{1,0:T(8,128)(2,1)S(1)} collective-permute-done((bf16[64,128]{1,0:T(8,128)(2,1)S(1)}, bf16[64,128]{1,0:T(8,128)(2,1)S(1)}, u32[]{:S(2)}, u32[]{:S(2)}) %collective-permute-start.5) | collective-permute-done | bytes 16416 | tf_op jit(solution)/shard_map/ppermute | solution.py:725
  28.3 1.8 %collective-permute-start.7 = (bf16[2,64,128]{2,1,0:T(8,128)(2,1)S(1)}, bf16[2,64,128]{2,1,0:T(8,128)(2,1)S(1)}, u32[]{:S(2)}, u32[]{:S(2)}) collective-permute-start(bf16[2,64,128]{2,1,0:T(8,128)(2,1)S(1)} %pad_maximum_fusion.refs_0_), channel_id=1, source_target_pairs={{0,4},{1,5},{2,6},{3,7},{4,0},{5,1},{6,2},{7,3},{8,12},{9,13},{10,... | collective-permute-start | bytes 98312 | tf_op jit(solution)/shard_map/ppermute | solution.py:728
  30.1 1.2 %collective-permute-start.6 = (bf16[2,64,128]{2,1,0:T(8,128)(2,1)S(1)}, bf16[2,64,128]{2,1,0:T(8,128)(2,1)S(1)}, u32[]{:S(2)}, u32[]{:S(2)}) collective-permute-start(bf16[2,64,128]{2,1,0:T(8,128)(2,1)S(1)} %pad_maximum_fusion.refs_0_), channel_id=1, source_target_pairs={{0,2},{1,3},{2,0},{3,1},{4,6},{5,7},{6,4},{7,5},{8,10},{9,11},{10,... | collective-permute-start | bytes 98312 | tf_op jit(solution)/shard_map/ppermute | solution.py:728
  31.3 1.5 %collective-permute-done.8.refs_3_ = bf16[2,64,128]{2,1,0:T(8,128)(2,1)S(1)} collective-permute-done((bf16[2,64,128]{2,1,0:T(8,128)(2,1)S(1)}, bf16[2,64,128]{2,1,0:T(8,128)(2,1)S(1)}, u32[]{:S(2)}, u32[]{:S(2)}) %collective-permute-start.8) | collective-permute-done | bytes 32800 | tf_op jit(solution)/shard_map/ppermute | solution.py:728
  32.8 1.2 %collective-permute-done.6.refs_1_ = bf16[2,64,128]{2,1,0:T(8,128)(2,1)S(1)} collective-permute-done((bf16[2,64,128]{2,1,0:T(8,128)(2,1)S(1)}, bf16[2,64,128]{2,1,0:T(8,128)(2,1)S(1)}, u32[]{:S(2)}, u32[]{:S(2)}) %collective-permute-start.6) | collective-permute-done | bytes 32800 | tf_op jit(solution)/shard_map/ppermute | solution.py:728
  34.0 6.6 %shard_map.96.refs_0_ = bf16[3,8,144]{2,1,0:T(8,128)(2,1)S(1)} custom-call(bf16[2,64,128]{2,1,0:T(8,128)(2,1)S(1)} %pad_maximum_fusion.refs_0_, bf16[2,64,128]{2,1,0:T(8,128)(2,1)S(1)} %collective-permute-done.6.refs_1_, bf16[2,64,128]{2,1,0:T(8,128)(2,1)S(1)} %collective-permute-done.7.refs_2_, bf16[2,64,128]{2,1,0:T(8,128)(2,1)S(1)} %collective-permute-done.8.refs_3_, ...), custom_call_target="tpu_custom_call" | custom-call | flops 4294967296 | bytes 1048576 | tf_op jit(solution)/shard_map/pallas_call | solution.py:743
  40.6 3.6 %collective-permute-start.11 = (bf16[3,8,144]{2,1,0:T(8,128)(2,1)S(1)}, bf16[3,8,144]{2,1,0:T(8,128)(2,1)S(1)}, u32[]{:S(2)}, u32[]{:S(2)}) collective-permute-start(bf16[3,8,144]{2,1,0:T(8,128)(2,1)S(1)} %shard_map.96.refs_0_), channel_id=1, source_target_pairs={{0,24},{8,16},{16,8},{24,0},{1,25},{9,17},{17,9},{25,1},{2,26},{10... | collective-permute-start | bytes 20744 | tf_op jit(solution)/shard_map/ppermute | solution.py:788
  44.2 0.8 %collective-permute-start.9 = (bf16[3,8,144]{2,1,0:T(8,128)(2,1)S(1)}, bf16[3,8,144]{2,1,0:T(8,128)(2,1)S(1)}, u32[]{:S(2)}, u32[]{:S(2)}) collective-permute-start(bf16[3,8,144]{2,1,0:T(8,128)(2,1)S(1)} %shard_map.96.refs_0_), channel_id=1, source_target_pairs={{0,8},{8,0},{16,24},{24,16},{1,9},{9,1},{17,25},{25,17},{2,10},{10... | collective-permute-start | bytes 20744 | tf_op jit(solution)/shard_map/ppermute | solution.py:788
  45.0 1.1 %collective-permute-done.11.refs_3_ = bf16[3,8,144]{2,1,0:T(8,128)(2,1)S(1)} collective-permute-done((bf16[3,8,144]{2,1,0:T(8,128)(2,1)S(1)}, bf16[3,8,144]{2,1,0:T(8,128)(2,1)S(1)}, u32[]{:S(2)}, u32[]{:S(2)}) %collective-permute-start.11) | collective-permute-done | bytes 6944 | tf_op jit(solution)/shard_map/ppermute | solution.py:788
  46.1 2.7 %collective-permute-done.10.refs_2_ = bf16[3,8,144]{2,1,0:T(8,128)(2,1)S(1)} collective-permute-done((bf16[3,8,144]{2,1,0:T(8,128)(2,1)S(1)}, bf16[3,8,144]{2,1,0:T(8,128)(2,1)S(1)}, u32[]{:S(2)}, u32[]{:S(2)}) %collective-permute-start.10) | collective-permute-done | bytes 6944 | tf_op jit(solution)/shard_map/ppermute | solution.py:788
  48.9 9.1 %shard_map.97 = (bf16[4,2,108,128]{3,2,1,0:T(8,128)(2,1)S(1)}, bf16[4,2,108,128]{3,2,1,0:T(8,128)(2,1)S(1)}) custom-call(bf16[3,8,144]{2,1,0:T(8,128)(2,1)S(1)} %shard_map.96.refs_0_, bf16[3,8,144]{2,1,0:T(8,128)(2,1)S(1)} %collective-permute-done.9.refs_1_, bf16[3,8,144]{2,1,0:T(8,128)(2,1)S(1)} %collective-permute-done.10.refs_2_, ...), custom_call_target="tpu_custom_call" | custom-call | flops 4294967296 | bytes 1048576 | tf_op jit(solution)/shard_map/pallas_call | solution.py:801
  58.1 1.5 %collective-permute-done.12 = bf16[4,2,108,128]{3,2,1,0:T(8,128)(2,1)S(1)} collective-permute-done((bf16[4,2,108,128]{3,2,1,0:T(8,128)(2,1)S(1)}, bf16[4,2,108,128]{3,2,1,0:T(8,128)(2,1)S(1)}, u32[]{:S(2)}, u32[]{:S(2)}) %collective-permute-start.12) | collective-permute-done | bytes 221216 | tf_op jit(solution)/shard_map/ppermute | solution.py:834
  59.6 1.2 %collective-permute-start.13 = (bf16[2,108,128]{2,1,0:T(8,128)(2,1)S(1)}, bf16[2,108,128]{2,1,0:T(8,128)(2,1)S(1)}, u32[]{:S(2)}, u32[]{:S(2)}) collective-permute-start(bf16[2,108,128]{2,1,0:T(8,128)(2,1)S(1)} %get-tuple-element.20), channel_id=1, source_target_pairs={{0,2},{1,3},{2,0},{3,1},{4,6},{5,7},{6,4},{7,5},{8,10},{9,11},{10,... | collective-permute-start | bytes 165896 | tf_op jit(solution)/shard_map/ppermute | solution.py:838
  60.9 0.8 %collective-permute-start.15 = (bf16[2,108,128]{2,1,0:T(8,128)(2,1)S(1)}, bf16[2,108,128]{2,1,0:T(8,128)(2,1)S(1)}, u32[]{:S(2)}, u32[]{:S(2)}) collective-permute-start(bf16[2,108,128]{2,1,0:T(8,128)(2,1)S(1)} %get-tuple-element.21), channel_id=1, source_target_pairs={{0,6},{1,7},{2,4},{3,5},{4,2},{5,3},{6,0},{7,1},{8,14},{9,15},{10,... | collective-permute-start | bytes 165896 | tf_op jit(solution)/shard_map/ppermute | solution.py:838
  61.7 1.5 %collective-permute-start.14 = (bf16[2,108,128]{2,1,0:T(8,128)(2,1)S(1)}, bf16[2,108,128]{2,1,0:T(8,128)(2,1)S(1)}, u32[]{:S(2)}, u32[]{:S(2)}) collective-permute-start(bf16[2,108,128]{2,1,0:T(8,128)(2,1)S(1)} %get-tuple-element.22), channel_id=1, source_target_pairs={{0,4},{1,5},{2,6},{3,7},{4,0},{5,1},{6,2},{7,3},{8,12},{9,13},{10,... | collective-permute-start | bytes 165896 | tf_op jit(solution)/shard_map/ppermute | solution.py:838
  63.2 0.7 %collective-permute-done.13 = bf16[2,108,128]{2,1,0:T(8,128)(2,1)S(1)} collective-permute-done((bf16[2,108,128]{2,1,0:T(8,128)(2,1)S(1)}, bf16[2,108,128]{2,1,0:T(8,128)(2,1)S(1)}, u32[]{:S(2)}, u32[]{:S(2)}) %collective-permute-start.13) | collective-permute-done | bytes 55328 | tf_op jit(solution)/shard_map/ppermute | solution.py:838
  63.9 2.2 %collective-permute-done.15 = bf16[2,108,128]{2,1,0:T(8,128)(2,1)S(1)} collective-permute-done((bf16[2,108,128]{2,1,0:T(8,128)(2,1)S(1)}, bf16[2,108,128]{2,1,0:T(8,128)(2,1)S(1)}, u32[]{:S(2)}, u32[]{:S(2)}) %collective-permute-start.15) | collective-permute-done | bytes 55328 | tf_op jit(solution)/shard_map/ppermute | solution.py:838
  (47 shorter events, 2.4 us)
Async XLA Ops:
  1.9 8.8 %copy-start = (bf16[3456,128]{1,0:T(8,128)(2,1)S(1)}, bf16[3456,128]{1,0:T(8,128)(2,1)}, u32[]{:S(2)}) copy-start(bf16[3456,128]{1,0:T(8,128)(2,1)} %refs_5_.2) | copy-start | bytes 2654212
  2.0 8.7 %collective-permute-start.2 = (bf16[3,16,16,128]{3,2,1,0:T(8,128)(2,1)S(1)}, bf16[3,16,16,128]{3,2,1,0:T(8,128)(2,1)S(1)}, u32[]{:S(2)}, u32[]{:S(2)}) collective-permute-start(bf16[3,16,16,128]{3,2,1,0:T(8,128)(2,1)S(1)} %pad.25), channel_id=1, source_target_pairs={{0,4},{1,5},{2,6},{3,7},{4,0},{5,1},{6,2},{7,3},{8,12},{9,13},{10,... | collective-permute-start | bytes 589832 | tf_op jit(solution)/shard_map/ppermute | solution.py:687
  5.1 5.6 %collective-permute-start = (bf16[8,3,16,128]{3,2,1,0:T(8,128)(2,1)S(1)}, bf16[8,3,16,128]{3,2,1,0:T(8,128)(2,1)S(1)}, u32[]{:S(2)}, u32[]{:S(2)}) collective-permute-start(bf16[8,3,16,128]{3,2,1,0:T(8,128)(2,1)S(1)} %pad.23), channel_id=1, source_target_pairs={{0,1},{1,0},{2,3},{3,2},{4,5},{5,4},{6,7},{7,6},{8,9},{9,8},{10,11... | collective-permute-start | bytes 294920 | tf_op jit(solution)/shard_map/ppermute | solution.py:687
  5.2 5.5 %collective-permute-start.1 = (bf16[8,3,16,128]{3,2,1,0:T(8,128)(2,1)S(1)}, bf16[8,3,16,128]{3,2,1,0:T(8,128)(2,1)S(1)}, u32[]{:S(2)}, u32[]{:S(2)}) collective-permute-start(bf16[8,3,16,128]{3,2,1,0:T(8,128)(2,1)S(1)} %pad.24), channel_id=1, source_target_pairs={{1,2},{2,1},{5,6},{6,5},{9,10},{10,9},{13,14},{14,13},{17,18},{18,... | collective-permute-start | bytes 294920 | tf_op jit(solution)/shard_map/ppermute | solution.py:687
  6.0 4.7 %collective-permute-start.3 = (bf16[3,3,16,128]{3,2,1,0:T(8,128)(2,1)S(1)}, bf16[3,3,16,128]{3,2,1,0:T(8,128)(2,1)S(1)}, u32[]{:S(2)}, u32[]{:S(2)}) collective-permute-start(bf16[3,3,16,128]{3,2,1,0:T(8,128)(2,1)S(1)} %pad.26), channel_id=1, source_target_pairs={{0,5},{1,4},{2,7},{3,6},{4,1},{5,0},{6,3},{7,2},{8,13},{9,12},{10,... | collective-permute-start | bytes 110600 | tf_op jit(solution)/shard_map/ppermute | solution.py:687
  9.1 1.6 %collective-permute-start.4 = (bf16[3,3,16,128]{3,2,1,0:T(8,128)(2,1)S(1)}, bf16[3,3,16,128]{3,2,1,0:T(8,128)(2,1)S(1)}, u32[]{:S(2)}, u32[]{:S(2)}) collective-permute-start(bf16[3,3,16,128]{3,2,1,0:T(8,128)(2,1)S(1)} %pad.27), channel_id=1, source_target_pairs={{1,6},{2,5},{5,2},{6,1},{9,14},{10,13},{13,10},{14,9},{17,22},{18,... | collective-permute-start | bytes 110600 | tf_op jit(solution)/shard_map/ppermute | solution.py:687
  9.9 24.1 %copy-start.2 = (bf16[576,128]{1,0:T(8,128)(2,1)S(1)}, bf16[576,128]{1,0:T(8,128)(2,1)}, u32[]{:S(2)}) copy-start(bf16[576,128]{1,0:T(8,128)(2,1)} %refs_6_.3) | copy-start | bytes 442372
  9.9 24.1 %copy-start.3 = (bf16[576,64]{0,1:T(8,128)(2,1)S(1)}, bf16[576,64]{0,1:T(8,128)(2,1)}, u32[]{:S(2)}) copy-start(bf16[576,64]{0,1:T(8,128)(2,1)} %param.14) | copy-start | bytes 221188
  9.9 24.1 %copy-start.5 = (bf16[27,64]{1,0:T(8,128)(2,1)S(1)}, bf16[27,64]{1,0:T(8,128)(2,1)}, u32[]{:S(2)}) copy-start(bf16[27,64]{1,0:T(8,128)(2,1)} %refs_4_.2) | copy-start | bytes 10372
  22.5 5.3 %collective-permute-start.5 = (bf16[64,128]{1,0:T(8,128)(2,1)S(1)}, bf16[64,128]{1,0:T(8,128)(2,1)S(1)}, u32[]{:S(2)}, u32[]{:S(2)}) collective-permute-start(bf16[64,128]{1,0:T(8,128)(2,1)S(1)} %get-tuple-element.9), channel_id=1, source_target_pairs={{0,1},{1,0},{2,3},{3,2},{4,5},{5,4},{6,7},{7,6},{8,9},{9,8},{10,11... | collective-permute-start | bytes 49160 | tf_op jit(solution)/shard_map/ppermute | solution.py:725
  27.8 5.0 %collective-permute-start.8 = (bf16[2,64,128]{2,1,0:T(8,128)(2,1)S(1)}, bf16[2,64,128]{2,1,0:T(8,128)(2,1)S(1)}, u32[]{:S(2)}, u32[]{:S(2)}) collective-permute-start(bf16[2,64,128]{2,1,0:T(8,128)(2,1)S(1)} %pad_maximum_fusion.refs_0_), channel_id=1, source_target_pairs={{0,6},{1,7},{2,4},{3,5},{4,2},{5,3},{6,0},{7,1},{8,14},{9,15},{10,... | collective-permute-start | bytes 98312 | tf_op jit(solution)/shard_map/ppermute | solution.py:728
  28.3 4.5 %collective-permute-start.7 = (bf16[2,64,128]{2,1,0:T(8,128)(2,1)S(1)}, bf16[2,64,128]{2,1,0:T(8,128)(2,1)S(1)}, u32[]{:S(2)}, u32[]{:S(2)}) collective-permute-start(bf16[2,64,128]{2,1,0:T(8,128)(2,1)S(1)} %pad_maximum_fusion.refs_0_), channel_id=1, source_target_pairs={{0,4},{1,5},{2,6},{3,7},{4,0},{5,1},{6,2},{7,3},{8,12},{9,13},{10,... | collective-permute-start | bytes 98312 | tf_op jit(solution)/shard_map/ppermute | solution.py:728
  30.1 3.9 %collective-permute-start.6 = (bf16[2,64,128]{2,1,0:T(8,128)(2,1)S(1)}, bf16[2,64,128]{2,1,0:T(8,128)(2,1)S(1)}, u32[]{:S(2)}, u32[]{:S(2)}) collective-permute-start(bf16[2,64,128]{2,1,0:T(8,128)(2,1)S(1)} %pad_maximum_fusion.refs_0_), channel_id=1, source_target_pairs={{0,2},{1,3},{2,0},{3,1},{4,6},{5,7},{6,4},{7,5},{8,10},{9,11},{10,... | collective-permute-start | bytes 98312 | tf_op jit(solution)/shard_map/ppermute | solution.py:728
  34.0 14.9 %copy-start.7 = (f32[10,288,128]{2,1,0:T(8,128)S(1)}, f32[10,288,128]{2,1,0:T(8,128)}, u32[]{:S(2)}) copy-start(f32[10,288,128]{2,1,0:T(8,128)} %get-tuple-element.11.refs_7_) | copy-start | bytes 4423684
  34.0 14.8 %copy-start.8 = (f32[8,256,128]{2,1,0:T(8,128)S(1)}, f32[8,256,128]{2,1,0:T(8,128)}, u32[]{:S(2)}) copy-start(f32[8,256,128]{2,1,0:T(8,128)} %get-tuple-element.10.refs_6_) | copy-start | bytes 3145732
  34.0 14.8 %copy-start.9 = (bf16[10,18,16,128]{3,2,1,0:T(8,128)(2,1)S(1)}, bf16[10,18,16,128]{3,2,1,0:T(8,128)(2,1)}, u32[]{:S(2)}) copy-start(bf16[10,18,16,128]{3,2,1,0:T(8,128)(2,1)} %get-tuple-element.12.refs_8_) | copy-start | bytes 2211844
  34.0 14.8 %copy-start.10 = (bf16[10,18,16,128]{3,2,1,0:T(8,128)(2,1)S(1)}, bf16[10,18,16,128]{3,2,1,0:T(8,128)(2,1)}, u32[]{:S(2)}) copy-start(bf16[10,18,16,128]{3,2,1,0:T(8,128)(2,1)} %get-tuple-element.13.refs_9_) | copy-start | bytes 2211844
  40.6 5.5 %collective-permute-start.11 = (bf16[3,8,144]{2,1,0:T(8,128)(2,1)S(1)}, bf16[3,8,144]{2,1,0:T(8,128)(2,1)S(1)}, u32[]{:S(2)}, u32[]{:S(2)}) collective-permute-start(bf16[3,8,144]{2,1,0:T(8,128)(2,1)S(1)} %shard_map.96.refs_0_), channel_id=1, source_target_pairs={{0,24},{8,16},{16,8},{24,0},{1,25},{9,17},{17,9},{25,1},{2,26},{10... | collective-permute-start | bytes 20744 | tf_op jit(solution)/shard_map/ppermute | solution.py:788
  44.2 4.6 %collective-permute-start.10 = (bf16[3,8,144]{2,1,0:T(8,128)(2,1)S(1)}, bf16[3,8,144]{2,1,0:T(8,128)(2,1)S(1)}, u32[]{:S(2)}, u32[]{:S(2)}) collective-permute-start(bf16[3,8,144]{2,1,0:T(8,128)(2,1)S(1)} %shard_map.96.refs_0_), channel_id=1, source_target_pairs={{0,16},{8,24},{16,0},{24,8},{1,17},{9,25},{17,1},{25,9},{2,18},{10... | collective-permute-start | bytes 20744 | tf_op jit(solution)/shard_map/ppermute | solution.py:788
  44.2 4.6 %collective-permute-start.9 = (bf16[3,8,144]{2,1,0:T(8,128)(2,1)S(1)}, bf16[3,8,144]{2,1,0:T(8,128)(2,1)S(1)}, u32[]{:S(2)}, u32[]{:S(2)}) collective-permute-start(bf16[3,8,144]{2,1,0:T(8,128)(2,1)S(1)} %shard_map.96.refs_0_), channel_id=1, source_target_pairs={{0,8},{8,0},{16,24},{24,16},{1,9},{9,1},{17,25},{25,17},{2,10},{10... | collective-permute-start | bytes 20744 | tf_op jit(solution)/shard_map/ppermute | solution.py:788
  58.0 1.6 %collective-permute-start.12 = (bf16[4,2,108,128]{3,2,1,0:T(8,128)(2,1)S(1)}, bf16[4,2,108,128]{3,2,1,0:T(8,128)(2,1)S(1)}, u32[]{:S(2)}, u32[]{:S(2)}) collective-permute-start(bf16[4,2,108,128]{3,2,1,0:T(8,128)(2,1)S(1)} %get-tuple-element.15), channel_id=1, source_target_pairs={{0,1},{1,0},{2,3},{3,2},{4,5},{5,4},{6,7},{7,6},{8,9},{9,8},{10,11... | collective-permute-start | bytes 663560 | tf_op jit(solution)/shard_map/ppermute | solution.py:834
  59.6 4.2 %collective-permute-start.13 = (bf16[2,108,128]{2,1,0:T(8,128)(2,1)S(1)}, bf16[2,108,128]{2,1,0:T(8,128)(2,1)S(1)}, u32[]{:S(2)}, u32[]{:S(2)}) collective-permute-start(bf16[2,108,128]{2,1,0:T(8,128)(2,1)S(1)} %get-tuple-element.20), channel_id=1, source_target_pairs={{0,2},{1,3},{2,0},{3,1},{4,6},{5,7},{6,4},{7,5},{8,10},{9,11},{10,... | collective-permute-start | bytes 165896 | tf_op jit(solution)/shard_map/ppermute | solution.py:838
  60.9 5.2 %collective-permute-start.15 = (bf16[2,108,128]{2,1,0:T(8,128)(2,1)S(1)}, bf16[2,108,128]{2,1,0:T(8,128)(2,1)S(1)}, u32[]{:S(2)}, u32[]{:S(2)}) collective-permute-start(bf16[2,108,128]{2,1,0:T(8,128)(2,1)S(1)} %get-tuple-element.21), channel_id=1, source_target_pairs={{0,6},{1,7},{2,4},{3,5},{4,2},{5,3},{6,0},{7,1},{8,14},{9,15},{10,... | collective-permute-start | bytes 165896 | tf_op jit(solution)/shard_map/ppermute | solution.py:838
  61.7 4.4 %collective-permute-start.14 = (bf16[2,108,128]{2,1,0:T(8,128)(2,1)S(1)}, bf16[2,108,128]{2,1,0:T(8,128)(2,1)S(1)}, u32[]{:S(2)}, u32[]{:S(2)}) collective-permute-start(bf16[2,108,128]{2,1,0:T(8,128)(2,1)S(1)} %get-tuple-element.22), channel_id=1, source_target_pairs={{0,4},{1,5},{2,6},{3,7},{4,0},{5,1},{6,2},{7,3},{8,12},{9,13},{10,... | collective-permute-start | bytes 165896 | tf_op jit(solution)/shard_map/ppermute | solution.py:838
  (3 other events, 26.4 us)

commit v6 on v5

--- a/solution.py
+++ b/solution.py
@@ -52,10 +52,21 @@
 
 def frame_weight(ref):
     third = ref.shape[0] // 3
-    return jnp.concatenate([ref[pl.ds(third * k, third)] for k in range(3)], axis=1)
-
-
-def conv_pairs(source, rows, cols, weight, use):
+    return jnp.concatenate([ref[pl.ds(third * k, third)] for k in range(2)], axis=1)
+
+
+def last_weight(ref):
+    third = ref.shape[0] // 3
+    size = third // 9
+    rows = []
+    for dr in range(3):
+        near = [ref[pl.ds(2 * third + (3 * dr + dc) * size, size)] for dc in range(3)]
+        rows.append(jnp.concatenate([near[1], near[0]], axis=1))
+        rows.append(jnp.concatenate([near[2], jnp.zeros_like(near[2])], axis=1))
+    return jnp.concatenate(rows, axis=0)
+
+
+def conv_pairs(source, rows, cols, weight, shifted_weight, use):
     slots, channels = source.shape[-2:]
     count = cols * slots
 
@@ -66,10 +77,18 @@
             for dc in range(3)
         ]
         sums = matmul(jnp.concatenate(slabs, axis=1), weight[...])
+        more = [
+            source[pl.ds(2 * q + dr, 2), pl.ds(dc, cols + 1)].reshape(-1, channels)
+            for dr in range(3)
+            for dc in range(2)
+        ]
+        last = matmul(jnp.concatenate(more, axis=1), shifted_weight[...])
+        last = last.reshape(2, count + slots, 2 * channels)
+        last = last[:, slots:, :channels] + last[:, :count, channels:]
         total = (
             pltpu.roll(sums[:, :channels], 1, 0)
-            + sums[:, channels : 2 * channels]
-            + pltpu.roll(sums[:, 2 * channels :], 2 * count - 1, 0)
+            + sums[:, channels:]
+            + pltpu.roll(last.reshape(2 * count, channels), 2 * count - 1, 0)
         )
         for k in range(2):
             use(2 * q + k, total[k * count : (k + 1) * count])
@@ -81,7 +100,7 @@
     near = refs[: len(places)]
     (
         first, second, rgb, target, cells_out, hidden_out, first_out, second_out, payload,
-        cells, hidden, slope_first, slope_second, spread_weight, picked, spaced, colour, project,
+        cells, hidden, slope_first, slope_second, spread_weight, shifted_weight, picked, spaced, colour, project,
         sems,
     ) = refs[len(places) :]
     rows, cols, slots, channels = own.shape
@@ -115,6 +134,7 @@
     ]
     copies[0].start()
     spread_weight[...] = frame_weight(first)
+    shifted_weight[...] = last_weight(first)
 
     def first_layer(r, pre):
         row = top - 2 + r
@@ -130,10 +150,11 @@
         def _():
             slope_first[r - 2] = slope[2 * slots : (2 + cols) * slots]
 
-    conv_pairs(cells, rows + 4, cols + 4, spread_weight, first_layer)
+    conv_pairs(cells, rows + 4, cols + 4, spread_weight, shifted_weight, first_layer)
     copies[1].start()
     copies[2].start()
     spread_weight[...] = frame_weight(second)
+    shifted_weight[...] = last_weight(second)
     own_slots = slots // groups
     spaced[...] = jnp.zeros(spaced.shape, f32)
     project[...] = jnp.zeros(project.shape, f32)
@@ -159,7 +180,7 @@
         at = jnp.clip(r - 1, -1, rows) + 1
         colour[pl.ds(pl.multiple_of(at * 8, 8), 8)] = line
 
-    conv_pairs(hidden, rows + 2, cols + 2, spread_weight, second_layer)
+    conv_pairs(hidden, rows + 2, cols + 2, spread_weight, shifted_weight, second_layer)
     copies[3].start()
     size, line = payload.shape
     pieces = [colour[pl.ds(8 + k, rows, stride=8)] for k in range(3)]
@@ -481,7 +502,7 @@
     ) = refs[groups : groups + 6]
     terms = refs[groups + 6 : groups + 6 + outs]
     (
-        slope_first, slope_second, cells, hidden, weight, back_second, paint, shown,
+        slope_first, slope_second, cells, hidden, weight, back_second, back_last, paint, shown,
         painted, hidden_grad, delta_second, delta_own, shifted, sums, sems,
     ) = refs[groups + 6 + outs :]
     copies = [
@@ -581,15 +602,23 @@
         for tap in range(9):
             at = (dt * 9 + tap) * channels
             turned = weight[at : at + channels].astype(jnp.float32).T.astype(jnp.bfloat16)
-            back_second[
-                (8 - tap) * channels : (9 - tap) * channels,
-                (2 - dt) * channels : (3 - dt) * channels,
-            ] = turned
+            at, dr, dc = 8 - tap, (8 - tap) // 3, (8 - tap) % 3
+            if dt > 0:
+                back_second[
+                    at * channels : (at + 1) * channels,
+                    (2 - dt) * channels : (3 - dt) * channels,
+                ] = turned
+                continue
+            into = (2 * dr + (dc == 2)) * channels
+            side = channels if dc == 0 else 0
+            back_last[into : into + channels, side : side + channels] = turned
+            if dc == 2:
+                back_last[into : into + channels, channels : 2 * channels] = jnp.zeros_like(turned)
 
     def back_row(r, back):
         delta_own[r] = (back * slope_first[r]).astype(jnp.bfloat16)
 
-    conv_pairs(delta_second, rows, cols, back_second, back_row)
+    conv_pairs(delta_second, rows, cols, back_second, back_last, back_row)
     gradient_taps(cells, delta_own, shifted, sums, first_tap)
     put(0)
 
@@ -707,7 +736,8 @@
             ((rows + 4, cols + 4, slots, channels), bf16),
             ((rows, cols * slots, channels), f32),
             ((rows + 2, (cols + 2) * slots, channels), f32),
-            ((9 * channels, 3 * channels), bf16),
+            ((9 * channels, 2 * channels), bf16),
+            ((6 * channels, 2 * channels), bf16),
             ((rows + 2, cols * slots, channels), f32),
             ((rows + 2, cols * half, channels), f32),
             (((rows + 2) * 8, cols * half), f32),
@@ -810,7 +840,8 @@
             ((rows + 2, cols + 2, slots, channels), bf16),
             ((rows + 2, cols + 2, slots, channels), bf16),
             (conv_second.shape, bf16),
-            ((9 * channels, 3 * channels), bf16),
+            ((9 * channels, 2 * channels), bf16),
+            ((6 * channels, 2 * channels), bf16),
             ((8, channels), f32),
             ((groups, number * 8, (cols + 2) * half), f32),
             ((number, groups, (cols + 2) * half, channels), f32),

time: 66.9 us -> 65.3 us (0.976)
  Pallas kernels: 27.4 us -> 25.8 us
    pallas_call x1, Pallas kernels: 11.7 us -> 10.4 us  [local(): call(functools.partial(forward_kernel, frames, parts, pack, places), (plt...]
where the time goes in v6:
time: 65.3 us; the launch traced here: 65.2 us
  Pallas kernels  25.8 us (40%)
  starting transfers between devices  23.5 us (36%)
  waiting for transfers between devices  12.5 us (19%)
  local copies, waits for them, and re-layouts  2.24 us (3%)
  between operations  0.96 us (1%)
    pallas_call x1, Pallas kernels, local(): call(functools.partial(forward_kernel, frames, parts, pack, places), (plt...  10.4 us
    pallas_call x1, Pallas kernels, local(): call(functools.partial(backward_kernel, parts=parts, out_rows=out_rows, g...  8.82 us
    ppermute x5, starting transfers between devices, local(): lax.ppermute(slotted(edge, slots), plane, moves)  7.51 us
    pallas_call x1, Pallas kernels, local(): call(functools.partial(perceptual_kernel, (rows, cols, blocks, block_fram...  6.58 us
    ppermute x1, starting transfers between devices, local(): other = lax.ppermute(payload, plane, [(i, i ^ 1) for i in range(devices)])  4.48 us
    ppermute x3, starting transfers between devices, local(): gathered.append(lax.ppermute(pixels, 'grp', partners(step, groups)))  4.42 us
    ppermute x3, waiting for transfers between devices, local(): gathered.append(lax.ppermute(pixels, 'grp', partners(step, groups)))  3.81 us
    ppermute x3, starting transfers between devices, local(): lax.ppermute(halves[k].astype(bf16), plane, partners(2 * k, devices))  3.55 us
  transfers between devices with their start and end apart: 16, of which 9 were waited for; matrix products, arithmetic and copies ran while one was open for 0% of the time, Pallas kernels for 0%

profile of v6, /device:TPU:0, one launch (start us, length us, event | category | flops | bytes accessed | tf_op | source)
XLA Modules:
  0.0 65.2 jit_solution(10913824155272437414)
XLA Ops:
  0.6 1.3 %copy.19 = bf16[12,8,16,128]{3,0,2,1:T(8,128)(2,1)S(1)} copy(bf16[12,8,16,128]{3,2,1,0:T(8,128)(2,1)} %bitcast.35) | data formatting | bytes 786432 | tf_op jit(solution)/shard_map/reshape | solution.py:713
  2.0 3.0 %collective-permute-start.2 = (bf16[3,16,16,128]{3,2,1,0:T(8,128)(2,1)S(1)}, bf16[3,16,16,128]{3,2,1,0:T(8,128)(2,1)S(1)}, u32[]{:S(2)}, u32[]{:S(2)}) collective-permute-start(bf16[3,16,16,128]{3,2,1,0:T(8,128)(2,1)S(1)} %pad.25), channel_id=1, source_target_pairs={{0,4},{1,5},{2,6},{3,7},{4,0},{5,1},{6,2},{7,3},{8,12},{9,13},{10,... | collective-permute-start | bytes 589832 | tf_op jit(solution)/shard_map/ppermute | solution.py:716
  5.2 0.7 %collective-permute-start.1 = (bf16[8,3,16,128]{3,2,1,0:T(8,128)(2,1)S(1)}, bf16[8,3,16,128]{3,2,1,0:T(8,128)(2,1)S(1)}, u32[]{:S(2)}, u32[]{:S(2)}) collective-permute-start(bf16[8,3,16,128]{3,2,1,0:T(8,128)(2,1)S(1)} %pad.24), channel_id=1, source_target_pairs={{1,2},{2,1},{5,6},{6,5},{9,10},{10,9},{13,14},{14,13},{17,18},{18,... | collective-permute-start | bytes 294920 | tf_op jit(solution)/shard_map/ppermute | solution.py:716
  6.0 3.1 %collective-permute-start.3 = (bf16[3,3,16,128]{3,2,1,0:T(8,128)(2,1)S(1)}, bf16[3,3,16,128]{3,2,1,0:T(8,128)(2,1)S(1)}, u32[]{:S(2)}, u32[]{:S(2)}) collective-permute-start(bf16[3,3,16,128]{3,2,1,0:T(8,128)(2,1)S(1)} %pad.26), channel_id=1, source_target_pairs={{0,5},{1,4},{2,7},{3,6},{4,1},{5,0},{6,3},{7,2},{8,13},{9,12},{10,... | collective-permute-start | bytes 110600 | tf_op jit(solution)/shard_map/ppermute | solution.py:716
  9.9 0.8 %collective-permute-done.3.refs_3_ = bf16[3,3,16,128]{3,2,1,0:T(8,128)(2,1)S(1)} collective-permute-done((bf16[3,3,16,128]{3,2,1,0:T(8,128)(2,1)S(1)}, bf16[3,3,16,128]{3,2,1,0:T(8,128)(2,1)S(1)}, u32[]{:S(2)}, u32[]{:S(2)}) %collective-permute-start.3) | collective-permute-done | bytes 36896 | tf_op jit(solution)/shard_map/ppermute | solution.py:716
  10.8 10.4 %shard_map.95 = (bf16[10,18,16,128]{3,2,1,0:T(8,128)(2,1)}, bf16[10,18,16,128]{3,2,1,0:T(8,128)(2,1)}, f32[8,256,128]{2,1,0:T(8,128)}, f32[10,288,128]{2,1,0:T(8,128)}, bf16[64,128]{1,0:T(8,128)(2,1)S(1)}) custom-call(bf16[8,16,16,128]{3,2,1,0:T(8,128)(2,1)S(1)} %pad.22.own, bf16[8,3,16,128]{3,2,1,0:T(8,128)(2,1)S(1)} %collective-permute-done.refs_0_, ...), custom_call_target="tpu_custom_call" | custom-call | flops 8589934592 | bytes 1048576 | tf_op jit(solution)/shard_map/pallas_call | solution.py:725
  21.1 4.5 %collective-permute-start.5 = (bf16[64,128]{1,0:T(8,128)(2,1)S(1)}, bf16[64,128]{1,0:T(8,128)(2,1)S(1)}, u32[]{:S(2)}, u32[]{:S(2)}) collective-permute-start(bf16[64,128]{1,0:T(8,128)(2,1)S(1)} %get-tuple-element.9), channel_id=1, source_target_pairs={{0,1},{1,0},{2,3},{3,2},{4,5},{5,4},{6,7},{7,6},{8,9},{9,8},{10,11... | collective-permute-start | bytes 49160 | tf_op jit(solution)/shard_map/ppermute | solution.py:755
  25.6 0.8 %collective-permute-done.5 = bf16[64,128]{1,0:T(8,128)(2,1)S(1)} collective-permute-done((bf16[64,128]{1,0:T(8,128)(2,1)S(1)}, bf16[64,128]{1,0:T(8,128)(2,1)S(1)}, u32[]{:S(2)}, u32[]{:S(2)}) %collective-permute-start.5) | collective-permute-done | bytes 16416 | tf_op jit(solution)/shard_map/ppermute | solution.py:755
  27.0 1.8 %collective-permute-start.7 = (bf16[2,64,128]{2,1,0:T(8,128)(2,1)S(1)}, bf16[2,64,128]{2,1,0:T(8,128)(2,1)S(1)}, u32[]{:S(2)}, u32[]{:S(2)}) collective-permute-start(bf16[2,64,128]{2,1,0:T(8,128)(2,1)S(1)} %pad_maximum_fusion.refs_0_), channel_id=1, source_target_pairs={{0,4},{1,5},{2,6},{3,7},{4,0},{5,1},{6,2},{7,3},{8,12},{9,13},{10,... | collective-permute-start | bytes 98312 | tf_op jit(solution)/shard_map/ppermute | solution.py:758
  28.8 1.2 %collective-permute-start.6 = (bf16[2,64,128]{2,1,0:T(8,128)(2,1)S(1)}, bf16[2,64,128]{2,1,0:T(8,128)(2,1)S(1)}, u32[]{:S(2)}, u32[]{:S(2)}) collective-permute-start(bf16[2,64,128]{2,1,0:T(8,128)(2,1)S(1)} %pad_maximum_fusion.refs_0_), channel_id=1, source_target_pairs={{0,2},{1,3},{2,0},{3,1},{4,6},{5,7},{6,4},{7,5},{8,10},{9,11},{10,... | collective-permute-start | bytes 98312 | tf_op jit(solution)/shard_map/ppermute | solution.py:758
  30.0 1.5 %collective-permute-done.8.refs_3_ = bf16[2,64,128]{2,1,0:T(8,128)(2,1)S(1)} collective-permute-done((bf16[2,64,128]{2,1,0:T(8,128)(2,1)S(1)}, bf16[2,64,128]{2,1,0:T(8,128)(2,1)S(1)}, u32[]{:S(2)}, u32[]{:S(2)}) %collective-permute-start.8) | collective-permute-done | bytes 32800 | tf_op jit(solution)/shard_map/ppermute | solution.py:758
  31.5 1.2 %collective-permute-done.6.refs_1_ = bf16[2,64,128]{2,1,0:T(8,128)(2,1)S(1)} collective-permute-done((bf16[2,64,128]{2,1,0:T(8,128)(2,1)S(1)}, bf16[2,64,128]{2,1,0:T(8,128)(2,1)S(1)}, u32[]{:S(2)}, u32[]{:S(2)}) %collective-permute-start.6) | collective-permute-done | bytes 32800 | tf_op jit(solution)/shard_map/ppermute | solution.py:758
  32.7 6.6 %shard_map.96.refs_0_ = bf16[3,8,144]{2,1,0:T(8,128)(2,1)S(1)} custom-call(bf16[2,64,128]{2,1,0:T(8,128)(2,1)S(1)} %pad_maximum_fusion.refs_0_, bf16[2,64,128]{2,1,0:T(8,128)(2,1)S(1)} %collective-permute-done.6.refs_1_, bf16[2,64,128]{2,1,0:T(8,128)(2,1)S(1)} %collective-permute-done.7.refs_2_, bf16[2,64,128]{2,1,0:T(8,128)(2,1)S(1)} %collective-permute-done.8.refs_3_, ...), custom_call_target="tpu_custom_call" | custom-call | flops 4294967296 | bytes 1048576 | tf_op jit(solution)/shard_map/pallas_call | solution.py:773
  39.3 3.6 %collective-permute-start.11 = (bf16[3,8,144]{2,1,0:T(8,128)(2,1)S(1)}, bf16[3,8,144]{2,1,0:T(8,128)(2,1)S(1)}, u32[]{:S(2)}, u32[]{:S(2)}) collective-permute-start(bf16[3,8,144]{2,1,0:T(8,128)(2,1)S(1)} %shard_map.96.refs_0_), channel_id=1, source_target_pairs={{0,24},{8,16},{16,8},{24,0},{1,25},{9,17},{17,9},{25,1},{2,26},{10... | collective-permute-start | bytes 20744 | tf_op jit(solution)/shard_map/ppermute | solution.py:818
  43.0 0.8 %collective-permute-start.9 = (bf16[3,8,144]{2,1,0:T(8,128)(2,1)S(1)}, bf16[3,8,144]{2,1,0:T(8,128)(2,1)S(1)}, u32[]{:S(2)}, u32[]{:S(2)}) collective-permute-start(bf16[3,8,144]{2,1,0:T(8,128)(2,1)S(1)} %shard_map.96.refs_0_), channel_id=1, source_target_pairs={{0,8},{8,0},{16,24},{24,16},{1,9},{9,1},{17,25},{25,17},{2,10},{10... | collective-permute-start | bytes 20744 | tf_op jit(solution)/shard_map/ppermute | solution.py:818
  43.7 1.1 %collective-permute-done.11.refs_3_ = bf16[3,8,144]{2,1,0:T(8,128)(2,1)S(1)} collective-permute-done((bf16[3,8,144]{2,1,0:T(8,128)(2,1)S(1)}, bf16[3,8,144]{2,1,0:T(8,128)(2,1)S(1)}, u32[]{:S(2)}, u32[]{:S(2)}) %collective-permute-start.11) | collective-permute-done | bytes 6944 | tf_op jit(solution)/shard_map/ppermute | solution.py:818
  44.8 2.7 %collective-permute-done.10.refs_2_ = bf16[3,8,144]{2,1,0:T(8,128)(2,1)S(1)} collective-permute-done((bf16[3,8,144]{2,1,0:T(8,128)(2,1)S(1)}, bf16[3,8,144]{2,1,0:T(8,128)(2,1)S(1)}, u32[]{:S(2)}, u32[]{:S(2)}) %collective-permute-start.10) | collective-permute-done | bytes 6944 | tf_op jit(solution)/shard_map/ppermute | solution.py:818
  47.6 8.8 %shard_map.97 = (bf16[4,2,108,128]{3,2,1,0:T(8,128)(2,1)S(1)}, bf16[4,2,108,128]{3,2,1,0:T(8,128)(2,1)S(1)}) custom-call(bf16[3,8,144]{2,1,0:T(8,128)(2,1)S(1)} %shard_map.96.refs_0_, bf16[3,8,144]{2,1,0:T(8,128)(2,1)S(1)} %collective-permute-done.9.refs_1_, bf16[3,8,144]{2,1,0:T(8,128)(2,1)S(1)} %collective-permute-done.10.refs_2_, ...), custom_call_target="tpu_custom_call" | custom-call | flops 4294967296 | bytes 1048576 | tf_op jit(solution)/shard_map/pallas_call | solution.py:831
  56.5 1.5 %collective-permute-done.12 = bf16[4,2,108,128]{3,2,1,0:T(8,128)(2,1)S(1)} collective-permute-done((bf16[4,2,108,128]{3,2,1,0:T(8,128)(2,1)S(1)}, bf16[4,2,108,128]{3,2,1,0:T(8,128)(2,1)S(1)}, u32[]{:S(2)}, u32[]{:S(2)}) %collective-permute-start.12) | collective-permute-done | bytes 221216 | tf_op jit(solution)/shard_map/ppermute | solution.py:865
  58.0 1.2 %collective-permute-start.13 = (bf16[2,108,128]{2,1,0:T(8,128)(2,1)S(1)}, bf16[2,108,128]{2,1,0:T(8,128)(2,1)S(1)}, u32[]{:S(2)}, u32[]{:S(2)}) collective-permute-start(bf16[2,108,128]{2,1,0:T(8,128)(2,1)S(1)} %get-tuple-element.20), channel_id=1, source_target_pairs={{0,2},{1,3},{2,0},{3,1},{4,6},{5,7},{6,4},{7,5},{8,10},{9,11},{10,... | collective-permute-start | bytes 165896 | tf_op jit(solution)/shard_map/ppermute | solution.py:869
  59.3 0.8 %collective-permute-start.15 = (bf16[2,108,128]{2,1,0:T(8,128)(2,1)S(1)}, bf16[2,108,128]{2,1,0:T(8,128)(2,1)S(1)}, u32[]{:S(2)}, u32[]{:S(2)}) collective-permute-start(bf16[2,108,128]{2,1,0:T(8,128)(2,1)S(1)} %get-tuple-element.21), channel_id=1, source_target_pairs={{0,6},{1,7},{2,4},{3,5},{4,2},{5,3},{6,0},{7,1},{8,14},{9,15},{10,... | collective-permute-start | bytes 165896 | tf_op jit(solution)/shard_map/ppermute | solution.py:869
  60.1 1.5 %collective-permute-start.14 = (bf16[2,108,128]{2,1,0:T(8,128)(2,1)S(1)}, bf16[2,108,128]{2,1,0:T(8,128)(2,1)S(1)}, u32[]{:S(2)}, u32[]{:S(2)}) collective-permute-start(bf16[2,108,128]{2,1,0:T(8,128)(2,1)S(1)} %get-tuple-element.22), channel_id=1, source_target_pairs={{0,4},{1,5},{2,6},{3,7},{4,0},{5,1},{6,2},{7,3},{8,12},{9,13},{10,... | collective-permute-start | bytes 165896 | tf_op jit(solution)/shard_map/ppermute | solution.py:869
  61.6 0.7 %collective-permute-done.13 = bf16[2,108,128]{2,1,0:T(8,128)(2,1)S(1)} collective-permute-done((bf16[2,108,128]{2,1,0:T(8,128)(2,1)S(1)}, bf16[2,108,128]{2,1,0:T(8,128)(2,1)S(1)}, u32[]{:S(2)}, u32[]{:S(2)}) %collective-permute-start.13) | collective-permute-done | bytes 55328 | tf_op jit(solution)/shard_map/ppermute | solution.py:869
  62.3 2.2 %collective-permute-done.15 = bf16[2,108,128]{2,1,0:T(8,128)(2,1)S(1)} collective-permute-done((bf16[2,108,128]{2,1,0:T(8,128)(2,1)S(1)}, bf16[2,108,128]{2,1,0:T(8,128)(2,1)S(1)}, u32[]{:S(2)}, u32[]{:S(2)}) %collective-permute-start.15) | collective-permute-done | bytes 55328 | tf_op jit(solution)/shard_map/ppermute | solution.py:869
  (47 shorter events, 2.4 us)
Async XLA Ops:
  1.9 8.8 %copy-start = (bf16[3456,128]{1,0:T(8,128)(2,1)S(1)}, bf16[3456,128]{1,0:T(8,128)(2,1)}, u32[]{:S(2)}) copy-start(bf16[3456,128]{1,0:T(8,128)(2,1)} %refs_5_.2) | copy-start | bytes 2654212
  2.0 8.7 %collective-permute-start.2 = (bf16[3,16,16,128]{3,2,1,0:T(8,128)(2,1)S(1)}, bf16[3,16,16,128]{3,2,1,0:T(8,128)(2,1)S(1)}, u32[]{:S(2)}, u32[]{:S(2)}) collective-permute-start(bf16[3,16,16,128]{3,2,1,0:T(8,128)(2,1)S(1)} %pad.25), channel_id=1, source_target_pairs={{0,4},{1,5},{2,6},{3,7},{4,0},{5,1},{6,2},{7,3},{8,12},{9,13},{10,... | collective-permute-start | bytes 589832 | tf_op jit(solution)/shard_map/ppermute | solution.py:716
  5.1 5.6 %collective-permute-start = (bf16[8,3,16,128]{3,2,1,0:T(8,128)(2,1)S(1)}, bf16[8,3,16,128]{3,2,1,0:T(8,128)(2,1)S(1)}, u32[]{:S(2)}, u32[]{:S(2)}) collective-permute-start(bf16[8,3,16,128]{3,2,1,0:T(8,128)(2,1)S(1)} %pad.23), channel_id=1, source_target_pairs={{0,1},{1,0},{2,3},{3,2},{4,5},{5,4},{6,7},{7,6},{8,9},{9,8},{10,11... | collective-permute-start | bytes 294920 | tf_op jit(solution)/shard_map/ppermute | solution.py:716
  5.2 5.5 %collective-permute-start.1 = (bf16[8,3,16,128]{3,2,1,0:T(8,128)(2,1)S(1)}, bf16[8,3,16,128]{3,2,1,0:T(8,128)(2,1)S(1)}, u32[]{:S(2)}, u32[]{:S(2)}) collective-permute-start(bf16[8,3,16,128]{3,2,1,0:T(8,128)(2,1)S(1)} %pad.24), channel_id=1, source_target_pairs={{1,2},{2,1},{5,6},{6,5},{9,10},{10,9},{13,14},{14,13},{17,18},{18,... | collective-permute-start | bytes 294920 | tf_op jit(solution)/shard_map/ppermute | solution.py:716
  6.0 4.7 %collective-permute-start.3 = (bf16[3,3,16,128]{3,2,1,0:T(8,128)(2,1)S(1)}, bf16[3,3,16,128]{3,2,1,0:T(8,128)(2,1)S(1)}, u32[]{:S(2)}, u32[]{:S(2)}) collective-permute-start(bf16[3,3,16,128]{3,2,1,0:T(8,128)(2,1)S(1)} %pad.26), channel_id=1, source_target_pairs={{0,5},{1,4},{2,7},{3,6},{4,1},{5,0},{6,3},{7,2},{8,13},{9,12},{10,... | collective-permute-start | bytes 110600 | tf_op jit(solution)/shard_map/ppermute | solution.py:716
  9.1 1.6 %collective-permute-start.4 = (bf16[3,3,16,128]{3,2,1,0:T(8,128)(2,1)S(1)}, bf16[3,3,16,128]{3,2,1,0:T(8,128)(2,1)S(1)}, u32[]{:S(2)}, u32[]{:S(2)}) collective-permute-start(bf16[3,3,16,128]{3,2,1,0:T(8,128)(2,1)S(1)} %pad.27), channel_id=1, source_target_pairs={{1,6},{2,5},{5,2},{6,1},{9,14},{10,13},{13,10},{14,9},{17,22},{18,... | collective-permute-start | bytes 110600 | tf_op jit(solution)/shard_map/ppermute | solution.py:716
  9.9 22.8 %copy-start.2 = (bf16[576,128]{1,0:T(8,128)(2,1)S(1)}, bf16[576,128]{1,0:T(8,128)(2,1)}, u32[]{:S(2)}) copy-start(bf16[576,128]{1,0:T(8,128)(2,1)} %refs_6_.3) | copy-start | bytes 442372
  9.9 22.8 %copy-start.3 = (bf16[576,64]{0,1:T(8,128)(2,1)S(1)}, bf16[576,64]{0,1:T(8,128)(2,1)}, u32[]{:S(2)}) copy-start(bf16[576,64]{0,1:T(8,128)(2,1)} %param.14) | copy-start | bytes 221188
  9.9 22.8 %copy-start.5 = (bf16[27,64]{1,0:T(8,128)(2,1)S(1)}, bf16[27,64]{1,0:T(8,128)(2,1)}, u32[]{:S(2)}) copy-start(bf16[27,64]{1,0:T(8,128)(2,1)} %refs_4_.2) | copy-start | bytes 10372
  21.1 5.3 %collective-permute-start.5 = (bf16[64,128]{1,0:T(8,128)(2,1)S(1)}, bf16[64,128]{1,0:T(8,128)(2,1)S(1)}, u32[]{:S(2)}, u32[]{:S(2)}) collective-permute-start(bf16[64,128]{1,0:T(8,128)(2,1)S(1)} %get-tuple-element.9), channel_id=1, source_target_pairs={{0,1},{1,0},{2,3},{3,2},{4,5},{5,4},{6,7},{7,6},{8,9},{9,8},{10,11... | collective-permute-start | bytes 49160 | tf_op jit(solution)/shard_map/ppermute | solution.py:755
  26.5 5.0 %collective-permute-start.8 = (bf16[2,64,128]{2,1,0:T(8,128)(2,1)S(1)}, bf16[2,64,128]{2,1,0:T(8,128)(2,1)S(1)}, u32[]{:S(2)}, u32[]{:S(2)}) collective-permute-start(bf16[2,64,128]{2,1,0:T(8,128)(2,1)S(1)} %pad_maximum_fusion.refs_0_), channel_id=1, source_target_pairs={{0,6},{1,7},{2,4},{3,5},{4,2},{5,3},{6,0},{7,1},{8,14},{9,15},{10,... | collective-permute-start | bytes 98312 | tf_op jit(solution)/shard_map/ppermute | solution.py:758
  27.0 4.5 %collective-permute-start.7 = (bf16[2,64,128]{2,1,0:T(8,128)(2,1)S(1)}, bf16[2,64,128]{2,1,0:T(8,128)(2,1)S(1)}, u32[]{:S(2)}, u32[]{:S(2)}) collective-permute-start(bf16[2,64,128]{2,1,0:T(8,128)(2,1)S(1)} %pad_maximum_fusion.refs_0_), channel_id=1, source_target_pairs={{0,4},{1,5},{2,6},{3,7},{4,0},{5,1},{6,2},{7,3},{8,12},{9,13},{10,... | collective-permute-start | bytes 98312 | tf_op jit(solution)/shard_map/ppermute | solution.py:758
  28.8 3.9 %collective-permute-start.6 = (bf16[2,64,128]{2,1,0:T(8,128)(2,1)S(1)}, bf16[2,64,128]{2,1,0:T(8,128)(2,1)S(1)}, u32[]{:S(2)}, u32[]{:S(2)}) collective-permute-start(bf16[2,64,128]{2,1,0:T(8,128)(2,1)S(1)} %pad_maximum_fusion.refs_0_), channel_id=1, source_target_pairs={{0,2},{1,3},{2,0},{3,1},{4,6},{5,7},{6,4},{7,5},{8,10},{9,11},{10,... | collective-permute-start | bytes 98312 | tf_op jit(solution)/shard_map/ppermute | solution.py:758
  32.7 14.9 %copy-start.7 = (f32[10,288,128]{2,1,0:T(8,128)S(1)}, f32[10,288,128]{2,1,0:T(8,128)}, u32[]{:S(2)}) copy-start(f32[10,288,128]{2,1,0:T(8,128)} %get-tuple-element.11.refs_7_) | copy-start | bytes 4423684
  32.7 14.9 %copy-start.8 = (f32[8,256,128]{2,1,0:T(8,128)S(1)}, f32[8,256,128]{2,1,0:T(8,128)}, u32[]{:S(2)}) copy-start(f32[8,256,128]{2,1,0:T(8,128)} %get-tuple-element.10.refs_6_) | copy-start | bytes 3145732
  32.7 14.8 %copy-start.9 = (bf16[10,18,16,128]{3,2,1,0:T(8,128)(2,1)S(1)}, bf16[10,18,16,128]{3,2,1,0:T(8,128)(2,1)}, u32[]{:S(2)}) copy-start(bf16[10,18,16,128]{3,2,1,0:T(8,128)(2,1)} %get-tuple-element.12.refs_8_) | copy-start | bytes 2211844
  32.7 14.8 %copy-start.10 = (bf16[10,18,16,128]{3,2,1,0:T(8,128)(2,1)S(1)}, bf16[10,18,16,128]{3,2,1,0:T(8,128)(2,1)}, u32[]{:S(2)}) copy-start(bf16[10,18,16,128]{3,2,1,0:T(8,128)(2,1)} %get-tuple-element.13.refs_9_) | copy-start | bytes 2211844
  39.3 5.5 %collective-permute-start.11 = (bf16[3,8,144]{2,1,0:T(8,128)(2,1)S(1)}, bf16[3,8,144]{2,1,0:T(8,128)(2,1)S(1)}, u32[]{:S(2)}, u32[]{:S(2)}) collective-permute-start(bf16[3,8,144]{2,1,0:T(8,128)(2,1)S(1)} %shard_map.96.refs_0_), channel_id=1, source_target_pairs={{0,24},{8,16},{16,8},{24,0},{1,25},{9,17},{17,9},{25,1},{2,26},{10... | collective-permute-start | bytes 20744 | tf_op jit(solution)/shard_map/ppermute | solution.py:818
  43.0 4.6 %collective-permute-start.10 = (bf16[3,8,144]{2,1,0:T(8,128)(2,1)S(1)}, bf16[3,8,144]{2,1,0:T(8,128)(2,1)S(1)}, u32[]{:S(2)}, u32[]{:S(2)}) collective-permute-start(bf16[3,8,144]{2,1,0:T(8,128)(2,1)S(1)} %shard_map.96.refs_0_), channel_id=1, source_target_pairs={{0,16},{8,24},{16,0},{24,8},{1,17},{9,25},{17,1},{25,9},{2,18},{10... | collective-permute-start | bytes 20744 | tf_op jit(solution)/shard_map/ppermute | solution.py:818
  43.0 4.6 %collective-permute-start.9 = (bf16[3,8,144]{2,1,0:T(8,128)(2,1)S(1)}, bf16[3,8,144]{2,1,0:T(8,128)(2,1)S(1)}, u32[]{:S(2)}, u32[]{:S(2)}) collective-permute-start(bf16[3,8,144]{2,1,0:T(8,128)(2,1)S(1)} %shard_map.96.refs_0_), channel_id=1, source_target_pairs={{0,8},{8,0},{16,24},{24,16},{1,9},{9,1},{17,25},{25,17},{2,10},{10... | collective-permute-start | bytes 20744 | tf_op jit(solution)/shard_map/ppermute | solution.py:818
  56.4 1.6 %collective-permute-start.12 = (bf16[4,2,108,128]{3,2,1,0:T(8,128)(2,1)S(1)}, bf16[4,2,108,128]{3,2,1,0:T(8,128)(2,1)S(1)}, u32[]{:S(2)}, u32[]{:S(2)}) collective-permute-start(bf16[4,2,108,128]{3,2,1,0:T(8,128)(2,1)S(1)} %get-tuple-element.15), channel_id=1, source_target_pairs={{0,1},{1,0},{2,3},{3,2},{4,5},{5,4},{6,7},{7,6},{8,9},{9,8},{10,11... | collective-permute-start | bytes 663560 | tf_op jit(solution)/shard_map/ppermute | solution.py:865
  58.0 4.2 %collective-permute-start.13 = (bf16[2,108,128]{2,1,0:T(8,128)(2,1)S(1)}, bf16[2,108,128]{2,1,0:T(8,128)(2,1)S(1)}, u32[]{:S(2)}, u32[]{:S(2)}) collective-permute-start(bf16[2,108,128]{2,1,0:T(8,128)(2,1)S(1)} %get-tuple-element.20), channel_id=1, source_target_pairs={{0,2},{1,3},{2,0},{3,1},{4,6},{5,7},{6,4},{7,5},{8,10},{9,11},{10,... | collective-permute-start | bytes 165896 | tf_op jit(solution)/shard_map/ppermute | solution.py:869
  59.3 5.2 %collective-permute-start.15 = (bf16[2,108,128]{2,1,0:T(8,128)(2,1)S(1)}, bf16[2,108,128]{2,1,0:T(8,128)(2,1)S(1)}, u32[]{:S(2)}, u32[]{:S(2)}) collective-permute-start(bf16[2,108,128]{2,1,0:T(8,128)(2,1)S(1)} %get-tuple-element.21), channel_id=1, source_target_pairs={{0,6},{1,7},{2,4},{3,5},{4,2},{5,3},{6,0},{7,1},{8,14},{9,15},{10,... | collective-permute-start | bytes 165896 | tf_op jit(solution)/shard_map/ppermute | solution.py:869
  60.1 4.4 %collective-permute-start.14 = (bf16[2,108,128]{2,1,0:T(8,128)(2,1)S(1)}, bf16[2,108,128]{2,1,0:T(8,128)(2,1)S(1)}, u32[]{:S(2)}, u32[]{:S(2)}) collective-permute-start(bf16[2,108,128]{2,1,0:T(8,128)(2,1)S(1)} %get-tuple-element.22), channel_id=1, source_target_pairs={{0,4},{1,5},{2,6},{3,7},{4,0},{5,1},{6,2},{7,3},{8,12},{9,13},{10,... | collective-permute-start | bytes 165896 | tf_op jit(solution)/shard_map/ppermute | solution.py:869
  (3 other events, 26.4 us)

commit v7 on v6

--- a/solution.py
+++ b/solution.py
@@ -477,19 +477,19 @@
 
     def turn(r):
         block = delta[r].astype(jnp.float32)
+        flat = block.T
         for dt in range(3):
-            moved = block if dt == 1 else pltpu.roll(block, (dt - 1) % count, 0)
-            shifted[dt, r] = moved.T.astype(jnp.bfloat16)
+            moved = flat if dt == 1 else pltpu.roll(flat, (dt - 1) % count, 1)
+            shifted[dt, r] = moved.astype(jnp.bfloat16)
 
     repeat(rows, turn, rows)
 
     def tap_step(step):
         tap = jnp.minimum(first_tap + step, 26)
         dt, dr, dc = tap // 9, tap // 3 % 3, tap % 3
-        total = 0.0
-        for r in range(rows):
-            slab = source[r + dr, pl.ds(dc, cols)].reshape(count, channels)
-            total = total + matmul(shifted[dt, r], slab)
+        slab = source[pl.ds(dr, rows), pl.ds(dc, cols)].reshape(rows * count, channels)
+        turned = jnp.concatenate([shifted[dt, r] for r in range(rows)], axis=1)
+        total = matmul(turned, slab)
         sums[pl.ds(pl.multiple_of(step * channels, channels), channels)] = total.T
 
     repeat(sums.shape[0] // channels, tap_step, 8)
@@ -556,7 +556,7 @@
         delta = jnp.where(inside, hidden_grad[a + 1] * slope_second[a], 0.0).astype(jnp.bfloat16)
         delta_second[a] = delta.reshape(cols + 2, slots, channels)
 
-    repeat(rows + 2, delta_step, 5)
+    repeat(rows + 2, delta_step, 10)
 
     first_row = lax.axis_index("grp") * out_rows
     first_tap = first_row // channels

time: 65.3 us -> 65.4 us (level)
  no operation moved by 1% of the time
where the time goes in v7:
time: 65.4 us; the launch traced here: 65.2 us
  Pallas kernels  25.8 us (39%)
  starting transfers between devices  23.5 us (36%)
  waiting for transfers between devices  12.5 us (19%)
  local copies, waits for them, and re-layouts  2.24 us (3%)
  between operations  0.96 us (1%)
    pallas_call x1, Pallas kernels, local(): call(functools.partial(forward_kernel, frames, parts, pack, places), (plt...  10.4 us
    pallas_call x1, Pallas kernels, local(): call(functools.partial(backward_kernel, parts=parts, out_rows=out_rows, g...  8.89 us
    ppermute x5, starting transfers between devices, local(): lax.ppermute(slotted(edge, slots), plane, moves)  7.51 us
    pallas_call x1, Pallas kernels, local(): call(functools.partial(perceptual_kernel, (rows, cols, blocks, block_fram...  6.58 us
    ppermute x1, starting transfers between devices, local(): other = lax.ppermute(payload, plane, [(i, i ^ 1) for i in range(devices)])  4.48 us
    ppermute x3, starting transfers between devices, local(): gathered.append(lax.ppermute(pixels, 'grp', partners(step, groups)))  4.42 us
    ppermute x3, waiting for transfers between devices, local(): gathered.append(lax.ppermute(pixels, 'grp', partners(step, groups)))  3.81 us
    ppermute x3, starting transfers between devices, local(): lax.ppermute(halves[k].astype(bf16), plane, partners(2 * k, devices))  3.55 us
  transfers between devices with their start and end apart: 16, of which 9 were waited for; matrix products, arithmetic and copies ran while one was open for 0% of the time, Pallas kernels for 0%

profile of v7, /device:TPU:0, one launch (start us, length us, event | category | flops | bytes accessed | tf_op | source)
XLA Modules:
  0.0 65.2 jit_solution(16785267206469579256)
XLA Ops:
  0.6 1.3 %copy.19 = bf16[12,8,16,128]{3,0,2,1:T(8,128)(2,1)S(1)} copy(bf16[12,8,16,128]{3,2,1,0:T(8,128)(2,1)} %bitcast.35) | data formatting | bytes 786432 | tf_op jit(solution)/shard_map/reshape | solution.py:713
  2.0 3.0 %collective-permute-start.2 = (bf16[3,16,16,128]{3,2,1,0:T(8,128)(2,1)S(1)}, bf16[3,16,16,128]{3,2,1,0:T(8,128)(2,1)S(1)}, u32[]{:S(2)}, u32[]{:S(2)}) collective-permute-start(bf16[3,16,16,128]{3,2,1,0:T(8,128)(2,1)S(1)} %pad.25), channel_id=1, source_target_pairs={{0,4},{1,5},{2,6},{3,7},{4,0},{5,1},{6,2},{7,3},{8,12},{9,13},{10,... | collective-permute-start | bytes 589832 | tf_op jit(solution)/shard_map/ppermute | solution.py:716
  5.2 0.7 %collective-permute-start.1 = (bf16[8,3,16,128]{3,2,1,0:T(8,128)(2,1)S(1)}, bf16[8,3,16,128]{3,2,1,0:T(8,128)(2,1)S(1)}, u32[]{:S(2)}, u32[]{:S(2)}) collective-permute-start(bf16[8,3,16,128]{3,2,1,0:T(8,128)(2,1)S(1)} %pad.24), channel_id=1, source_target_pairs={{1,2},{2,1},{5,6},{6,5},{9,10},{10,9},{13,14},{14,13},{17,18},{18,... | collective-permute-start | bytes 294920 | tf_op jit(solution)/shard_map/ppermute | solution.py:716
  6.0 3.1 %collective-permute-start.3 = (bf16[3,3,16,128]{3,2,1,0:T(8,128)(2,1)S(1)}, bf16[3,3,16,128]{3,2,1,0:T(8,128)(2,1)S(1)}, u32[]{:S(2)}, u32[]{:S(2)}) collective-permute-start(bf16[3,3,16,128]{3,2,1,0:T(8,128)(2,1)S(1)} %pad.26), channel_id=1, source_target_pairs={{0,5},{1,4},{2,7},{3,6},{4,1},{5,0},{6,3},{7,2},{8,13},{9,12},{10,... | collective-permute-start | bytes 110600 | tf_op jit(solution)/shard_map/ppermute | solution.py:716
  9.9 0.8 %collective-permute-done.3.refs_3_ = bf16[3,3,16,128]{3,2,1,0:T(8,128)(2,1)S(1)} collective-permute-done((bf16[3,3,16,128]{3,2,1,0:T(8,128)(2,1)S(1)}, bf16[3,3,16,128]{3,2,1,0:T(8,128)(2,1)S(1)}, u32[]{:S(2)}, u32[]{:S(2)}) %collective-permute-start.3) | collective-permute-done | bytes 36896 | tf_op jit(solution)/shard_map/ppermute | solution.py:716
  10.8 10.4 %shard_map.95 = (bf16[10,18,16,128]{3,2,1,0:T(8,128)(2,1)}, bf16[10,18,16,128]{3,2,1,0:T(8,128)(2,1)}, f32[8,256,128]{2,1,0:T(8,128)}, f32[10,288,128]{2,1,0:T(8,128)}, bf16[64,128]{1,0:T(8,128)(2,1)S(1)}) custom-call(bf16[8,16,16,128]{3,2,1,0:T(8,128)(2,1)S(1)} %pad.22.own, bf16[8,3,16,128]{3,2,1,0:T(8,128)(2,1)S(1)} %collective-permute-done.refs_0_, ...), custom_call_target="tpu_custom_call" | custom-call | flops 8589934592 | bytes 1048576 | tf_op jit(solution)/shard_map/pallas_call | solution.py:725
  21.1 4.5 %collective-permute-start.5 = (bf16[64,128]{1,0:T(8,128)(2,1)S(1)}, bf16[64,128]{1,0:T(8,128)(2,1)S(1)}, u32[]{:S(2)}, u32[]{:S(2)}) collective-permute-start(bf16[64,128]{1,0:T(8,128)(2,1)S(1)} %get-tuple-element.9), channel_id=1, source_target_pairs={{0,1},{1,0},{2,3},{3,2},{4,5},{5,4},{6,7},{7,6},{8,9},{9,8},{10,11... | collective-permute-start | bytes 49160 | tf_op jit(solution)/shard_map/ppermute | solution.py:755
  25.6 0.8 %collective-permute-done.5 = bf16[64,128]{1,0:T(8,128)(2,1)S(1)} collective-permute-done((bf16[64,128]{1,0:T(8,128)(2,1)S(1)}, bf16[64,128]{1,0:T(8,128)(2,1)S(1)}, u32[]{:S(2)}, u32[]{:S(2)}) %collective-permute-start.5) | collective-permute-done | bytes 16416 | tf_op jit(solution)/shard_map/ppermute | solution.py:755
  27.0 1.8 %collective-permute-start.7 = (bf16[2,64,128]{2,1,0:T(8,128)(2,1)S(1)}, bf16[2,64,128]{2,1,0:T(8,128)(2,1)S(1)}, u32[]{:S(2)}, u32[]{:S(2)}) collective-permute-start(bf16[2,64,128]{2,1,0:T(8,128)(2,1)S(1)} %pad_maximum_fusion.refs_0_), channel_id=1, source_target_pairs={{0,4},{1,5},{2,6},{3,7},{4,0},{5,1},{6,2},{7,3},{8,12},{9,13},{10,... | collective-permute-start | bytes 98312 | tf_op jit(solution)/shard_map/ppermute | solution.py:758
  28.8 1.2 %collective-permute-start.6 = (bf16[2,64,128]{2,1,0:T(8,128)(2,1)S(1)}, bf16[2,64,128]{2,1,0:T(8,128)(2,1)S(1)}, u32[]{:S(2)}, u32[]{:S(2)}) collective-permute-start(bf16[2,64,128]{2,1,0:T(8,128)(2,1)S(1)} %pad_maximum_fusion.refs_0_), channel_id=1, source_target_pairs={{0,2},{1,3},{2,0},{3,1},{4,6},{5,7},{6,4},{7,5},{8,10},{9,11},{10,... | collective-permute-start | bytes 98312 | tf_op jit(solution)/shard_map/ppermute | solution.py:758
  30.0 1.5 %collective-permute-done.8.refs_3_ = bf16[2,64,128]{2,1,0:T(8,128)(2,1)S(1)} collective-permute-done((bf16[2,64,128]{2,1,0:T(8,128)(2,1)S(1)}, bf16[2,64,128]{2,1,0:T(8,128)(2,1)S(1)}, u32[]{:S(2)}, u32[]{:S(2)}) %collective-permute-start.8) | collective-permute-done | bytes 32800 | tf_op jit(solution)/shard_map/ppermute | solution.py:758
  31.5 1.2 %collective-permute-done.6.refs_1_ = bf16[2,64,128]{2,1,0:T(8,128)(2,1)S(1)} collective-permute-done((bf16[2,64,128]{2,1,0:T(8,128)(2,1)S(1)}, bf16[2,64,128]{2,1,0:T(8,128)(2,1)S(1)}, u32[]{:S(2)}, u32[]{:S(2)}) %collective-permute-start.6) | collective-permute-done | bytes 32800 | tf_op jit(solution)/shard_map/ppermute | solution.py:758
  32.7 6.6 %shard_map.96.refs_0_ = bf16[3,8,144]{2,1,0:T(8,128)(2,1)S(1)} custom-call(bf16[2,64,128]{2,1,0:T(8,128)(2,1)S(1)} %pad_maximum_fusion.refs_0_, bf16[2,64,128]{2,1,0:T(8,128)(2,1)S(1)} %collective-permute-done.6.refs_1_, bf16[2,64,128]{2,1,0:T(8,128)(2,1)S(1)} %collective-permute-done.7.refs_2_, bf16[2,64,128]{2,1,0:T(8,128)(2,1)S(1)} %collective-permute-done.8.refs_3_, ...), custom_call_target="tpu_custom_call" | custom-call | flops 4294967296 | bytes 1048576 | tf_op jit(solution)/shard_map/pallas_call | solution.py:773
  39.3 3.6 %collective-permute-start.11 = (bf16[3,8,144]{2,1,0:T(8,128)(2,1)S(1)}, bf16[3,8,144]{2,1,0:T(8,128)(2,1)S(1)}, u32[]{:S(2)}, u32[]{:S(2)}) collective-permute-start(bf16[3,8,144]{2,1,0:T(8,128)(2,1)S(1)} %shard_map.96.refs_0_), channel_id=1, source_target_pairs={{0,24},{8,16},{16,8},{24,0},{1,25},{9,17},{17,9},{25,1},{2,26},{10... | collective-permute-start | bytes 20744 | tf_op jit(solution)/shard_map/ppermute | solution.py:818
  43.0 0.8 %collective-permute-start.9 = (bf16[3,8,144]{2,1,0:T(8,128)(2,1)S(1)}, bf16[3,8,144]{2,1,0:T(8,128)(2,1)S(1)}, u32[]{:S(2)}, u32[]{:S(2)}) collective-permute-start(bf16[3,8,144]{2,1,0:T(8,128)(2,1)S(1)} %shard_map.96.refs_0_), channel_id=1, source_target_pairs={{0,8},{8,0},{16,24},{24,16},{1,9},{9,1},{17,25},{25,17},{2,10},{10... | collective-permute-start | bytes 20744 | tf_op jit(solution)/shard_map/ppermute | solution.py:818
  43.7 1.1 %collective-permute-done.11.refs_3_ = bf16[3,8,144]{2,1,0:T(8,128)(2,1)S(1)} collective-permute-done((bf16[3,8,144]{2,1,0:T(8,128)(2,1)S(1)}, bf16[3,8,144]{2,1,0:T(8,128)(2,1)S(1)}, u32[]{:S(2)}, u32[]{:S(2)}) %collective-permute-start.11) | collective-permute-done | bytes 6944 | tf_op jit(solution)/shard_map/ppermute | solution.py:818
  44.8 2.7 %collective-permute-done.10.refs_2_ = bf16[3,8,144]{2,1,0:T(8,128)(2,1)S(1)} collective-permute-done((bf16[3,8,144]{2,1,0:T(8,128)(2,1)S(1)}, bf16[3,8,144]{2,1,0:T(8,128)(2,1)S(1)}, u32[]{:S(2)}, u32[]{:S(2)}) %collective-permute-start.10) | collective-permute-done | bytes 6944 | tf_op jit(solution)/shard_map/ppermute | solution.py:818
  47.6 8.9 %shard_map.97 = (bf16[4,2,108,128]{3,2,1,0:T(8,128)(2,1)S(1)}, bf16[4,2,108,128]{3,2,1,0:T(8,128)(2,1)S(1)}) custom-call(bf16[3,8,144]{2,1,0:T(8,128)(2,1)S(1)} %shard_map.96.refs_0_, bf16[3,8,144]{2,1,0:T(8,128)(2,1)S(1)} %collective-permute-done.9.refs_1_, bf16[3,8,144]{2,1,0:T(8,128)(2,1)S(1)} %collective-permute-done.10.refs_2_, ...), custom_call_target="tpu_custom_call" | custom-call | flops 4294967296 | bytes 1048576 | tf_op jit(solution)/shard_map/pallas_call | solution.py:831
  56.6 1.5 %collective-permute-done.12 = bf16[4,2,108,128]{3,2,1,0:T(8,128)(2,1)S(1)} collective-permute-done((bf16[4,2,108,128]{3,2,1,0:T(8,128)(2,1)S(1)}, bf16[4,2,108,128]{3,2,1,0:T(8,128)(2,1)S(1)}, u32[]{:S(2)}, u32[]{:S(2)}) %collective-permute-start.12) | collective-permute-done | bytes 221216 | tf_op jit(solution)/shard_map/ppermute | solution.py:865
  58.1 1.2 %collective-permute-start.13 = (bf16[2,108,128]{2,1,0:T(8,128)(2,1)S(1)}, bf16[2,108,128]{2,1,0:T(8,128)(2,1)S(1)}, u32[]{:S(2)}, u32[]{:S(2)}) collective-permute-start(bf16[2,108,128]{2,1,0:T(8,128)(2,1)S(1)} %get-tuple-element.20), channel_id=1, source_target_pairs={{0,2},{1,3},{2,0},{3,1},{4,6},{5,7},{6,4},{7,5},{8,10},{9,11},{10,... | collective-permute-start | bytes 165896 | tf_op jit(solution)/shard_map/ppermute | solution.py:869
  59.3 0.8 %collective-permute-start.15 = (bf16[2,108,128]{2,1,0:T(8,128)(2,1)S(1)}, bf16[2,108,128]{2,1,0:T(8,128)(2,1)S(1)}, u32[]{:S(2)}, u32[]{:S(2)}) collective-permute-start(bf16[2,108,128]{2,1,0:T(8,128)(2,1)S(1)} %get-tuple-element.21), channel_id=1, source_target_pairs={{0,6},{1,7},{2,4},{3,5},{4,2},{5,3},{6,0},{7,1},{8,14},{9,15},{10,... | collective-permute-start | bytes 165896 | tf_op jit(solution)/shard_map/ppermute | solution.py:869
  60.2 1.5 %collective-permute-start.14 = (bf16[2,108,128]{2,1,0:T(8,128)(2,1)S(1)}, bf16[2,108,128]{2,1,0:T(8,128)(2,1)S(1)}, u32[]{:S(2)}, u32[]{:S(2)}) collective-permute-start(bf16[2,108,128]{2,1,0:T(8,128)(2,1)S(1)} %get-tuple-element.22), channel_id=1, source_target_pairs={{0,4},{1,5},{2,6},{3,7},{4,0},{5,1},{6,2},{7,3},{8,12},{9,13},{10,... | collective-permute-start | bytes 165896 | tf_op jit(solution)/shard_map/ppermute | solution.py:869
  61.6 0.7 %collective-permute-done.13 = bf16[2,108,128]{2,1,0:T(8,128)(2,1)S(1)} collective-permute-done((bf16[2,108,128]{2,1,0:T(8,128)(2,1)S(1)}, bf16[2,108,128]{2,1,0:T(8,128)(2,1)S(1)}, u32[]{:S(2)}, u32[]{:S(2)}) %collective-permute-start.13) | collective-permute-done | bytes 55328 | tf_op jit(solution)/shard_map/ppermute | solution.py:869
  62.3 2.2 %collective-permute-done.15 = bf16[2,108,128]{2,1,0:T(8,128)(2,1)S(1)} collective-permute-done((bf16[2,108,128]{2,1,0:T(8,128)(2,1)S(1)}, bf16[2,108,128]{2,1,0:T(8,128)(2,1)S(1)}, u32[]{:S(2)}, u32[]{:S(2)}) %collective-permute-start.15) | collective-permute-done | bytes 55328 | tf_op jit(solution)/shard_map/ppermute | solution.py:869
  (47 shorter events, 2.4 us)
Async XLA Ops:
  1.9 8.8 %copy-start = (bf16[3456,128]{1,0:T(8,128)(2,1)S(1)}, bf16[3456,128]{1,0:T(8,128)(2,1)}, u32[]{:S(2)}) copy-start(bf16[3456,128]{1,0:T(8,128)(2,1)} %refs_5_.2) | copy-start | bytes 2654212
  2.0 8.7 %collective-permute-start.2 = (bf16[3,16,16,128]{3,2,1,0:T(8,128)(2,1)S(1)}, bf16[3,16,16,128]{3,2,1,0:T(8,128)(2,1)S(1)}, u32[]{:S(2)}, u32[]{:S(2)}) collective-permute-start(bf16[3,16,16,128]{3,2,1,0:T(8,128)(2,1)S(1)} %pad.25), channel_id=1, source_target_pairs={{0,4},{1,5},{2,6},{3,7},{4,0},{5,1},{6,2},{7,3},{8,12},{9,13},{10,... | collective-permute-start | bytes 589832 | tf_op jit(solution)/shard_map/ppermute | solution.py:716
  5.1 5.6 %collective-permute-start = (bf16[8,3,16,128]{3,2,1,0:T(8,128)(2,1)S(1)}, bf16[8,3,16,128]{3,2,1,0:T(8,128)(2,1)S(1)}, u32[]{:S(2)}, u32[]{:S(2)}) collective-permute-start(bf16[8,3,16,128]{3,2,1,0:T(8,128)(2,1)S(1)} %pad.23), channel_id=1, source_target_pairs={{0,1},{1,0},{2,3},{3,2},{4,5},{5,4},{6,7},{7,6},{8,9},{9,8},{10,11... | collective-permute-start | bytes 294920 | tf_op jit(solution)/shard_map/ppermute | solution.py:716
  5.2 5.5 %collective-permute-start.1 = (bf16[8,3,16,128]{3,2,1,0:T(8,128)(2,1)S(1)}, bf16[8,3,16,128]{3,2,1,0:T(8,128)(2,1)S(1)}, u32[]{:S(2)}, u32[]{:S(2)}) collective-permute-start(bf16[8,3,16,128]{3,2,1,0:T(8,128)(2,1)S(1)} %pad.24), channel_id=1, source_target_pairs={{1,2},{2,1},{5,6},{6,5},{9,10},{10,9},{13,14},{14,13},{17,18},{18,... | collective-permute-start | bytes 294920 | tf_op jit(solution)/shard_map/ppermute | solution.py:716
  6.0 4.7 %collective-permute-start.3 = (bf16[3,3,16,128]{3,2,1,0:T(8,128)(2,1)S(1)}, bf16[3,3,16,128]{3,2,1,0:T(8,128)(2,1)S(1)}, u32[]{:S(2)}, u32[]{:S(2)}) collective-permute-start(bf16[3,3,16,128]{3,2,1,0:T(8,128)(2,1)S(1)} %pad.26), channel_id=1, source_target_pairs={{0,5},{1,4},{2,7},{3,6},{4,1},{5,0},{6,3},{7,2},{8,13},{9,12},{10,... | collective-permute-start | bytes 110600 | tf_op jit(solution)/shard_map/ppermute | solution.py:716
  9.1 1.6 %collective-permute-start.4 = (bf16[3,3,16,128]{3,2,1,0:T(8,128)(2,1)S(1)}, bf16[3,3,16,128]{3,2,1,0:T(8,128)(2,1)S(1)}, u32[]{:S(2)}, u32[]{:S(2)}) collective-permute-start(bf16[3,3,16,128]{3,2,1,0:T(8,128)(2,1)S(1)} %pad.27), channel_id=1, source_target_pairs={{1,6},{2,5},{5,2},{6,1},{9,14},{10,13},{13,10},{14,9},{17,22},{18,... | collective-permute-start | bytes 110600 | tf_op jit(solution)/shard_map/ppermute | solution.py:716
  9.9 22.8 %copy-start.2 = (bf16[576,128]{1,0:T(8,128)(2,1)S(1)}, bf16[576,128]{1,0:T(8,128)(2,1)}, u32[]{:S(2)}) copy-start(bf16[576,128]{1,0:T(8,128)(2,1)} %refs_6_.3) | copy-start | bytes 442372
  9.9 22.8 %copy-start.3 = (bf16[576,64]{0,1:T(8,128)(2,1)S(1)}, bf16[576,64]{0,1:T(8,128)(2,1)}, u32[]{:S(2)}) copy-start(bf16[576,64]{0,1:T(8,128)(2,1)} %param.14) | copy-start | bytes 221188
  9.9 22.8 %copy-start.5 = (bf16[27,64]{1,0:T(8,128)(2,1)S(1)}, bf16[27,64]{1,0:T(8,128)(2,1)}, u32[]{:S(2)}) copy-start(bf16[27,64]{1,0:T(8,128)(2,1)} %refs_4_.2) | copy-start | bytes 10372
  21.1 5.3 %collective-permute-start.5 = (bf16[64,128]{1,0:T(8,128)(2,1)S(1)}, bf16[64,128]{1,0:T(8,128)(2,1)S(1)}, u32[]{:S(2)}, u32[]{:S(2)}) collective-permute-start(bf16[64,128]{1,0:T(8,128)(2,1)S(1)} %get-tuple-element.9), channel_id=1, source_target_pairs={{0,1},{1,0},{2,3},{3,2},{4,5},{5,4},{6,7},{7,6},{8,9},{9,8},{10,11... | collective-permute-start | bytes 49160 | tf_op jit(solution)/shard_map/ppermute | solution.py:755
  26.5 5.0 %collective-permute-start.8 = (bf16[2,64,128]{2,1,0:T(8,128)(2,1)S(1)}, bf16[2,64,128]{2,1,0:T(8,128)(2,1)S(1)}, u32[]{:S(2)}, u32[]{:S(2)}) collective-permute-start(bf16[2,64,128]{2,1,0:T(8,128)(2,1)S(1)} %pad_maximum_fusion.refs_0_), channel_id=1, source_target_pairs={{0,6},{1,7},{2,4},{3,5},{4,2},{5,3},{6,0},{7,1},{8,14},{9,15},{10,... | collective-permute-start | bytes 98312 | tf_op jit(solution)/shard_map/ppermute | solution.py:758
  27.0 4.5 %collective-permute-start.7 = (bf16[2,64,128]{2,1,0:T(8,128)(2,1)S(1)}, bf16[2,64,128]{2,1,0:T(8,128)(2,1)S(1)}, u32[]{:S(2)}, u32[]{:S(2)}) collective-permute-start(bf16[2,64,128]{2,1,0:T(8,128)(2,1)S(1)} %pad_maximum_fusion.refs_0_), channel_id=1, source_target_pairs={{0,4},{1,5},{2,6},{3,7},{4,0},{5,1},{6,2},{7,3},{8,12},{9,13},{10,... | collective-permute-start | bytes 98312 | tf_op jit(solution)/shard_map/ppermute | solution.py:758
  28.8 3.9 %collective-permute-start.6 = (bf16[2,64,128]{2,1,0:T(8,128)(2,1)S(1)}, bf16[2,64,128]{2,1,0:T(8,128)(2,1)S(1)}, u32[]{:S(2)}, u32[]{:S(2)}) collective-permute-start(bf16[2,64,128]{2,1,0:T(8,128)(2,1)S(1)} %pad_maximum_fusion.refs_0_), channel_id=1, source_target_pairs={{0,2},{1,3},{2,0},{3,1},{4,6},{5,7},{6,4},{7,5},{8,10},{9,11},{10,... | collective-permute-start | bytes 98312 | tf_op jit(solution)/shard_map/ppermute | solution.py:758
  32.7 14.9 %copy-start.7 = (f32[10,288,128]{2,1,0:T(8,128)S(1)}, f32[10,288,128]{2,1,0:T(8,128)}, u32[]{:S(2)}) copy-start(f32[10,288,128]{2,1,0:T(8,128)} %get-tuple-element.11.refs_7_) | copy-start | bytes 4423684
  32.7 14.9 %copy-start.8 = (f32[8,256,128]{2,1,0:T(8,128)S(1)}, f32[8,256,128]{2,1,0:T(8,128)}, u32[]{:S(2)}) copy-start(f32[8,256,128]{2,1,0:T(8,128)} %get-tuple-element.10.refs_6_) | copy-start | bytes 3145732
  32.7 14.8 %copy-start.9 = (bf16[10,18,16,128]{3,2,1,0:T(8,128)(2,1)S(1)}, bf16[10,18,16,128]{3,2,1,0:T(8,128)(2,1)}, u32[]{:S(2)}) copy-start(bf16[10,18,16,128]{3,2,1,0:T(8,128)(2,1)} %get-tuple-element.12.refs_8_) | copy-start | bytes 2211844
  32.7 14.8 %copy-start.10 = (bf16[10,18,16,128]{3,2,1,0:T(8,128)(2,1)S(1)}, bf16[10,18,16,128]{3,2,1,0:T(8,128)(2,1)}, u32[]{:S(2)}) copy-start(bf16[10,18,16,128]{3,2,1,0:T(8,128)(2,1)} %get-tuple-element.13.refs_9_) | copy-start | bytes 2211844
  39.3 5.5 %collective-permute-start.11 = (bf16[3,8,144]{2,1,0:T(8,128)(2,1)S(1)}, bf16[3,8,144]{2,1,0:T(8,128)(2,1)S(1)}, u32[]{:S(2)}, u32[]{:S(2)}) collective-permute-start(bf16[3,8,144]{2,1,0:T(8,128)(2,1)S(1)} %shard_map.96.refs_0_), channel_id=1, source_target_pairs={{0,24},{8,16},{16,8},{24,0},{1,25},{9,17},{17,9},{25,1},{2,26},{10... | collective-permute-start | bytes 20744 | tf_op jit(solution)/shard_map/ppermute | solution.py:818
  43.0 4.6 %collective-permute-start.10 = (bf16[3,8,144]{2,1,0:T(8,128)(2,1)S(1)}, bf16[3,8,144]{2,1,0:T(8,128)(2,1)S(1)}, u32[]{:S(2)}, u32[]{:S(2)}) collective-permute-start(bf16[3,8,144]{2,1,0:T(8,128)(2,1)S(1)} %shard_map.96.refs_0_), channel_id=1, source_target_pairs={{0,16},{8,24},{16,0},{24,8},{1,17},{9,25},{17,1},{25,9},{2,18},{10... | collective-permute-start | bytes 20744 | tf_op jit(solution)/shard_map/ppermute | solution.py:818
  43.0 4.6 %collective-permute-start.9 = (bf16[3,8,144]{2,1,0:T(8,128)(2,1)S(1)}, bf16[3,8,144]{2,1,0:T(8,128)(2,1)S(1)}, u32[]{:S(2)}, u32[]{:S(2)}) collective-permute-start(bf16[3,8,144]{2,1,0:T(8,128)(2,1)S(1)} %shard_map.96.refs_0_), channel_id=1, source_target_pairs={{0,8},{8,0},{16,24},{24,16},{1,9},{9,1},{17,25},{25,17},{2,10},{10... | collective-permute-start | bytes 20744 | tf_op jit(solution)/shard_map/ppermute | solution.py:818
  56.5 1.6 %collective-permute-start.12 = (bf16[4,2,108,128]{3,2,1,0:T(8,128)(2,1)S(1)}, bf16[4,2,108,128]{3,2,1,0:T(8,128)(2,1)S(1)}, u32[]{:S(2)}, u32[]{:S(2)}) collective-permute-start(bf16[4,2,108,128]{3,2,1,0:T(8,128)(2,1)S(1)} %get-tuple-element.15), channel_id=1, source_target_pairs={{0,1},{1,0},{2,3},{3,2},{4,5},{5,4},{6,7},{7,6},{8,9},{9,8},{10,11... | collective-permute-start | bytes 663560 | tf_op jit(solution)/shard_map/ppermute | solution.py:865
  58.1 4.2 %collective-permute-start.13 = (bf16[2,108,128]{2,1,0:T(8,128)(2,1)S(1)}, bf16[2,108,128]{2,1,0:T(8,128)(2,1)S(1)}, u32[]{:S(2)}, u32[]{:S(2)}) collective-permute-start(bf16[2,108,128]{2,1,0:T(8,128)(2,1)S(1)} %get-tuple-element.20), channel_id=1, source_target_pairs={{0,2},{1,3},{2,0},{3,1},{4,6},{5,7},{6,4},{7,5},{8,10},{9,11},{10,... | collective-permute-start | bytes 165896 | tf_op jit(solution)/shard_map/ppermute | solution.py:869
  59.3 5.2 %collective-permute-start.15 = (bf16[2,108,128]{2,1,0:T(8,128)(2,1)S(1)}, bf16[2,108,128]{2,1,0:T(8,128)(2,1)S(1)}, u32[]{:S(2)}, u32[]{:S(2)}) collective-permute-start(bf16[2,108,128]{2,1,0:T(8,128)(2,1)S(1)} %get-tuple-element.21), channel_id=1, source_target_pairs={{0,6},{1,7},{2,4},{3,5},{4,2},{5,3},{6,0},{7,1},{8,14},{9,15},{10,... | collective-permute-start | bytes 165896 | tf_op jit(solution)/shard_map/ppermute | solution.py:869
  60.2 4.4 %collective-permute-start.14 = (bf16[2,108,128]{2,1,0:T(8,128)(2,1)S(1)}, bf16[2,108,128]{2,1,0:T(8,128)(2,1)S(1)}, u32[]{:S(2)}, u32[]{:S(2)}) collective-permute-start(bf16[2,108,128]{2,1,0:T(8,128)(2,1)S(1)} %get-tuple-element.22), channel_id=1, source_target_pairs={{0,4},{1,5},{2,6},{3,7},{4,0},{5,1},{6,2},{7,3},{8,12},{9,13},{10,... | collective-permute-start | bytes 165896 | tf_op jit(solution)/shard_map/ppermute | solution.py:869
  (3 other events, 26.4 us)
